TPU v7x, 256 devices: a whole 4x4x8 slice. The times are simulated.
256 devices in a mesh: seq: 64 (over z, y, core), head: 4 (over x).
Axes of the slice: x: 4, y: 4, z: 8, core: 2. Of those that a mesh axis runs over, the one named last changes fastest.
Arguments:
- query: bfloat16 [8192, 64, 576], P('seq', 'head'), may hold values from -10 to 10
- cache: bfloat16 [32768, 576], P('seq'), may hold values from -6 to 6
- grad_out: bfloat16 [8192, 64, 128], P('seq', 'head'), may hold values from -6 to 6
- value_weight: bfloat16 [64, 512, 128], P('head'), may hold values from -0.25 to 0.25
- picked: int32 [256, 4], P('seq'), may hold values from 0 to 255, as said below
Outputs:
- d_query: bfloat16 [8192, 64, 576], P('seq', 'head')
- d_cache: float32 [256, 128, 576], P('seq', 'head')
- d_value_weight: bfloat16 [64, 512, 128], P('head')
Inputs may be any that keep to these rules, and one draw needn't show every extreme that they name: `picked`: row g names 4 different blocks, each starting at or before the first query of block g. One of them is the block that holds query block g; every other one ends before position 24576. The rows of one index of seq together name at most 1 different blocks of any one owner (owner o holds blocks o * 4 to o * 4 + 3), and in every draw some owner has exactly 1 of its blocks named by every index of seq.
All inputs are finite; a program needn't handle non-finite values.
Results may differ from a plain program's by a relative error of at most 0.01.
Values may be sent and summed in bfloat16 or wider, within the bound.
No kernel may reach another device: no remote copies, remote signals or barrier semaphores. Data moves between devices by JAX's collectives and lax.ppermute only.
A program may use at most 128 MiB of HBM per device.

v0:
```python
import jax
import jax.numpy as jnp
from jax import lax
from jax.experimental import pallas as pl
from jax.experimental.pallas import tpu as pltpu
from jax.sharding import PartitionSpec as P

KVL = 512
BLOCK = 128
QB = 32
TOPB = 4
OTHERS = TOPB - 1

SCORE_SCALE = 0.07216878364870323
MASKED = -1e30

Z, Y, C = 8, 4, 2
X = 4
Z_FULL = 6
FIRST_OWN_OWNER = Z_FULL * Y * C


F32 = jnp.float32
BF16 = jnp.bfloat16


def seq_of(z, y, c):
    return ((z % Z) * Y + y % Y) * C + c


def shift_z(array, step, sends=lambda z: True):
    pairs = [
        (seq_of(z, y, c), seq_of(z + step, y, c))
        for z in range(Z)
        for y in range(Y)
        for c in range(C)
        if sends(z)
    ]
    return lax.ppermute(array, "seq", pairs)


def shift_y(array, step):
    pairs = [
        (seq_of(z, y, c), seq_of(z, y + step, c))
        for z in range(Z)
        for y in range(Y)
        for c in range(C)
    ]
    return lax.ppermute(array, "seq", pairs)


def swap_core(array):
    return lax.ppermute(array, "seq", [(s, s ^ 1) for s in range(Z * Y * C)])


def shift_x(array, step):
    return lax.ppermute(array, "head", [(x, (x + step) % X) for x in range(X)])


def trade_yc(blocks):
    groups = [[seq_of(z, 0, 0) + i for i in range(Y * C)] for z in range(Z)]
    return lax.all_to_all(
        blocks, "seq", split_axis=0, concat_axis=0, axis_index_groups=groups, tiled=True
    )


def narrow(array):
    return array.astype(BF16)


def wide(array):
    return array.astype(F32)


def pack_kernel(block_ref, z_ref, *refs):
    pieces, out_ref, sem = refs[:Z], refs[Z], refs[Z + 1]
    for j in range(Z):
        owner_z = (z_ref[0] + j) % Z

        @pl.when(owner_z < Z_FULL)
        def _():
            for peer in range(Y * C):
                place = peer * Z_FULL + owner_z
                pltpu.make_async_copy(
                    pieces[j].at[block_ref[place]], out_ref.at[place], sem
                ).start()

    pltpu.make_async_copy(out_ref, out_ref, sem).wait()


def pack(blocks, z, pieces):
    hbm = pl.BlockSpec(memory_space=pltpu.HBM)
    smem = pl.BlockSpec(memory_space=pltpu.SMEM)
    return pl.pallas_call(
        pack_kernel,
        in_specs=[smem, smem] + [hbm] * Z,
        out_specs=hbm,
        out_shape=jax.ShapeDtypeStruct((blocks.shape[0], *pieces[0].shape[1:]), BF16),
        scratch_shapes=[pltpu.SemaphoreType.DMA],
        name="pack",
    )(blocks, z.reshape(1), *pieces)


def pick_kernel(place_ref, own_ref, fetched_ref, *refs):
    owns, (low_ref, high_ref, low_sem, high_sem) = refs[:-4], refs[-4:]
    n_low, n_high = low_ref.shape[0], high_ref.shape[0]
    for j, own in enumerate(owns):

        @pl.when(own_ref[0] == j)
        def _():
            pltpu.make_async_copy(own, low_ref.at[n_low - 1], low_sem).start()

    for slot in range(n_low - 1):
        pltpu.make_async_copy(
            fetched_ref.at[place_ref[slot]], low_ref.at[slot], low_sem
        ).start()
    for slot in range(n_high):
        pltpu.make_async_copy(
            fetched_ref.at[place_ref[n_low - 1 + slot]], high_ref.at[slot], high_sem
        ).start()
    pltpu.make_async_copy(low_ref, low_ref, low_sem).wait()
    pltpu.make_async_copy(high_ref, high_ref, high_sem).wait()


def pick(place, own_index, fetched, owns):
    hbm = pl.BlockSpec(memory_space=pltpu.HBM)
    smem = pl.BlockSpec(memory_space=pltpu.SMEM)
    n_high = place.shape[0] // 2
    n_low = place.shape[0] - n_high + 1
    return pl.pallas_call(
        pick_kernel,
        in_specs=[smem, smem, hbm] + [hbm] * len(owns),
        out_specs=[hbm, hbm],
        out_shape=[
            jax.ShapeDtypeStruct((n_low, *fetched.shape[1:]), BF16),
            jax.ShapeDtypeStruct((n_high, *fetched.shape[1:]), BF16),
        ],
        scratch_shapes=[pltpu.SemaphoreType.DMA] * 2,
        name="pick",
    )(place, own_index.reshape(1), fetched, *owns)


def attend_kernel(x_ref, q_ref, dl_ref, *refs):
    low_refs, own_refs, high_refs = refs[:X], refs[X : 2 * X], refs[2 * X : 3 * X]
    dq_ref, lat_ref = refs[3 * X : 3 * X + 2]
    d_low_refs, d_high_refs = refs[3 * X + 2 : 4 * X + 2], refs[4 * X + 2 : 5 * X + 2]
    keys, own_sum = refs[5 * X + 2 :]
    block = pl.program_id(0)
    half_blocks = pl.num_programs(0) // 2
    rows, width = q_ref.shape
    heads = rows // QB
    quarter = own_refs[0].shape[1]
    n_part = OTHERS * quarter
    n_other = X * n_part

    @pl.when(block < half_blocks)
    def _():
        for j in range(X):
            keys[j * n_part : (j + 1) * n_part] = low_refs[j][...].reshape(n_part, width)

    @pl.when(block >= half_blocks)
    def _():
        for j in range(X):
            keys[j * n_part : (j + 1) * n_part] = high_refs[j][...].reshape(n_part, width)

    @pl.when(block == 0)
    def _():
        for j in range(X):
            keys[n_other + j * quarter : n_other + (j + 1) * quarter] = own_refs[j][0]

    q = q_ref[...]
    dl = dl_ref[...]
    k = keys[...]
    v = keys[:, :KVL]
    n_keys = k.shape[0]
    scores = lax.dot_general(q, k, (((1,), (1,)), ((), ())), preferred_element_type=F32)
    scores = scores * SCORE_SCALE
    col = lax.broadcasted_iota(jnp.int32, (rows, n_keys - n_other), 1)
    row = lax.broadcasted_iota(jnp.int32, (rows, n_keys - n_other), 0)
    source = (x_ref[0] + X - col // quarter) % X
    visible = source * quarter + col % quarter <= block * QB + row // heads
    scores = jnp.concatenate(
        [scores[:, :n_other], jnp.where(visible, scores[:, n_other:], MASKED)], axis=1
    )
    row_max = jnp.max(scores, axis=1, keepdims=True)
    exp_scores = jnp.exp(scores - row_max)
    weights = exp_scores / jnp.sum(exp_scores, axis=1, keepdims=True)
    weights_low = narrow(weights)
    latent = narrow(jnp.dot(weights_low, v, preferred_element_type=F32))
    lat_ref[...] = latent
    delta = jnp.sum(wide(dl) * wide(latent), axis=1, keepdims=True)
    d_probs = lax.dot_general(dl, v, (((1,), (1,)), ((), ())), preferred_element_type=F32)
    d_scores = narrow(SCORE_SCALE * weights * (d_probs - delta))
    dq_ref[...] = narrow(jnp.dot(d_scores, k, preferred_element_type=F32))
    d_keys = lax.dot_general(d_scores, q, (((0,), (0,)), ((), ())), preferred_element_type=F32)
    d_values = lax.dot_general(
        weights_low, dl, (((0,), (0,)), ((), ())), preferred_element_type=F32
    )
    d_keys = jnp.concatenate([d_keys[:, :KVL] + d_values, d_keys[:, KVL:]], axis=1)
    d_other = narrow(d_keys[:n_other]).reshape(X, OTHERS, quarter, width)

    @pl.when(block < half_blocks)
    def _():
        for j in range(X):
            d_low_refs[j][pl.ds(OTHERS * block, OTHERS)] = d_other[j]

    @pl.when(block >= half_blocks)
    def _():
        for j in range(X):
            d_high_refs[j][pl.ds(OTHERS * (block - half_blocks), OTHERS)] = d_other[j]

    d_own = d_keys[n_other:]

    @pl.when(block == 0)
    def _():
        own_sum[...] = d_own

    @pl.when(block > 0)
    def _():
        own_sum[...] += d_own

    @pl.when(block == pl.num_programs(0) - 1)
    def _():
        last = d_low_refs[0].shape[0] - 1
        for j in range(X):
            d_low_refs[j][last] = narrow(own_sum[j * quarter : (j + 1) * quarter])


def attend(x, q, dl, low, high, interpret=False):
    rows, width = q.shape
    n_low, quarter, _ = low[0].shape
    n_high = high[0].shape[0]
    blocks = (n_low - 1 + n_high) // OTHERS
    half = blocks // 2
    per = rows // blocks
    n_keys = TOPB * X * quarter
    part = (OTHERS, quarter, width)
    return pl.pallas_call(
        attend_kernel,
        grid_spec=pltpu.PrefetchScalarGridSpec(
            num_scalar_prefetch=1,
            grid=(blocks,),
            in_specs=[
                pl.BlockSpec((per, width), lambda g, x: (g, 0)),
                pl.BlockSpec((per, KVL), lambda g, x: (g, 0)),
            ]
            + [pl.BlockSpec(part, lambda g, x: (jnp.minimum(g, half - 1), 0, 0))] * X
            + [pl.BlockSpec((1, quarter, width), lambda g, x: (n_low - 1, 0, 0))] * X
            + [pl.BlockSpec(part, lambda g, x: (jnp.maximum(g - half, 0), 0, 0))] * X,
            out_specs=[
                pl.BlockSpec((per, width), lambda g, x: (g, 0)),
                pl.BlockSpec((per, KVL), lambda g, x: (g, 0)),
            ]
            + [pl.BlockSpec((n_low, quarter, width), lambda g, x: (0, 0, 0))] * X
            + [pl.BlockSpec((n_high, quarter, width), lambda g, x: (0, 0, 0))] * X,
            scratch_shapes=[
                pltpu.VMEM((n_keys, width), BF16),
                pltpu.VMEM((X * quarter, width), F32),
            ],
        ),
        out_shape=[
            jax.ShapeDtypeStruct((rows, width), BF16),
            jax.ShapeDtypeStruct((rows, KVL), BF16),
        ]
        + [jax.ShapeDtypeStruct((n_low, quarter, width), BF16)] * X
        + [jax.ShapeDtypeStruct((n_high, quarter, width), BF16)] * X,
        interpret=interpret,
        compiler_params=pltpu.CompilerParams(vmem_limit_bytes=56 * 2**20),
        name="attend",
    )(x.reshape(1), q, dl, *low, *low, *high)


def send_back_kernel(at_ref, *refs):
    low_refs, high_refs = refs[:3], refs[3:6]
    out_ref, own_ref, total = refs[6:]
    n_low, n_high = low_refs[0].shape[0], high_refs[0].shape[0]
    total[...] = jnp.zeros_like(total)
    for slot in range(n_low + n_high - 1):
        refs_here, index = (low_refs, slot) if slot < n_low - 1 else (high_refs, slot - n_low + 1)
        share = wide(refs_here[0][index]) + wide(refs_here[1][index]) + wide(refs_here[2][index])
        total[at_ref[slot]] += share
    last = n_low - 1
    own_ref[...] = narrow(
        wide(low_refs[0][last]) + wide(low_refs[1][last]) + wide(low_refs[2][last])
    )
    out_ref[...] = narrow(total[...])


def send_back(at, low, high, places, interpret=False):
    _, quarter, width = low[0].shape
    vmem = pl.BlockSpec(memory_space=pltpu.VMEM)
    return pl.pallas_call(
        send_back_kernel,
        in_specs=[pl.BlockSpec(memory_space=pltpu.SMEM)] + [vmem] * 6,
        out_specs=[vmem, vmem],
        out_shape=[
            jax.ShapeDtypeStruct((places, quarter, width), BF16),
            jax.ShapeDtypeStruct((quarter, width), BF16),
        ],
        scratch_shapes=[pltpu.VMEM((places, quarter, width), F32)],
        interpret=interpret,
        compiler_params=pltpu.CompilerParams(vmem_limit_bytes=40 * 2**20),
        name="send_back",
    )(at, *low, *high)


def by_owner_kernel(at_ref, in_ref, *refs):
    out_refs, total = refs[:-1], refs[-1]
    total[...] = jnp.zeros_like(total)
    for slot in range(in_ref.shape[0]):
        total[at_ref[slot]] += wide(in_ref[slot])
    blocks = out_refs[0].shape[0]
    for j, out_ref in enumerate(out_refs):
        out_ref[...] = narrow(total[j * blocks : (j + 1) * blocks])


def by_owner(at, received, blocks, interpret=False):
    _, quarter, width = received.shape
    vmem = pl.BlockSpec(memory_space=pltpu.VMEM)
    return pl.pallas_call(
        by_owner_kernel,
        in_specs=[pl.BlockSpec(memory_space=pltpu.SMEM), vmem],
        out_specs=[vmem] * Z,
        out_shape=[jax.ShapeDtypeStruct((blocks, quarter, width), BF16)] * Z,
        scratch_shapes=[pltpu.VMEM((Z * blocks + 1, quarter, width), F32)],
        interpret=interpret,
        compiler_params=pltpu.CompilerParams(vmem_limit_bytes=40 * 2**20),
        name="by_owner",
    )(at, received)


def fold_core_kernel(at_ref, terms_ref, arrived_ref, *out_refs):
    for j, out_ref in enumerate(out_refs):
        y = (at_ref[0] + j) % Y
        out_ref[...] = narrow(wide(terms_ref[y, at_ref[1]]) + wide(arrived_ref[y]))


def fold_core(y, c, terms, arrived):
    vmem = pl.BlockSpec(memory_space=pltpu.VMEM)
    return pl.pallas_call(
        fold_core_kernel,
        in_specs=[pl.BlockSpec(memory_space=pltpu.SMEM), vmem, vmem],
        out_specs=[vmem] * Y,
        out_shape=[jax.ShapeDtypeStruct(terms.shape[2:], BF16)] * Y,
        name="fold_core",
    )(jnp.stack([y, c]), terms, arrived)


def fold_y_kernel(z_ref, *refs):
    terms, out_refs = refs[:Y], refs[Y:]
    lines = out_refs[0].shape[0]
    for j, out_ref in enumerate(out_refs):
        part = pl.ds((z_ref[0] + j) % Z * lines, lines)
        total = wide(terms[0][part])
        for term in terms[1:]:
            total += wide(term[part])
        out_ref[...] = narrow(total)


def fold_y(z, terms):
    lines, v_dim = terms[0].shape
    vmem = pl.BlockSpec(memory_space=pltpu.VMEM)
    return pl.pallas_call(
        fold_y_kernel,
        in_specs=[pl.BlockSpec(memory_space=pltpu.SMEM)] + [vmem] * Y,
        out_specs=[vmem] * Z,
        out_shape=[jax.ShapeDtypeStruct((lines // Z, v_dim), BF16)] * Z,
        name="fold_y",
    )(z.reshape(1), *terms)


def copies_kernel(z_ref, *refs):
    pieces, out_ref = refs[:-1], refs[-1]
    lines = pieces[0].shape[0]
    for j, piece in enumerate(pieces):
        part = pl.ds((z_ref[0] + j) % Z * lines, lines)
        for peer in range(out_ref.shape[0]):
            out_ref[peer, part] = piece[...]


def copies(z, pieces):
    lines, v_dim = pieces[0].shape
    vmem = pl.BlockSpec(memory_space=pltpu.VMEM)
    return pl.pallas_call(
        copies_kernel,
        in_specs=[pl.BlockSpec(memory_space=pltpu.SMEM)] + [vmem] * Z,
        out_specs=vmem,
        out_shape=jax.ShapeDtypeStruct((Y * C, Z * lines, v_dim), BF16),
        name="copies",
    )(z.reshape(1), *pieces)


def local(query, cache, grad_out, value_weight, picked):
    q_dev, heads_here, width = query.shape
    block_count = cache.shape[0] // BLOCK
    seq = lax.axis_index("seq")
    x = lax.axis_index("head")
    z, y, c = seq // (Y * C), seq // C % Y, seq % C
    peers = Y * C
    quarter = BLOCK // X
    g_here = q_dev // QB
    others = g_here * OTHERS
    rows = q_dev * heads_here

    own_id = FIRST_OWN_OWNER * block_count + seq
    is_other = picked != own_id
    rank = jnp.cumsum(is_other.astype(jnp.int32), axis=1) - 1
    at_rank = is_other[:, :, None] & (rank[:, :, None] == jnp.arange(OTHERS, dtype=jnp.int32))
    ids = jnp.sum(jnp.where(at_rank, picked[:, :, None], 0), axis=1).reshape(others)
    owner, block = ids // block_count, ids % block_count
    place = owner % peers * Z_FULL + owner // peers
    places = peers * Z_FULL
    asked = place[:, None] == jnp.arange(places, dtype=jnp.int32)[None, :]
    wanted = jnp.max(jnp.where(asked, block[:, None], -1), axis=0)
    asked_here = trade_yc(wanted.reshape(peers, 1, Z_FULL)).reshape(peers, Z_FULL)
    z_off = (jnp.arange(Z_FULL, dtype=jnp.int32) - z) % Z
    valid = (asked_here >= 0).reshape(places)
    at_piece = (z_off[None, :] * block_count + asked_here).reshape(places)

    part_rows = jnp.arange(block_count * quarter, dtype=jnp.int32)
    part_rows = part_rows // quarter * BLOCK + x * quarter + part_rows % quarter
    take_part = part_rows[:, None] == jnp.arange(cache.shape[0], dtype=jnp.int32)[None, :]
    part = jnp.dot(take_part.astype(BF16), cache, preferred_element_type=F32)
    part = narrow(part).reshape(block_count, quarter, width)
    steps = (4, -3, 3, -2, 2, -1, 1)
    pieces = [part] + [None] * (Z - 1)
    for step in steps:
        pieces[-step % Z] = shift_z(part, step, lambda z: z < Z_FULL)
    owns = []
    for j in range(block_count):
        owns.append(
            lax.ppermute(
                part[j],
                "seq",
                [
                    (o, (o - FIRST_OWN_OWNER) * block_count + j)
                    for o in range(FIRST_OWN_OWNER, Z * peers)
                ],
            )
        )
    packed = pack(jnp.maximum(asked_here, 0).reshape(places), z, pieces)
    fetched = trade_yc(packed.reshape(peers, Z_FULL, quarter, width))
    d_latent = narrow(
        jnp.einsum("qhv,hcv->qhc", grad_out, value_weight, preferred_element_type=F32)
    )
    fetched, d_latent, query_rows = lax.optimization_barrier(
        (fetched, d_latent.reshape(rows, KVL), query.reshape(rows, width))
    )
    low, high = pick(place, seq % block_count, fetched.reshape(places, quarter, width), owns)

    low_from_left = shift_x(low, 1)
    high_from_right = shift_x(high, -1)
    low_from_right = shift_x(low, -1)
    high_from_left = shift_x(high, 1)
    low_far = shift_x(low_from_left, 1)
    high_far = shift_x(high_from_right, -1)

    d_query, latent_out, *d_keys = attend(
        x,
        query_rows,
        d_latent,
        [low, low_from_left, low_far, low_from_right],
        [high, high_from_left, high_far, high_from_right],
    )
    d_low, d_high = d_keys[:X], d_keys[X:]

    low_relay = shift_x(d_low[2], -1)
    high_relay = shift_x(d_high[2], 1)
    high_left = shift_x(d_high[1], -1)
    low_right = shift_x(d_low[3], 1)
    low_pair = narrow(wide(low_relay) + wide(d_low[1]))
    high_pair = narrow(wide(high_relay) + wide(d_high[3]))
    low_left = shift_x(low_pair, -1)
    high_right = shift_x(high_pair, 1)

    terms = narrow(
        jnp.einsum(
            "qhc,qhv->hcv",
            latent_out.reshape(q_dev, heads_here, KVL),
            grad_out,
            preferred_element_type=F32,
        )
    )
    v_dim = terms.shape[-1]
    terms = terms.reshape(Y, C, -1, v_dim)
    arrived = swap_core(lax.dynamic_index_in_dim(terms, 1 - c, 1, keepdims=False))
    folded = list(fold_core(y, c, terms, arrived))
    for step in (2, -1, 1):
        folded[step % Y] = shift_y(folded[step % Y], step)
    folded = fold_y(z, folded)
    total = wide(folded[0])
    for step in steps:
        total = total + wide(shift_z(folded[step % Z], step))
    total = narrow(total)
    pieces = [total] * Z
    for step in steps:
        pieces[-step % Z] = shift_z(total, step)
    terms = trade_yc(copies(z, pieces))
    d_value_weight = terms.reshape(value_weight.shape)

    back, own_share = send_back(
        place, [d_low[0], low_right, low_left], [d_high[0], high_left, high_right], places
    )
    received = trade_yc(back.reshape(peers, Z_FULL, quarter, width))
    own_back = []
    for j in range(block_count):
        own_back.append(
            lax.ppermute(
                own_share,
                "seq",
                [
                    ((o - FIRST_OWN_OWNER) * block_count + j, o)
                    for o in range(FIRST_OWN_OWNER, Z * peers)
                ],
            )
        )
    by_z = by_owner(
        jnp.where(valid, at_piece, Z * block_count),
        received.reshape(places, quarter, width),
        block_count,
    )
    d_cache = wide(by_z[0]) + wide(jnp.stack(own_back))
    for step in steps:
        arrived = shift_z(by_z[step % Z], step, lambda z: (z + step) % Z < Z_FULL)
        d_cache = d_cache + wide(arrived)
    return d_query.reshape(query.shape), d_cache, d_value_weight


def solution(mesh):
    in_specs = (
        P("seq", "head", None),
        P("seq", None),
        P("seq", "head", None),
        P("head", None, None),
        P("seq", None),
    )
    out_specs = (P("seq", "head", None), P("seq", "head", None), P("head", None, None))
    return jax.shard_map(local, mesh=mesh, in_specs=in_specs, out_specs=out_specs, check_vma=False)
```

profile of v0, /device:TPU:1, one launch (start us, length us, event | category | flops | bytes accessed | tf_op | source)
XLA Modules:
  0.0 365.0 jit_solution(10231765439051060985)
XLA Ops:
  2.2 4.4 %collective-permute-start.6 = (bf16[4,32,576]{2,1,0:T(8,128)(2,1)S(1)}, bf16[4,32,576]{2,1,0:T(8,128)(2,1)S(1)}, u32[]{:S(2)}, u32[]{:S(2)}) collective-permute-start(bf16[4,32,576]{2,1,0:T(8,128)(2,1)S(1)} %bitcast.35), channel_id=1, source_target_pairs={{0,32},{4,36},{8,40},{12,44},{16,48},{20,52},{24,56},{28,60},{32,6... | collective-permute-start | bytes 442376 | tf_op jit(solution)/shard_map/ppermute | solution.py:39
  6.6 4.9 %collective-permute-start.5 = (bf16[4,32,576]{2,1,0:T(8,128)(2,1)S(1)}, bf16[4,32,576]{2,1,0:T(8,128)(2,1)S(1)}, u32[]{:S(2)}, u32[]{:S(2)}) collective-permute-start(bf16[4,32,576]{2,1,0:T(8,128)(2,1)S(1)} %bitcast.36), channel_id=1, source_target_pairs={{0,64},{4,68},{8,72},{12,76},{16,80},{20,84},{24,88},{28,92},{32,9... | collective-permute-start | bytes 442376 | tf_op jit(solution)/shard_map/ppermute | solution.py:39
  11.5 5.7 %collective-permute-start.4 = (bf16[4,32,576]{2,1,0:T(8,128)(2,1)S(1)}, bf16[4,32,576]{2,1,0:T(8,128)(2,1)S(1)}, u32[]{:S(2)}, u32[]{:S(2)}) collective-permute-start(bf16[4,32,576]{2,1,0:T(8,128)(2,1)S(1)} %bitcast.37), channel_id=1, source_target_pairs={{0,96},{4,100},{8,104},{12,108},{16,112},{20,116},{24,120},{28,124... | collective-permute-start | bytes 442376 | tf_op jit(solution)/shard_map/ppermute | solution.py:39
  19.1 5.7 %collective-permute-start.2 = (bf16[4,32,576]{2,1,0:T(8,128)(2,1)S(1)}, bf16[4,32,576]{2,1,0:T(8,128)(2,1)S(1)}, u32[]{:S(2)}, u32[]{:S(2)}) collective-permute-start(bf16[4,32,576]{2,1,0:T(8,128)(2,1)S(1)} %bitcast.39), channel_id=1, source_target_pairs={{0,160},{4,164},{8,168},{12,172},{16,176},{20,180},{24,184},{28,18... | collective-permute-start | bytes 442376 | tf_op jit(solution)/shard_map/ppermute | solution.py:39
  27.5 6.3 %all-to-all-start = ((s32[8,1,6]{2,1,0:T(1,128)}), s32[8,1,6]{2,1,0:T(1,128)S(1)}, u32[]{:S(2)}, u32[]{:S(2)}) async-start(s32[8,1,6]{2,1,0:T(1,128)} %bitcast.1), calls=%async_computation | async-start | bytes 8192 | tf_op jit(solution)/shard_map/all_to_all | solution.py:62
  33.8 4.6 %all-to-all-done = s32[8,1,6]{2,1,0:T(1,128)S(1)} async-done(((s32[8,1,6]{2,1,0:T(1,128)}), s32[8,1,6]{2,1,0:T(1,128)S(1)}, u32[]{:S(2)}, u32[]{:S(2)}) %all-to-all-start) | async-done | bytes 224 | tf_op jit(solution)/shard_map/all_to_all | solution.py:62
  44.2 5.6 %collective-permute-done.1.refs_2_ = bf16[4,32,576]{2,1,0:T(8,128)(2,1)S(1)} collective-permute-done((bf16[4,32,576]{2,1,0:T(8,128)(2,1)S(1)}, bf16[4,32,576]{2,1,0:T(8,128)(2,1)S(1)}, u32[]{:S(2)}, u32[]{:S(2)}) %collective-permute-start.1) | collective-permute-done | bytes 147488 | tf_op jit(solution)/shard_map/ppermute | solution.py:39
  52.3 61.4 %pack.1 = bf16[48,32,576]{2,1,0:T(8,128)(2,1)} custom-call(s32[48]{0:T(128)} %get-tuple-element.96.block_ref, s32[1]{0:T(128)} %bitcast.2.z_ref, bf16[4,32,576]{2,1,0:T(8,128)(2,1)} %bitcast.42, bf16[4,32,576]{2,1,0:T(8,128)(2,1)} %copy-done.24, bf16[4,32,576]{2,1,0:T(8,128)(2,1)} %copy-done.23, bf16[4,32,576]{2,1,0:T(8,128)(2,1)} %copy-done.22, ...), custom_call_target="tpu_custom_call" | custom-call | tf_op jit(solution)/shard_map/pack/pallas_call | solution.py:94
  113.7 5.8 %all-to-all-start.1 = ((bf16[8,6,32,576]{3,2,1,0:T(8,128)(2,1)}), bf16[8,6,32,576]{3,2,1,0:T(8,128)(2,1)}, u32[]{:S(2)}, u32[]{:S(2)}) async-start(bf16[8,6,32,576]{3,2,1,0:T(8,128)(2,1)} %bitcast.32), calls=%async_computation.1 | async-start | bytes 3932160 | tf_op jit(solution)/shard_map/all_to_all | solution.py:62
  124.9 4.1 %copy.34 = bf16[128,16,512]{2,1,0:T(8,128)(2,1)} copy(bf16[128,16,512]{2,0,1:T(8,128)(2,1)} %convert_bitcast_fusion) | data formatting | bytes 4194304 | tf_op jit(solution)/shard_map/convert_element_type | solution.py:68
  128.9 4.9 %copy.35 = bf16[128,16,576]{2,1,0:T(8,128)(2,1)} copy(bf16[128,16,576]{0,2,1:T(8,128)(2,1)} %param.5) | data formatting | bytes 4718592 | tf_op args[0]
  133.8 10.6 %all-to-all-done.1 = bf16[8,6,32,576]{3,2,1,0:T(8,128)(2,1)} async-done(((bf16[8,6,32,576]{3,2,1,0:T(8,128)(2,1)}), bf16[8,6,32,576]{3,2,1,0:T(8,128)(2,1)}, u32[]{:S(2)}, u32[]{:S(2)}) %all-to-all-start.1) | async-done | bytes 1769504 | tf_op jit(solution)/shard_map/all_to_all | solution.py:62
  145.1 17.9 %pick.1 = (bf16[7,32,576]{2,1,0:T(8,128)(2,1)}, bf16[6,32,576]{2,1,0:T(8,128)(2,1)}) custom-call(s32[12]{0:T(128)} %copy-done.4, s32[1]{0:T(128)} %bitcast.8.own_ref, bf16[48,32,576]{2,1,0:T(8,128)(2,1)} %bitcast.9.fetched_ref, bf16[32,576]{1,0:T(8,128)(2,1)} %copy-done.32, bf16[32,576]{1,0:T(8,128)(2,1)} %copy-done.31, bf16[32,576]{1,0:T(8,128)(2,1)} %copy-done.30, ...), custom_call_target="tpu_custom_call" | custom-call | tf_op jit(solution)/shard_map/pick/pallas_call | solution.py:130
  167.0 4.9 %collective-permute-done.11.refs_1_.refs_5_ = bf16[7,32,576]{2,1,0:T(8,128)(2,1)S(1)} collective-permute-done((bf16[7,32,576]{2,1,0:T(8,128)(2,1)}, bf16[7,32,576]{2,1,0:T(8,128)(2,1)S(1)}, u32[]{:S(2)}, u32[]{:S(2)}) %collective-permute-start.11) | collective-permute-done | bytes 258080 | tf_op jit(solution)/shard_map/ppermute | solution.py:57
  174.7 10.4 %collective-permute-done.14.refs_9_ = bf16[6,32,576]{2,1,0:T(8,128)(2,1)} collective-permute-done((bf16[6,32,576]{2,1,0:T(8,128)(2,1)}, bf16[6,32,576]{2,1,0:T(8,128)(2,1)}, u32[]{:S(2)}, u32[]{:S(2)}) %collective-permute-start.14) | collective-permute-done | bytes 221216 | tf_op jit(solution)/shard_map/ppermute | solution.py:57
  185.9 14.6 %attend.1 = (bf16[2048,576]{1,0:T(8,128)(2,1)}, bf16[2048,512]{1,0:T(8,128)(2,1)}, bf16[7,32,576]{2,1,0:T(8,128)(2,1)}, bf16[7,32,576]{2,1,0:T(8,128)(2,1)}, bf1...) custom-call(s32[1]{0:T(128)} %bitcast.x_ref, ...), custom_call_target="tpu_custom_call" | custom-call | tf_op jit(solution)/shard_map/attend/pallas_call | solution.py:238
  204.9 4.1 %fusion.2 = bf16[16,512,128]{2,1,0:T(8,128)(2,1)S(1)} fusion(bf16[128,16,512]{2,1,0:T(8,128)(2,1)} %bitcast.34, bf16[128,16,128]{2,1,0:T(8,128)(2,1)S(1)} %copy-done.7), kind=kOutput, calls=%fused_computation.3 | convolution fusion | flops 269484032 | bytes 4718592 | tf_op jit(solution)/shard_map/qhc,qhv->hcv/dot_general | solution.py:477
  221.0 8.2 %all-to-all-start.2 = ((bf16[8,6,32,576]{3,2,1,0:T(8,128)(2,1)}), bf16[8,6,32,576]{3,2,1,0:T(8,128)(2,1)}, u32[]{:S(2)}, u32[]{:S(2)}) async-start(bf16[8,6,32,576]{3,2,1,0:T(8,128)(2,1)} %bitcast.27), calls=%async_computation.2 | async-start | bytes 3932160 | tf_op jit(solution)/shard_map/all_to_all | solution.py:62
  234.3 9.8 %collective-permute-start.36 = (bf16[1024,128]{1,0:T(8,128)(2,1)}, bf16[1024,128]{1,0:T(8,128)(2,1)S(1)}, u32[]{:S(2)}, u32[]{:S(2)}) collective-permute-start(bf16[1024,128]{1,0:T(8,128)(2,1)} %get-tuple-element.67), channel_id=1, source_target_pairs={{0,16},{4,20},{8,24},{12,28},{16,0},{20,4},{24,8},{28,12},{32,48},... | collective-permute-start | bytes 786440 | tf_op jit(solution)/shard_map/ppermute | solution.py:49
  244.1 11.8 %collective-permute-start.37 = (bf16[1024,128]{1,0:T(8,128)(2,1)}, bf16[1024,128]{1,0:T(8,128)(2,1)S(1)}, u32[]{:S(2)}, u32[]{:S(2)}) collective-permute-start(bf16[1024,128]{1,0:T(8,128)(2,1)} %get-tuple-element.68), channel_id=1, source_target_pairs={{0,24},{4,28},{8,0},{12,4},{16,8},{20,12},{24,16},{28,20},{32,56},... | collective-permute-start | bytes 786440 | tf_op jit(solution)/shard_map/ppermute | solution.py:49
  255.9 3.7 %collective-permute-done.35.refs_1_ = bf16[1024,128]{1,0:T(8,128)(2,1)S(1)} collective-permute-done((bf16[1024,128]{1,0:T(8,128)(2,1)}, bf16[1024,128]{1,0:T(8,128)(2,1)S(1)}, u32[]{:S(2)}, u32[]{:S(2)}) %collective-permute-start.35) | collective-permute-done | bytes 262176 | tf_op jit(solution)/shard_map/ppermute | solution.py:49
  259.6 5.7 %collective-permute-done.36.refs_2_ = bf16[1024,128]{1,0:T(8,128)(2,1)S(1)} collective-permute-done((bf16[1024,128]{1,0:T(8,128)(2,1)}, bf16[1024,128]{1,0:T(8,128)(2,1)S(1)}, u32[]{:S(2)}, u32[]{:S(2)}) %collective-permute-start.36) | collective-permute-done | bytes 262176 | tf_op jit(solution)/shard_map/ppermute | solution.py:49
  268.1 4.5 %collective-permute-start.38 = (bf16[128,128]{1,0:T(8,128)(2,1)}, bf16[128,128]{1,0:T(8,128)(2,1)S(1)}, u32[]{:S(2)}, u32[]{:S(2)}) collective-permute-start(bf16[128,128]{1,0:T(8,128)(2,1)} %get-tuple-element.70), channel_id=1, source_target_pairs={{0,128},{4,132},{8,136},{12,140},{16,144},{20,148},{24,152},{28,15... | collective-permute-start | bytes 98312 | tf_op jit(solution)/shard_map/ppermute | solution.py:39
  275.9 3.8 %collective-permute-start.41 = (bf16[128,128]{1,0:T(8,128)(2,1)}, bf16[128,128]{1,0:T(8,128)(2,1)S(1)}, u32[]{:S(2)}, u32[]{:S(2)}) collective-permute-start(bf16[128,128]{1,0:T(8,128)(2,1)} %get-tuple-element.73), channel_id=1, source_target_pairs={{0,192},{4,196},{8,200},{12,204},{16,208},{20,212},{24,216},{28,22... | collective-permute-start | bytes 98312 | tf_op jit(solution)/shard_map/ppermute | solution.py:39
  292.0 3.6 collective-permute-start.47
  305.0 10.1 %all-to-all-start.3 = ((bf16[8,1024,128]{2,1,0:T(8,128)(2,1)}), bf16[8,1024,128]{2,1,0:T(8,128)(2,1)}, u32[]{:S(2)}, u32[]{:S(2)}) async-start(bf16[8,1024,128]{2,1,0:T(8,128)(2,1)} %copies.1), calls=%async_computation.3 | async-start | bytes 4194304 | tf_op jit(solution)/shard_map/all_to_all | solution.py:62
  320.9 3.8 %collective-permute-start.28 = (bf16[4,32,576]{2,1,0:T(8,128)(2,1)S(1)}, bf16[4,32,576]{2,1,0:T(8,128)(2,1)S(1)}, u32[]{:S(2)}, u32[]{:S(2)}) collective-permute-start(bf16[4,32,576]{2,1,0:T(8,128)(2,1)S(1)} %get-tuple-element.58), channel_id=1, source_target_pairs={{0,160},{4,164},{8,168},{12,172},{16,176},{20,180},{24,184},{28,18... | collective-permute-start | bytes 442376 | tf_op jit(solution)/shard_map/ppermute | solution.py:39
  326.1 4.1 %collective-permute-start.24 = (bf16[32,576]{1,0:T(8,128)(2,1)S(1)}, bf16[32,576]{1,0:T(8,128)(2,1)S(1)}, u32[]{:S(2)}, u32[]{:S(2)}) collective-permute-start(bf16[32,576]{1,0:T(8,128)(2,1)S(1)} %get-tuple-element.56), channel_id=1, source_target_pairs={{4,192},{20,196},{36,200},{52,204},{68,208},{84,212},{100,216},{11... | collective-permute-start | bytes 110600 | tf_op jit(solution)/shard_map/ppermute | solution.py:508
  330.9 9.8 %collective-permute-start.29 = (bf16[4,32,576]{2,1,0:T(8,128)(2,1)S(1)}, bf16[4,32,576]{2,1,0:T(8,128)(2,1)}, u32[]{:S(2)}, u32[]{:S(2)}) collective-permute-start(bf16[4,32,576]{2,1,0:T(8,128)(2,1)S(1)} %get-tuple-element.59), channel_id=1, source_target_pairs={{0,96},{4,100},{8,104},{12,108},{16,112},{20,116},{24,120},{28,124... | collective-permute-start | bytes 442376 | tf_op jit(solution)/shard_map/ppermute | solution.py:39
  342.0 4.9 %collective-permute-start.31 = (bf16[4,32,576]{2,1,0:T(8,128)(2,1)S(1)}, bf16[4,32,576]{2,1,0:T(8,128)(2,1)}, u32[]{:S(2)}, u32[]{:S(2)}) collective-permute-start(bf16[4,32,576]{2,1,0:T(8,128)(2,1)S(1)} %get-tuple-element.61), channel_id=1, source_target_pairs={{0,64},{4,68},{8,72},{12,76},{16,80},{20,84},{24,88},{28,92},{32,9... | collective-permute-start | bytes 442376 | tf_op jit(solution)/shard_map/ppermute | solution.py:39
  348.3 4.0 %collective-permute-start.33 = (bf16[4,32,576]{2,1,0:T(8,128)(2,1)S(1)}, bf16[4,32,576]{2,1,0:T(8,128)(2,1)}, u32[]{:S(2)}, u32[]{:S(2)}) collective-permute-start(bf16[4,32,576]{2,1,0:T(8,128)(2,1)S(1)} %get-tuple-element.63), channel_id=1, source_target_pairs={{0,32},{4,36},{8,40},{12,44},{16,48},{20,52},{24,56},{28,60},{32,6... | collective-permute-start | bytes 442376 | tf_op jit(solution)/shard_map/ppermute | solution.py:39
  352.3 4.7 %copy.38 = bf16[128,16,576]{0,2,1:T(8,128)(2,1)} copy(bf16[128,16,576]{2,1,0:T(8,128)(2,1)} %bitcast.33) | data formatting | bytes 4718592
  (199 shorter events, 95.5 us)
Async XLA Ops:
  2.2 37.4 %collective-permute-start.6 = (bf16[4,32,576]{2,1,0:T(8,128)(2,1)S(1)}, bf16[4,32,576]{2,1,0:T(8,128)(2,1)S(1)}, u32[]{:S(2)}, u32[]{:S(2)}) collective-permute-start(bf16[4,32,576]{2,1,0:T(8,128)(2,1)S(1)} %bitcast.35), channel_id=1, source_target_pairs={{0,32},{4,36},{8,40},{12,44},{16,48},{20,52},{24,56},{28,60},{32,6... | collective-permute-start | bytes 442376 | tf_op jit(solution)/shard_map/ppermute | solution.py:39
  6.6 35.0 %collective-permute-start.5 = (bf16[4,32,576]{2,1,0:T(8,128)(2,1)S(1)}, bf16[4,32,576]{2,1,0:T(8,128)(2,1)S(1)}, u32[]{:S(2)}, u32[]{:S(2)}) collective-permute-start(bf16[4,32,576]{2,1,0:T(8,128)(2,1)S(1)} %bitcast.36), channel_id=1, source_target_pairs={{0,64},{4,68},{8,72},{12,76},{16,80},{20,84},{24,88},{28,92},{32,9... | collective-permute-start | bytes 442376 | tf_op jit(solution)/shard_map/ppermute | solution.py:39
  11.5 32.6 %collective-permute-start.4 = (bf16[4,32,576]{2,1,0:T(8,128)(2,1)S(1)}, bf16[4,32,576]{2,1,0:T(8,128)(2,1)S(1)}, u32[]{:S(2)}, u32[]{:S(2)}) collective-permute-start(bf16[4,32,576]{2,1,0:T(8,128)(2,1)S(1)} %bitcast.37), channel_id=1, source_target_pairs={{0,96},{4,100},{8,104},{12,108},{16,112},{20,116},{24,120},{28,124... | collective-permute-start | bytes 442376 | tf_op jit(solution)/shard_map/ppermute | solution.py:39
  17.2 27.0 %collective-permute-start.3 = (bf16[4,32,576]{2,1,0:T(8,128)(2,1)S(1)}, bf16[4,32,576]{2,1,0:T(8,128)(2,1)S(1)}, u32[]{:S(2)}, u32[]{:S(2)}) collective-permute-start(bf16[4,32,576]{2,1,0:T(8,128)(2,1)S(1)} %bitcast.38), channel_id=1, source_target_pairs={{0,128},{4,132},{8,136},{12,140},{16,144},{20,148},{24,152},{28,15... | collective-permute-start | bytes 442376 | tf_op jit(solution)/shard_map/ppermute | solution.py:39
  19.1 25.1 %collective-permute-start.2 = (bf16[4,32,576]{2,1,0:T(8,128)(2,1)S(1)}, bf16[4,32,576]{2,1,0:T(8,128)(2,1)S(1)}, u32[]{:S(2)}, u32[]{:S(2)}) collective-permute-start(bf16[4,32,576]{2,1,0:T(8,128)(2,1)S(1)} %bitcast.39), channel_id=1, source_target_pairs={{0,160},{4,164},{8,168},{12,172},{16,176},{20,180},{24,184},{28,18... | collective-permute-start | bytes 442376 | tf_op jit(solution)/shard_map/ppermute | solution.py:39
  113.7 30.7 %all-to-all-start.1 = ((bf16[8,6,32,576]{3,2,1,0:T(8,128)(2,1)}), bf16[8,6,32,576]{3,2,1,0:T(8,128)(2,1)}, u32[]{:S(2)}, u32[]{:S(2)}) async-start(bf16[8,6,32,576]{3,2,1,0:T(8,128)(2,1)} %bitcast.32), calls=%async_computation.1 | async-start | bytes 3932160 | tf_op jit(solution)/shard_map/all_to_all | solution.py:62
  119.5 24.9 %collective-permute-start.10 = (bf16[32,576]{1,0:T(8,128)(2,1)S(1)}, bf16[32,576]{1,0:T(8,128)(2,1)S(1)}, u32[]{:S(2)}, u32[]{:S(2)}) collective-permute-start(bf16[32,576]{1,0:T(8,128)(2,1)S(1)} %get-tuple-element.91), channel_id=1, source_target_pairs={{192,12},{196,28},{200,44},{204,60},{208,76},{212,92},{216,108},{2... | collective-permute-start | bytes 110600 | tf_op jit(solution)/shard_map/ppermute | solution.py:432
  120.2 24.2 %collective-permute-start.9 = (bf16[32,576]{1,0:T(8,128)(2,1)S(1)}, bf16[32,576]{1,0:T(8,128)(2,1)S(1)}, u32[]{:S(2)}, u32[]{:S(2)}) collective-permute-start(bf16[32,576]{1,0:T(8,128)(2,1)S(1)} %get-tuple-element.92), channel_id=1, source_target_pairs={{192,8},{196,24},{200,40},{204,56},{208,72},{212,88},{216,104},{22... | collective-permute-start | bytes 110600 | tf_op jit(solution)/shard_map/ppermute | solution.py:432
  120.8 23.6 %collective-permute-start.8 = (bf16[32,576]{1,0:T(8,128)(2,1)S(1)}, bf16[32,576]{1,0:T(8,128)(2,1)S(1)}, u32[]{:S(2)}, u32[]{:S(2)}) collective-permute-start(bf16[32,576]{1,0:T(8,128)(2,1)S(1)} %get-tuple-element.93), channel_id=1, source_target_pairs={{192,4},{196,20},{200,36},{204,52},{208,68},{212,84},{216,100},{22... | collective-permute-start | bytes 110600 | tf_op jit(solution)/shard_map/ppermute | solution.py:432
  122.1 22.3 %collective-permute-start.7 = (bf16[32,576]{1,0:T(8,128)(2,1)S(1)}, bf16[32,576]{1,0:T(8,128)(2,1)S(1)}, u32[]{:S(2)}, u32[]{:S(2)}) collective-permute-start(bf16[32,576]{1,0:T(8,128)(2,1)S(1)} %get-tuple-element.94), channel_id=1, source_target_pairs={{192,0},{196,16},{200,32},{204,48},{208,64},{212,80},{216,96},{220... | collective-permute-start | bytes 110600 | tf_op jit(solution)/shard_map/ppermute | solution.py:432
  165.8 19.3 %collective-permute-start.13 = (bf16[7,32,576]{2,1,0:T(8,128)(2,1)}, bf16[7,32,576]{2,1,0:T(8,128)(2,1)S(1)}, u32[]{:S(2)}, u32[]{:S(2)}) collective-permute-start(bf16[7,32,576]{2,1,0:T(8,128)(2,1)} %get-tuple-element.43.refs_0_.refs_4_), channel_id=1, source_target_pairs={{0,3},{1,0},{2,1},{3,2},{4,7},{5,4},{6,5},{7,6},{8,11},{9,8},{10,9... | collective-permute-start | bytes 774152 | tf_op jit(solution)/shard_map/ppermute | solution.py:57
  171.9 13.2 %collective-permute-start.12 = (bf16[7,32,576]{2,1,0:T(8,128)(2,1)S(1)}, bf16[7,32,576]{2,1,0:T(8,128)(2,1)S(1)}, u32[]{:S(2)}, u32[]{:S(2)}) collective-permute-start(bf16[7,32,576]{2,1,0:T(8,128)(2,1)S(1)} %collective-permute-done.11.refs_1_.refs_5_), channel_id=1, source_target_pairs={{0,1},{1,2},{2,3},{3,0},{4,5},{5,6},{6,7},{7,4},{8,9},{9,10},{10,1... | collective-permute-start | bytes 774152 | tf_op jit(solution)/shard_map/ppermute | solution.py:57
  172.0 13.1 %collective-permute-start.14 = (bf16[6,32,576]{2,1,0:T(8,128)(2,1)}, bf16[6,32,576]{2,1,0:T(8,128)(2,1)}, u32[]{:S(2)}, u32[]{:S(2)}) collective-permute-start(bf16[6,32,576]{2,1,0:T(8,128)(2,1)} %get-tuple-element.44.refs_8_), channel_id=1, source_target_pairs={{0,1},{1,2},{2,3},{3,0},{4,5},{5,6},{6,7},{7,4},{8,9},{9,10},{10,1... | collective-permute-start | bytes 663560 | tf_op jit(solution)/shard_map/ppermute | solution.py:57
  173.2 11.9 %collective-permute-start.16 = (bf16[6,32,576]{2,1,0:T(8,128)(2,1)}, bf16[6,32,576]{2,1,0:T(8,128)(2,1)}, u32[]{:S(2)}, u32[]{:S(2)}) collective-permute-start(bf16[6,32,576]{2,1,0:T(8,128)(2,1)} %collective-permute-done.15.refs_11_), channel_id=1, source_target_pairs={{0,3},{1,0},{2,1},{3,2},{4,7},{5,4},{6,5},{7,6},{8,11},{9,8},{10,9... | collective-permute-start | bytes 663560 | tf_op jit(solution)/shard_map/ppermute | solution.py:57
  200.5 17.5 %collective-permute-start.20 = (bf16[6,32,576]{2,1,0:T(8,128)(2,1)}, bf16[6,32,576]{2,1,0:T(8,128)(2,1)S(1)}, u32[]{:S(2)}, u32[]{:S(2)}) collective-permute-start(bf16[6,32,576]{2,1,0:T(8,128)(2,1)} %get-tuple-element.51), channel_id=1, source_target_pairs={{0,3},{1,0},{2,1},{3,2},{4,7},{5,4},{6,5},{7,6},{8,11},{9,8},{10,9... | collective-permute-start | bytes 663560 | tf_op jit(solution)/shard_map/ppermute | solution.py:57
  202.2 15.7 %collective-permute-start.17 = (bf16[7,32,576]{2,1,0:T(8,128)(2,1)}, bf16[7,32,576]{2,1,0:T(8,128)(2,1)S(1)}, u32[]{:S(2)}, u32[]{:S(2)}) collective-permute-start(bf16[7,32,576]{2,1,0:T(8,128)(2,1)} %get-tuple-element.47), channel_id=1, source_target_pairs={{0,1},{1,2},{2,3},{3,0},{4,5},{5,6},{6,7},{7,4},{8,9},{9,10},{10,1... | collective-permute-start | bytes 774152 | tf_op jit(solution)/shard_map/ppermute | solution.py:57
  215.0 14.9 %collective-permute-start.34 = (bf16[4,1024,128]{2,1,0:T(8,128)(2,1)S(1)}, bf16[4,1024,128]{2,1,0:T(8,128)(2,1)}, u32[]{:S(2)}, u32[]{:S(2)}) collective-permute-start(bf16[4,1024,128]{2,1,0:T(8,128)(2,1)S(1)} %dynamic-slice_bitcast_fusion), channel_id=1, source_target_pairs={{0,4},{4,0},{8,12},{12,8},{16,20},{20,16},{24,28},{28,24},{32,36},... | collective-permute-start | bytes 3145736 | tf_op jit(solution)/shard_map/ppermute | solution.py:53
  221.0 84.0 %all-to-all-start.2 = ((bf16[8,6,32,576]{3,2,1,0:T(8,128)(2,1)}), bf16[8,6,32,576]{3,2,1,0:T(8,128)(2,1)}, u32[]{:S(2)}, u32[]{:S(2)}) async-start(bf16[8,6,32,576]{3,2,1,0:T(8,128)(2,1)} %bitcast.27), calls=%async_computation.2 | async-start | bytes 3932160 | tf_op jit(solution)/shard_map/all_to_all | solution.py:62
  232.9 26.7 %collective-permute-start.35 = (bf16[1024,128]{1,0:T(8,128)(2,1)}, bf16[1024,128]{1,0:T(8,128)(2,1)S(1)}, u32[]{:S(2)}, u32[]{:S(2)}) collective-permute-start(bf16[1024,128]{1,0:T(8,128)(2,1)} %get-tuple-element.66), channel_id=1, source_target_pairs={{0,8},{4,12},{8,16},{12,20},{16,24},{20,28},{24,0},{28,4},{32,40},... | collective-permute-start | bytes 786440 | tf_op jit(solution)/shard_map/ppermute | solution.py:49
  234.3 31.1 %collective-permute-start.36 = (bf16[1024,128]{1,0:T(8,128)(2,1)}, bf16[1024,128]{1,0:T(8,128)(2,1)S(1)}, u32[]{:S(2)}, u32[]{:S(2)}) collective-permute-start(bf16[1024,128]{1,0:T(8,128)(2,1)} %get-tuple-element.67), channel_id=1, source_target_pairs={{0,16},{4,20},{8,24},{12,28},{16,0},{20,4},{24,8},{28,12},{32,48},... | collective-permute-start | bytes 786440 | tf_op jit(solution)/shard_map/ppermute | solution.py:49
  244.1 21.3 %collective-permute-start.37 = (bf16[1024,128]{1,0:T(8,128)(2,1)}, bf16[1024,128]{1,0:T(8,128)(2,1)S(1)}, u32[]{:S(2)}, u32[]{:S(2)}) collective-permute-start(bf16[1024,128]{1,0:T(8,128)(2,1)} %get-tuple-element.68), channel_id=1, source_target_pairs={{0,24},{4,28},{8,0},{12,4},{16,8},{20,12},{24,16},{28,20},{32,56},... | collective-permute-start | bytes 786440 | tf_op jit(solution)/shard_map/ppermute | solution.py:49
  268.1 11.5 %collective-permute-start.38 = (bf16[128,128]{1,0:T(8,128)(2,1)}, bf16[128,128]{1,0:T(8,128)(2,1)S(1)}, u32[]{:S(2)}, u32[]{:S(2)}) collective-permute-start(bf16[128,128]{1,0:T(8,128)(2,1)} %get-tuple-element.70), channel_id=1, source_target_pairs={{0,128},{4,132},{8,136},{12,140},{16,144},{20,148},{24,152},{28,15... | collective-permute-start | bytes 98312 | tf_op jit(solution)/shard_map/ppermute | solution.py:39
  286.3 12.4 %collective-permute-start.50 = (bf16[128,128]{1,0:T(8,128)(2,1)S(1)}, bf16[128,128]{1,0:T(8,128)(2,1)S(1)}, u32[]{:S(2)}, u32[]{:S(2)}) collective-permute-start(bf16[128,128]{1,0:T(8,128)(2,1)S(1)} %add_convert_fusion.2.refs_0_), channel_id=1, source_target_pairs={{0,64},{4,68},{8,72},{12,76},{16,80},{20,84},{24,88},{28,92},{32,9... | collective-permute-start | bytes 98312 | tf_op jit(solution)/shard_map/ppermute | solution.py:39
  288.3 11.9 %collective-permute-start.49 = (bf16[128,128]{1,0:T(8,128)(2,1)S(1)}, bf16[128,128]{1,0:T(8,128)(2,1)S(1)}, u32[]{:S(2)}, u32[]{:S(2)}) collective-permute-start(bf16[128,128]{1,0:T(8,128)(2,1)S(1)} %add_convert_fusion.2.refs_0_), channel_id=1, source_target_pairs={{0,96},{4,100},{8,104},{12,108},{16,112},{20,116},{24,120},{28,124... | collective-permute-start | bytes 98312 | tf_op jit(solution)/shard_map/ppermute | solution.py:39
  305.0 56.9 %all-to-all-start.3 = ((bf16[8,1024,128]{2,1,0:T(8,128)(2,1)}), bf16[8,1024,128]{2,1,0:T(8,128)(2,1)}, u32[]{:S(2)}, u32[]{:S(2)}) async-start(bf16[8,1024,128]{2,1,0:T(8,128)(2,1)} %copies.1), calls=%async_computation.3 | async-start | bytes 4194304 | tf_op jit(solution)/shard_map/all_to_all | solution.py:62
  317.3 29.6 %collective-permute-start.27 = (bf16[4,32,576]{2,1,0:T(8,128)(2,1)S(1)}, bf16[4,32,576]{2,1,0:T(8,128)(2,1)S(1)}, u32[]{:S(2)}, u32[]{:S(2)}) collective-permute-start(bf16[4,32,576]{2,1,0:T(8,128)(2,1)S(1)} %get-tuple-element.57), channel_id=1, source_target_pairs={{0,128},{4,132},{8,136},{12,140},{16,144},{20,148},{24,152},{28,15... | collective-permute-start | bytes 442376 | tf_op jit(solution)/shard_map/ppermute | solution.py:39
  320.9 27.3 %collective-permute-start.28 = (bf16[4,32,576]{2,1,0:T(8,128)(2,1)S(1)}, bf16[4,32,576]{2,1,0:T(8,128)(2,1)S(1)}, u32[]{:S(2)}, u32[]{:S(2)}) collective-permute-start(bf16[4,32,576]{2,1,0:T(8,128)(2,1)S(1)} %get-tuple-element.58), channel_id=1, source_target_pairs={{0,160},{4,164},{8,168},{12,172},{16,176},{20,180},{24,184},{28,18... | collective-permute-start | bytes 442376 | tf_op jit(solution)/shard_map/ppermute | solution.py:39
  326.1 14.6 %collective-permute-start.24 = (bf16[32,576]{1,0:T(8,128)(2,1)S(1)}, bf16[32,576]{1,0:T(8,128)(2,1)S(1)}, u32[]{:S(2)}, u32[]{:S(2)}) collective-permute-start(bf16[32,576]{1,0:T(8,128)(2,1)S(1)} %get-tuple-element.56), channel_id=1, source_target_pairs={{4,192},{20,196},{36,200},{52,204},{68,208},{84,212},{100,216},{11... | collective-permute-start | bytes 110600 | tf_op jit(solution)/shard_map/ppermute | solution.py:508
  330.2 11.8 %collective-permute-start.23 = (bf16[32,576]{1,0:T(8,128)(2,1)S(1)}, bf16[32,576]{1,0:T(8,128)(2,1)S(1)}, u32[]{:S(2)}, u32[]{:S(2)}) collective-permute-start(bf16[32,576]{1,0:T(8,128)(2,1)S(1)} %get-tuple-element.56), channel_id=1, source_target_pairs={{0,192},{16,196},{32,200},{48,204},{64,208},{80,212},{96,216},{112... | collective-permute-start | bytes 110600 | tf_op jit(solution)/shard_map/ppermute | solution.py:508
  330.9 26.1 %collective-permute-start.29 = (bf16[4,32,576]{2,1,0:T(8,128)(2,1)S(1)}, bf16[4,32,576]{2,1,0:T(8,128)(2,1)}, u32[]{:S(2)}, u32[]{:S(2)}) collective-permute-start(bf16[4,32,576]{2,1,0:T(8,128)(2,1)S(1)} %get-tuple-element.59), channel_id=1, source_target_pairs={{0,96},{4,100},{8,104},{12,108},{16,112},{20,116},{24,120},{28,124... | collective-permute-start | bytes 442376 | tf_op jit(solution)/shard_map/ppermute | solution.py:39
  340.7 16.3 %collective-permute-start.30 = (bf16[4,32,576]{2,1,0:T(8,128)(2,1)S(1)}, bf16[4,32,576]{2,1,0:T(8,128)(2,1)}, u32[]{:S(2)}, u32[]{:S(2)}) collective-permute-start(bf16[4,32,576]{2,1,0:T(8,128)(2,1)S(1)} %get-tuple-element.60), channel_id=1, source_target_pairs={{64,0},{68,4},{72,8},{76,12},{80,16},{84,20},{88,24},{92,28},{96,3... | collective-permute-start | bytes 442376 | tf_op jit(solution)/shard_map/ppermute | solution.py:39
  342.0 14.9 %collective-permute-start.31 = (bf16[4,32,576]{2,1,0:T(8,128)(2,1)S(1)}, bf16[4,32,576]{2,1,0:T(8,128)(2,1)}, u32[]{:S(2)}, u32[]{:S(2)}) collective-permute-start(bf16[4,32,576]{2,1,0:T(8,128)(2,1)S(1)} %get-tuple-element.61), channel_id=1, source_target_pairs={{0,64},{4,68},{8,72},{12,76},{16,80},{20,84},{24,88},{28,92},{32,9... | collective-permute-start | bytes 442376 | tf_op jit(solution)/shard_map/ppermute | solution.py:39
  (64 other events, 643.0 us)
where the time goes:
time: 372 us; the launch traced here: 365 us
  starting transfers between devices  162 us (44%)
  Pallas kernels  105 us (28%)
  waiting for transfers between devices  59.3 us (16%)
  local copies, waits for them, and re-layouts  23.2 us (6%)
  matrix products  7.68 us (2%)
  other arithmetic  6.85 us (2%)
    ppermute x28, starting transfers between devices, shift_z(): return lax.ppermute(array, 'seq', pairs)  81.9 us
    pallas_call x1, Pallas kernels, pack(): pl.pallas_call(pack_kernel, in_specs=[smem, smem] + [hbm] * Z, out_specs=...  61.4 us
    all_to_all x4, starting transfers between devices, trade_yc(): lax.all_to_all(blocks, 'seq', split_axis=0, concat_axis=0, axis_index_gro...  30.3 us
    ppermute x3, starting transfers between devices, shift_y(): return lax.ppermute(array, 'seq', pairs)  23 us
    ppermute x12, waiting for transfers between devices, shift_x(): return lax.ppermute(array, 'head', [(x, (x + step) % X) for x in range(X)])  18.6 us
    pallas_call x1, Pallas kernels, pick(): pl.pallas_call(pick_kernel, in_specs=[smem, smem, hbm] + [hbm] * len(owns...  17.9 us
    unnamed x83, local copies, waits for them, and re-layouts  17.5 us
    ppermute x28, waiting for transfers between devices, shift_z(): return lax.ppermute(array, 'seq', pairs)  16.1 us
  transfers between devices with their start and end apart: 56, of which 14 were waited for; matrix products, arithmetic and copies ran while one was open for 8% of the time, Pallas kernels for 3%

commit v1 on v0

--- a/solution.py
+++ b/solution.py
@@ -39,9 +39,30 @@
     return lax.ppermute(array, "seq", pairs)
 
 
-def shift_y(array, step):
+def gather_z(own, limit):
+    right, left = [own], [own]
+    for hop in range(4):
+        right.append(shift_z(right[-1], 1, lambda z: (z - hop) % Z < limit))
+        if hop < 3:
+            left.append(shift_z(left[-1], -1, lambda z: (z + hop) % Z < limit))
+    return [own, left[1], left[2], left[3], right[4], right[3], right[2], right[1]]
+
+
+def reduce_z(terms, limit):
+    right, left = terms[4], terms[5]
+    for hop in range(4):
+        right = shift_z(right, 1, lambda z: (z + 4 - hop) % Z < limit)
+        if hop < 3:
+            right = narrow(wide(right) + wide(terms[3 - hop]))
+            left = shift_z(left, -1, lambda z: (z - 3 + hop) % Z < limit)
+        if hop < 2:
+            left = narrow(wide(left) + wide(terms[6 + hop]))
+    return wide(terms[0]) + wide(right) + wide(left)
+
+
+def shift_yc(array, y_step, c_step):
     pairs = [
-        (seq_of(z, y, c), seq_of(z, y + step, c))
+        (seq_of(z, y, c), seq_of(z, y + y_step, c ^ c_step))
         for z in range(Z)
         for y in range(Y)
         for c in range(C)
@@ -57,13 +78,17 @@
     return lax.ppermute(array, "head", [(x, (x + step) % X) for x in range(X)])
 
 
-def trade_yc(blocks):
-    groups = [[seq_of(z, 0, 0) + i for i in range(Y * C)] for z in range(Z)]
+def trade(blocks, groups):
     return lax.all_to_all(
         blocks, "seq", split_axis=0, concat_axis=0, axis_index_groups=groups, tiled=True
     )
 
 
+YC_GROUPS = [[seq_of(z, y, c) for y in range(Y) for c in range(C)] for z in range(Z)]
+Y_GROUPS = [[seq_of(z, y, c) for y in range(Y)] for z in range(Z) for c in range(C)]
+Z_GROUPS = [[seq_of(z, y, c) for z in range(Z)] for y in range(Y) for c in range(C)]
+
+
 def narrow(array):
     return array.astype(BF16)
 
@@ -73,7 +98,7 @@
 
 
 def pack_kernel(block_ref, z_ref, *refs):
-    pieces, out_ref, sem = refs[:Z], refs[Z], refs[Z + 1]
+    pieces, out_ref = refs[:Z], refs[Z]
     for j in range(Z):
         owner_z = (z_ref[0] + j) % Z
 
@@ -81,61 +106,49 @@
         def _():
             for peer in range(Y * C):
                 place = peer * Z_FULL + owner_z
-                pltpu.make_async_copy(
-                    pieces[j].at[block_ref[place]], out_ref.at[place], sem
-                ).start()
-
-    pltpu.make_async_copy(out_ref, out_ref, sem).wait()
+                out_ref[place] = pieces[j][block_ref[place]]
 
 
 def pack(blocks, z, pieces):
-    hbm = pl.BlockSpec(memory_space=pltpu.HBM)
+    vmem = pl.BlockSpec(memory_space=pltpu.VMEM)
     smem = pl.BlockSpec(memory_space=pltpu.SMEM)
     return pl.pallas_call(
         pack_kernel,
-        in_specs=[smem, smem] + [hbm] * Z,
-        out_specs=hbm,
+        in_specs=[smem, smem] + [vmem] * Z,
+        out_specs=vmem,
         out_shape=jax.ShapeDtypeStruct((blocks.shape[0], *pieces[0].shape[1:]), BF16),
-        scratch_shapes=[pltpu.SemaphoreType.DMA],
         name="pack",
     )(blocks, z.reshape(1), *pieces)
 
 
 def pick_kernel(place_ref, own_ref, fetched_ref, *refs):
-    owns, (low_ref, high_ref, low_sem, high_sem) = refs[:-4], refs[-4:]
+    owns, (low_ref, high_ref) = refs[:-2], refs[-2:]
     n_low, n_high = low_ref.shape[0], high_ref.shape[0]
     for j, own in enumerate(owns):
 
         @pl.when(own_ref[0] == j)
         def _():
-            pltpu.make_async_copy(own, low_ref.at[n_low - 1], low_sem).start()
+            low_ref[n_low - 1] = own[...]
 
     for slot in range(n_low - 1):
-        pltpu.make_async_copy(
-            fetched_ref.at[place_ref[slot]], low_ref.at[slot], low_sem
-        ).start()
+        low_ref[slot] = fetched_ref[place_ref[slot]]
     for slot in range(n_high):
-        pltpu.make_async_copy(
-            fetched_ref.at[place_ref[n_low - 1 + slot]], high_ref.at[slot], high_sem
-        ).start()
-    pltpu.make_async_copy(low_ref, low_ref, low_sem).wait()
-    pltpu.make_async_copy(high_ref, high_ref, high_sem).wait()
+        high_ref[slot] = fetched_ref[place_ref[n_low - 1 + slot]]
 
 
 def pick(place, own_index, fetched, owns):
-    hbm = pl.BlockSpec(memory_space=pltpu.HBM)
+    vmem = pl.BlockSpec(memory_space=pltpu.VMEM)
     smem = pl.BlockSpec(memory_space=pltpu.SMEM)
     n_high = place.shape[0] // 2
     n_low = place.shape[0] - n_high + 1
     return pl.pallas_call(
         pick_kernel,
-        in_specs=[smem, smem, hbm] + [hbm] * len(owns),
-        out_specs=[hbm, hbm],
+        in_specs=[smem, smem, vmem] + [vmem] * len(owns),
+        out_specs=[vmem, vmem],
         out_shape=[
             jax.ShapeDtypeStruct((n_low, *fetched.shape[1:]), BF16),
             jax.ShapeDtypeStruct((n_high, *fetched.shape[1:]), BF16),
         ],
-        scratch_shapes=[pltpu.SemaphoreType.DMA] * 2,
         name="pick",
     )(place, own_index.reshape(1), fetched, *owns)
 
@@ -272,7 +285,7 @@
 
 def send_back_kernel(at_ref, *refs):
     low_refs, high_refs = refs[:3], refs[3:6]
-    out_ref, own_ref, total = refs[6:]
+    out_refs, own_ref, total = refs[6:-2], refs[-2], refs[-1]
     n_low, n_high = low_refs[0].shape[0], high_refs[0].shape[0]
     total[...] = jnp.zeros_like(total)
     for slot in range(n_low + n_high - 1):
@@ -283,111 +296,48 @@
     own_ref[...] = narrow(
         wide(low_refs[0][last]) + wide(low_refs[1][last]) + wide(low_refs[2][last])
     )
-    out_ref[...] = narrow(total[...])
-
-
-def send_back(at, low, high, places, interpret=False):
+    for j, out_ref in enumerate(out_refs):
+        out_ref[...] = narrow(total[j * Z_FULL : (j + 1) * Z_FULL])
+
+
+def send_back(at, low, high):
     _, quarter, width = low[0].shape
     vmem = pl.BlockSpec(memory_space=pltpu.VMEM)
     return pl.pallas_call(
         send_back_kernel,
         in_specs=[pl.BlockSpec(memory_space=pltpu.SMEM)] + [vmem] * 6,
-        out_specs=[vmem, vmem],
-        out_shape=[
-            jax.ShapeDtypeStruct((places, quarter, width), BF16),
-            jax.ShapeDtypeStruct((quarter, width), BF16),
-        ],
-        scratch_shapes=[pltpu.VMEM((places, quarter, width), F32)],
-        interpret=interpret,
+        out_specs=[vmem] * (Y * C + 1),
+        out_shape=[jax.ShapeDtypeStruct((Z_FULL, quarter, width), BF16)] * (Y * C)
+        + [jax.ShapeDtypeStruct((quarter, width), BF16)],
+        scratch_shapes=[pltpu.VMEM((Y * C * Z_FULL, quarter, width), F32)],
         compiler_params=pltpu.CompilerParams(vmem_limit_bytes=40 * 2**20),
         name="send_back",
     )(at, *low, *high)
 
 
-def by_owner_kernel(at_ref, in_ref, *refs):
-    out_refs, total = refs[:-1], refs[-1]
+def by_owner_kernel(at_ref, *refs):
+    in_refs, out_refs, total = refs[: Y * C], refs[Y * C : -1], refs[-1]
     total[...] = jnp.zeros_like(total)
-    for slot in range(in_ref.shape[0]):
-        total[at_ref[slot]] += wide(in_ref[slot])
+    for i, in_ref in enumerate(in_refs):
+        for slot in range(Z_FULL):
+            total[at_ref[i * Z_FULL + slot]] += wide(in_ref[slot])
     blocks = out_refs[0].shape[0]
     for j, out_ref in enumerate(out_refs):
         out_ref[...] = narrow(total[j * blocks : (j + 1) * blocks])
 
 
-def by_owner(at, received, blocks, interpret=False):
-    _, quarter, width = received.shape
+def by_owner(at, received, blocks):
+    _, quarter, width = received[0].shape
     vmem = pl.BlockSpec(memory_space=pltpu.VMEM)
     return pl.pallas_call(
         by_owner_kernel,
-        in_specs=[pl.BlockSpec(memory_space=pltpu.SMEM), vmem],
+        in_specs=[pl.BlockSpec(memory_space=pltpu.SMEM)] + [vmem] * (Y * C),
         out_specs=[vmem] * Z,
         out_shape=[jax.ShapeDtypeStruct((blocks, quarter, width), BF16)] * Z,
         scratch_shapes=[pltpu.VMEM((Z * blocks + 1, quarter, width), F32)],
-        interpret=interpret,
         compiler_params=pltpu.CompilerParams(vmem_limit_bytes=40 * 2**20),
         name="by_owner",
-    )(at, received)
-
-
-def fold_core_kernel(at_ref, terms_ref, arrived_ref, *out_refs):
-    for j, out_ref in enumerate(out_refs):
-        y = (at_ref[0] + j) % Y
-        out_ref[...] = narrow(wide(terms_ref[y, at_ref[1]]) + wide(arrived_ref[y]))
-
-
-def fold_core(y, c, terms, arrived):
-    vmem = pl.BlockSpec(memory_space=pltpu.VMEM)
-    return pl.pallas_call(
-        fold_core_kernel,
-        in_specs=[pl.BlockSpec(memory_space=pltpu.SMEM), vmem, vmem],
-        out_specs=[vmem] * Y,
-        out_shape=[jax.ShapeDtypeStruct(terms.shape[2:], BF16)] * Y,
-        name="fold_core",
-    )(jnp.stack([y, c]), terms, arrived)
-
-
-def fold_y_kernel(z_ref, *refs):
-    terms, out_refs = refs[:Y], refs[Y:]
-    lines = out_refs[0].shape[0]
-    for j, out_ref in enumerate(out_refs):
-        part = pl.ds((z_ref[0] + j) % Z * lines, lines)
-        total = wide(terms[0][part])
-        for term in terms[1:]:
-            total += wide(term[part])
-        out_ref[...] = narrow(total)
-
-
-def fold_y(z, terms):
-    lines, v_dim = terms[0].shape
-    vmem = pl.BlockSpec(memory_space=pltpu.VMEM)
-    return pl.pallas_call(
-        fold_y_kernel,
-        in_specs=[pl.BlockSpec(memory_space=pltpu.SMEM)] + [vmem] * Y,
-        out_specs=[vmem] * Z,
-        out_shape=[jax.ShapeDtypeStruct((lines // Z, v_dim), BF16)] * Z,
-        name="fold_y",
-    )(z.reshape(1), *terms)
-
-
-def copies_kernel(z_ref, *refs):
-    pieces, out_ref = refs[:-1], refs[-1]
-    lines = pieces[0].shape[0]
-    for j, piece in enumerate(pieces):
-        part = pl.ds((z_ref[0] + j) % Z * lines, lines)
-        for peer in range(out_ref.shape[0]):
-            out_ref[peer, part] = piece[...]
-
-
-def copies(z, pieces):
-    lines, v_dim = pieces[0].shape
-    vmem = pl.BlockSpec(memory_space=pltpu.VMEM)
-    return pl.pallas_call(
-        copies_kernel,
-        in_specs=[pl.BlockSpec(memory_space=pltpu.SMEM)] + [vmem] * Z,
-        out_specs=vmem,
-        out_shape=jax.ShapeDtypeStruct((Y * C, Z * lines, v_dim), BF16),
-        name="copies",
-    )(z.reshape(1), *pieces)
+    )(at, *received)
 
 
 def local(query, cache, grad_out, value_weight, picked):
@@ -412,20 +362,24 @@
     places = peers * Z_FULL
     asked = place[:, None] == jnp.arange(places, dtype=jnp.int32)[None, :]
     wanted = jnp.max(jnp.where(asked, block[:, None], -1), axis=0)
-    asked_here = trade_yc(wanted.reshape(peers, 1, Z_FULL)).reshape(peers, Z_FULL)
+    asked_here = trade(wanted.reshape(peers, 1, Z_FULL), YC_GROUPS).reshape(peers, Z_FULL)
     z_off = (jnp.arange(Z_FULL, dtype=jnp.int32) - z) % Z
-    valid = (asked_here >= 0).reshape(places)
-    at_piece = (z_off[None, :] * block_count + asked_here).reshape(places)
+    distance = jnp.arange(peers, dtype=jnp.int32)
+    from_peer = (y - distance // C) % Y * C + (c ^ distance % C)
+    pick_peer = from_peer[:, None, None] == jnp.arange(peers, dtype=jnp.int32)[None, :, None]
+    asked_from = jnp.sum(jnp.where(pick_peer, asked_here[None], 0), axis=1)
+    at_owner = jnp.where(
+        asked_from >= 0, z_off[None, :] * block_count + asked_from, Z * block_count
+    ).reshape(places)
+    place_back = (owner // C % Y - y) % Y * C + (owner % C ^ c)
+    place_back = place_back * Z_FULL + owner // peers
 
     part_rows = jnp.arange(block_count * quarter, dtype=jnp.int32)
     part_rows = part_rows // quarter * BLOCK + x * quarter + part_rows % quarter
     take_part = part_rows[:, None] == jnp.arange(cache.shape[0], dtype=jnp.int32)[None, :]
     part = jnp.dot(take_part.astype(BF16), cache, preferred_element_type=F32)
     part = narrow(part).reshape(block_count, quarter, width)
-    steps = (4, -3, 3, -2, 2, -1, 1)
-    pieces = [part] + [None] * (Z - 1)
-    for step in steps:
-        pieces[-step % Z] = shift_z(part, step, lambda z: z < Z_FULL)
+    pieces = gather_z(part, Z_FULL)
     owns = []
     for j in range(block_count):
         owns.append(
@@ -439,7 +393,7 @@
             )
         )
     packed = pack(jnp.maximum(asked_here, 0).reshape(places), z, pieces)
-    fetched = trade_yc(packed.reshape(peers, Z_FULL, quarter, width))
+    fetched = trade(packed.reshape(peers, Z_FULL, quarter, width), YC_GROUPS)
     d_latent = narrow(
         jnp.einsum("qhv,hcv->qhc", grad_out, value_weight, preferred_element_type=F32)
     )
@@ -484,24 +438,22 @@
     v_dim = terms.shape[-1]
     terms = terms.reshape(Y, C, -1, v_dim)
     arrived = swap_core(lax.dynamic_index_in_dim(terms, 1 - c, 1, keepdims=False))
-    folded = list(fold_core(y, c, terms, arrived))
-    for step in (2, -1, 1):
-        folded[step % Y] = shift_y(folded[step % Y], step)
-    folded = fold_y(z, folded)
-    total = wide(folded[0])
-    for step in steps:
-        total = total + wide(shift_z(folded[step % Z], step))
-    total = narrow(total)
-    pieces = [total] * Z
-    for step in steps:
-        pieces[-step % Z] = shift_z(total, step)
-    terms = trade_yc(copies(z, pieces))
+    terms = lax.dynamic_index_in_dim(terms, c, 1, keepdims=False)
+    terms = narrow(wide(terms) + wide(arrived))
+    terms = trade(terms, Y_GROUPS)
+    terms = narrow(jnp.sum(wide(terms), axis=0))
+    terms = trade(terms.reshape(Z, -1, v_dim), Z_GROUPS)
+    terms = narrow(jnp.sum(wide(terms), axis=0))
+    terms = trade(jnp.broadcast_to(terms, (Z, *terms.shape)), Z_GROUPS).reshape(-1, v_dim)
+    terms = trade(jnp.broadcast_to(terms, (peers, *terms.shape)), YC_GROUPS)
     d_value_weight = terms.reshape(value_weight.shape)
 
-    back, own_share = send_back(
-        place, [d_low[0], low_right, low_left], [d_high[0], high_left, high_right], places
-    )
-    received = trade_yc(back.reshape(peers, Z_FULL, quarter, width))
+    *back, own_share = send_back(
+        place_back, [d_low[0], low_right, low_left], [d_high[0], high_left, high_right]
+    )
+    received = [back[0]] + [None] * (peers - 1)
+    for i in (5, 4, 3, 7, 2, 6, 1):
+        received[i] = shift_yc(back[i], i // C, i % C)
     own_back = []
     for j in range(block_count):
         own_back.append(
@@ -514,16 +466,11 @@
                 ],
             )
         )
-    by_z = by_owner(
-        jnp.where(valid, at_piece, Z * block_count),
-        received.reshape(places, quarter, width),
-        block_count,
-    )
-    d_cache = wide(by_z[0]) + wide(jnp.stack(own_back))
-    for step in steps:
-        arrived = shift_z(by_z[step % Z], step, lambda z: (z + step) % Z < Z_FULL)
-        d_cache = d_cache + wide(arrived)
-    return d_query.reshape(query.shape), d_cache, d_value_weight
+    d_query = jnp.transpose(d_query.reshape(query.shape), (1, 2, 0))
+    received, d_query = lax.optimization_barrier((received, d_query))
+    by_z = by_owner(at_owner, received, block_count)
+    d_cache = reduce_z(by_z, Z_FULL) + wide(jnp.stack(own_back))
+    return jnp.transpose(d_query, (2, 0, 1)), d_cache, d_value_weight
 
 
 def solution(mesh):

time: 372 us -> 294 us (0.79)
  the two profiles are of different devices: /device:TPU:1 before, /device:TPU:193 now
where the time goes in v1:
time: 294 us; the launch traced here: 292 us
  starting transfers between devices  118 us (40%)
  waiting for transfers between devices  98.6 us (34%)
  local copies, waits for them, and re-layouts  30.4 us (10%)
  Pallas kernels  23.8 us (8%)
  other arithmetic  12 us (4%)
  matrix products  7.61 us (3%)
    all_to_all x6, starting transfers between devices, trade(): lax.all_to_all(blocks, 'seq', split_axis=0, concat_axis=0, axis_index_gro...  35.4 us
    ppermute x14, starting transfers between devices, shift_z(): return lax.ppermute(array, 'seq', pairs)  28.3 us
    ppermute x7, waiting for transfers between devices, shift_yc(): return lax.ppermute(array, 'seq', pairs)  28.3 us
    all_to_all x6, waiting for transfers between devices, trade(): lax.all_to_all(blocks, 'seq', split_axis=0, concat_axis=0, axis_index_gro...  27.1 us
    ppermute x12, waiting for transfers between devices, shift_x(): return lax.ppermute(array, 'head', [(x, (x + step) % X) for x in range(X)])  21.2 us
    ppermute x4, starting transfers between devices, local(): lax.ppermute(own_share, 'seq', [((o - FIRST_OWN_OWNER) * block_count + j,...  18.1 us
    unnamed x62, local copies, waits for them, and re-layouts  16.6 us
    pallas_call x1, Pallas kernels, attend(): pl.pallas_call(attend_kernel, grid_spec=pltpu.PrefetchScalarGridSpec(num_...  14.6 us
  transfers between devices with their start and end apart: 48, of which 18 were waited for; matrix products, arithmetic and copies ran while one was open for 10% of the time, Pallas kernels for 1%

profile of v1, /device:TPU:193, one launch (start us, length us, event | category | flops | bytes accessed | tf_op | source)
XLA Modules:
  0.0 291.9 jit_solution(4321944101737451348)
XLA Ops:
  5.1 4.1 %collective-permute-done.3.refs_7_ = bf16[4,32,576]{2,1,0:T(8,128)(2,1)S(1)} collective-permute-done((bf16[4,32,576]{2,1,0:T(8,128)(2,1)S(1)}, bf16[4,32,576]{2,1,0:T(8,128)(2,1)S(1)}, u32[]{:S(2)}, u32[]{:S(2)}) %collective-permute-start.3) | collective-permute-done | bytes 147488 | tf_op jit(solution)/shard_map/ppermute | solution.py:39
  24.4 8.0 %all-to-all-start = ((s32[8,1,6]{2,1,0:T(1,128)}), s32[8,1,6]{2,1,0:T(1,128)S(1)}, u32[]{:S(2)}, u32[]{:S(2)}) async-start(s32[8,1,6]{2,1,0:T(1,128)} %bitcast.1), calls=%async_computation | async-start | bytes 8192 | tf_op jit(solution)/shard_map/all_to_all | solution.py:82
  32.4 4.6 %all-to-all-done = s32[8,1,6]{2,1,0:T(1,128)S(1)} async-done(((s32[8,1,6]{2,1,0:T(1,128)}), s32[8,1,6]{2,1,0:T(1,128)S(1)}, u32[]{:S(2)}, u32[]{:S(2)}) %all-to-all-start) | async-done | bytes 224 | tf_op jit(solution)/shard_map/all_to_all | solution.py:82
  38.3 3.0 %pack.1 = bf16[48,32,576]{2,1,0:T(8,128)(2,1)} custom-call(s32[48]{0:T(128)} %max.8.block_ref, s32[1]{0:T(128)} %bitcast.2.z_ref, bf16[4,32,576]{2,1,0:T(8,128)(2,1)} %bitcast.40, bf16[4,32,576]{2,1,0:T(8,128)(2,1)} %copy-done.19, bf16[4,32,576]{2,1,0:T(8,128)(2,1)} %copy-done.21, bf16[4,32,576]{2,1,0:T(8,128)(2,1)} %copy-done.23, ...), custom_call_target="tpu_custom_call" | custom-call | tf_op jit(solution)/shard_map/pack/pallas_call | solution.py:115
  41.3 5.0 %all-to-all-start.1 = ((bf16[8,6,32,576]{3,2,1,0:T(8,128)(2,1)}), bf16[8,6,32,576]{3,2,1,0:T(8,128)(2,1)}, u32[]{:S(2)}, u32[]{:S(2)}) async-start(bf16[8,6,32,576]{3,2,1,0:T(8,128)(2,1)} %bitcast.35), calls=%async_computation.1 | async-start | bytes 3932160 | tf_op jit(solution)/shard_map/all_to_all | solution.py:82
  46.4 5.4 %collective-permute-start.10 = (bf16[32,576]{1,0:T(8,128)(2,1)S(1)}, bf16[32,576]{1,0:T(8,128)(2,1)S(1)}, u32[]{:S(2)}, u32[]{:S(2)}) collective-permute-start(bf16[32,576]{1,0:T(8,128)(2,1)S(1)} %get-tuple-element.90), channel_id=1, source_target_pairs={{192,12},{196,28},{200,44},{204,60},{208,76},{212,92},{216,108},{2... | collective-permute-start | bytes 110600 | tf_op jit(solution)/shard_map/ppermute | solution.py:386
  58.4 4.1 %copy.34 = bf16[128,16,512]{2,1,0:T(8,128)(2,1)} copy(bf16[128,16,512]{2,0,1:T(8,128)(2,1)} %convert_bitcast_fusion) | data formatting | bytes 4194304 | tf_op jit(solution)/shard_map/convert_element_type | solution.py:93
  62.5 4.9 %copy.35 = bf16[128,16,576]{2,1,0:T(8,128)(2,1)} copy(bf16[128,16,576]{0,2,1:T(8,128)(2,1)} %param.5) | data formatting | bytes 4718592 | tf_op args[0]
  67.4 5.7 %all-to-all-done.1 = bf16[8,6,32,576]{3,2,1,0:T(8,128)(2,1)} async-done(((bf16[8,6,32,576]{3,2,1,0:T(8,128)(2,1)}), bf16[8,6,32,576]{3,2,1,0:T(8,128)(2,1)}, u32[]{:S(2)}, u32[]{:S(2)}) %all-to-all-start.1) | async-done | bytes 1769504 | tf_op jit(solution)/shard_map/all_to_all | solution.py:82
  80.1 4.9 %collective-permute-done.11.refs_1_.refs_5_ = bf16[7,32,576]{2,1,0:T(8,128)(2,1)S(1)} collective-permute-done((bf16[7,32,576]{2,1,0:T(8,128)(2,1)}, bf16[7,32,576]{2,1,0:T(8,128)(2,1)S(1)}, u32[]{:S(2)}, u32[]{:S(2)}) %collective-permute-start.11) | collective-permute-done | bytes 258080 | tf_op jit(solution)/shard_map/ppermute | solution.py:78
  87.8 10.4 %collective-permute-done.14.refs_9_ = bf16[6,32,576]{2,1,0:T(8,128)(2,1)} collective-permute-done((bf16[6,32,576]{2,1,0:T(8,128)(2,1)}, bf16[6,32,576]{2,1,0:T(8,128)(2,1)}, u32[]{:S(2)}, u32[]{:S(2)}) %collective-permute-start.14) | collective-permute-done | bytes 221216 | tf_op jit(solution)/shard_map/ppermute | solution.py:78
  99.1 14.6 %attend.1 = (bf16[2048,576]{1,0:T(8,128)(2,1)}, bf16[2048,512]{1,0:T(8,128)(2,1)}, bf16[7,32,576]{2,1,0:T(8,128)(2,1)}, bf16[7,32,576]{2,1,0:T(8,128)(2,1)}, bf1...) custom-call(s32[1]{0:T(128)} %bitcast.x_ref, ...), custom_call_target="tpu_custom_call" | custom-call | tf_op jit(solution)/shard_map/attend/pallas_call | solution.py:251
  113.6 4.0 %fusion.3 = bf16[16,512,128]{2,1,0:T(8,128)(2,1)S(1)} fusion(bf16[128,16,512]{2,1,0:T(8,128)(2,1)} %bitcast.37, bf16[128,16,128]{2,1,0:T(8,128)(2,1)S(1)} %copy-done.11), kind=kOutput, calls=%fused_computation.5 | convolution fusion | flops 269484032 | bytes 4718592 | tf_op jit(solution)/shard_map/qhc,qhv->hcv/dot_general | solution.py:431
  119.1 2.8 collective-permute-start.41
  124.3 2.8 fusion
  127.0 4.4 %all-to-all-start.2 = ((bf16[4,1024,128]{2,1,0:T(8,128)(2,1)}), bf16[4,1024,128]{2,1,0:T(8,128)(2,1)}, u32[]{:S(2)}, u32[]{:S(2)}) async-start(bf16[4,1024,128]{2,1,0:T(8,128)(2,1)} %fusion), calls=%async_computation.2 | async-start | bytes 2097152 | tf_op jit(solution)/shard_map/all_to_all | solution.py:82
  131.7 14.6 %all-to-all-done.2 = bf16[4,1024,128]{2,1,0:T(8,128)(2,1)} async-done(((bf16[4,1024,128]{2,1,0:T(8,128)(2,1)}), bf16[4,1024,128]{2,1,0:T(8,128)(2,1)}, u32[]{:S(2)}, u32[]{:S(2)}) %all-to-all-start.2) | async-done | bytes 1048608 | tf_op jit(solution)/shard_map/all_to_all | solution.py:82
  148.5 7.6 %all-to-all-start.3 = ((bf16[8,128,128]{2,1,0:T(8,128)(2,1)}), bf16[8,128,128]{2,1,0:T(8,128)(2,1)}, u32[]{:S(2)}, u32[]{:S(2)}) async-start(bf16[8,128,128]{2,1,0:T(8,128)(2,1)} %bitcast.22), calls=%async_computation.3 | async-start | bytes 524288 | tf_op jit(solution)/shard_map/all_to_all | solution.py:82
  165.9 6.1 %all-to-all-start.4 = ((bf16[8,128,128]{2,1,0:T(8,128)(2,1)}), bf16[8,128,128]{2,1,0:T(8,128)(2,1)}, u32[]{:S(2)}, u32[]{:S(2)}) async-start(bf16[8,128,128]{2,1,0:T(8,128)(2,1)} %broadcast_in_dim.77), calls=%async_computation.4 | async-start | bytes 524288 | tf_op jit(solution)/shard_map/all_to_all | solution.py:82
  174.2 5.9 %collective-permute-done.22.refs_5_ = bf16[6,32,576]{2,1,0:T(8,128)(2,1)S(1)} collective-permute-done((bf16[6,32,576]{2,1,0:T(8,128)(2,1)S(1)}, bf16[6,32,576]{2,1,0:T(8,128)(2,1)S(1)}, u32[]{:S(2)}, u32[]{:S(2)}) %collective-permute-start.22) | collective-permute-done | bytes 221216 | tf_op jit(solution)/shard_map/ppermute | solution.py:78
  186.4 3.7 %collective-permute-start.23 = (bf16[6,32,576]{2,1,0:T(8,128)(2,1)}, bf16[6,32,576]{2,1,0:T(8,128)(2,1)S(1)}, u32[]{:S(2)}, u32[]{:S(2)}) collective-permute-start(bf16[6,32,576]{2,1,0:T(8,128)(2,1)} %get-tuple-element.58), channel_id=1, source_target_pairs={{0,4},{4,0},{8,12},{12,8},{16,20},{20,16},{24,28},{28,24},{32,36},... | collective-permute-start | bytes 663560 | tf_op jit(solution)/shard_map/ppermute | solution.py:70
  197.8 4.3 %all-to-all-start.5 = ((bf16[8,1024,128]{2,1,0:T(8,128)(2,1)}), bf16[8,1024,128]{2,1,0:T(8,128)(2,1)}, u32[]{:S(2)}, u32[]{:S(2)}) async-start(bf16[8,1024,128]{2,1,0:T(8,128)(2,1)} %broadcast_in_dim.78), calls=%async_computation.5 | async-start | bytes 4194304 | tf_op jit(solution)/shard_map/all_to_all | solution.py:82
  206.0 4.7 %copy.36 = bf16[128,16,576]{0,2,1:T(8,128)(2,1)} copy(bf16[128,16,576]{2,1,0:T(8,128)(2,1)} %bitcast.36) | data formatting | bytes 4718592 | tf_op jit(solution)/shard_map/reshape | solution.py:469
  210.7 6.0 %collective-permute-done.27.refs_5_ = bf16[6,32,576]{2,1,0:T(8,128)(2,1)} collective-permute-done((bf16[6,32,576]{2,1,0:T(8,128)(2,1)}, bf16[6,32,576]{2,1,0:T(8,128)(2,1)}, u32[]{:S(2)}, u32[]{:S(2)}) %collective-permute-start.27) | collective-permute-done | bytes 221216 | tf_op jit(solution)/shard_map/ppermute | solution.py:70
  216.7 16.7 %collective-permute-done.28.refs_6_ = bf16[6,32,576]{2,1,0:T(8,128)(2,1)} collective-permute-done((bf16[6,32,576]{2,1,0:T(8,128)(2,1)}, bf16[6,32,576]{2,1,0:T(8,128)(2,1)}, u32[]{:S(2)}, u32[]{:S(2)}) %collective-permute-start.28) | collective-permute-done | bytes 221216 | tf_op jit(solution)/shard_map/ppermute | solution.py:70
  233.3 5.7 %collective-permute-done.29.refs_7_ = bf16[6,32,576]{2,1,0:T(8,128)(2,1)} collective-permute-done((bf16[6,32,576]{2,1,0:T(8,128)(2,1)}, bf16[6,32,576]{2,1,0:T(8,128)(2,1)}, u32[]{:S(2)}, u32[]{:S(2)}) %collective-permute-start.29) | collective-permute-done | bytes 221216 | tf_op jit(solution)/shard_map/ppermute | solution.py:70
  243.1 3.1 %collective-permute-start.34 = (bf16[4,32,576]{2,1,0:T(8,128)(2,1)S(1)}, bf16[4,32,576]{2,1,0:T(8,128)(2,1)S(1)}, u32[]{:S(2)}, u32[]{:S(2)}) collective-permute-start(bf16[4,32,576]{2,1,0:T(8,128)(2,1)S(1)} %get-tuple-element.80), channel_id=1, source_target_pairs={{0,224},{4,228},{8,232},{12,236},{16,240},{20,244},{24,248},{28,25... | collective-permute-start | bytes 442376 | tf_op jit(solution)/shard_map/ppermute | solution.py:39
  250.9 3.1 %collective-permute-start.35 = (bf16[4,32,576]{2,1,0:T(8,128)(2,1)S(1)}, bf16[4,32,576]{2,1,0:T(8,128)(2,1)S(1)}, u32[]{:S(2)}, u32[]{:S(2)}) collective-permute-start(bf16[4,32,576]{2,1,0:T(8,128)(2,1)S(1)} %add_convert_fusion.3), channel_id=1, source_target_pairs={{64,32},{68,36},{72,40},{76,44},{80,48},{84,52},{88,56},{92,60},{9... | collective-permute-start | bytes 442376 | tf_op jit(solution)/shard_map/ppermute | solution.py:39
  257.7 2.8 collective-permute-start.36
  263.9 14.2 %collective-permute-start.38 = (bf16[32,576]{1,0:T(8,128)(2,1)S(1)}, bf16[32,576]{1,0:T(8,128)(2,1)S(1)}, u32[]{:S(2)}, u32[]{:S(2)}) collective-permute-start(bf16[32,576]{1,0:T(8,128)(2,1)S(1)} %get-tuple-element.83), channel_id=1, source_target_pairs={{4,192},{20,196},{36,200},{52,204},{68,208},{84,212},{100,216},{11... | collective-permute-start | bytes 110600 | tf_op jit(solution)/shard_map/ppermute | solution.py:460
  279.4 8.5 %collective-permute-done.37 = bf16[32,576]{1,0:T(8,128)(2,1)S(1)} collective-permute-done((bf16[32,576]{1,0:T(8,128)(2,1)S(1)}, bf16[32,576]{1,0:T(8,128)(2,1)S(1)}, u32[]{:S(2)}, u32[]{:S(2)}) %collective-permute-start.37) | collective-permute-done | bytes 36896 | tf_op jit(solution)/shard_map/ppermute | solution.py:460
  288.8 3.1 %copy.51 = bf16[16,512,128]{2,1,0:T(8,128)(2,1)} copy(bf16[16,512,128]{2,1,0:T(8,128)(2,1)} %bitcast.24) | data formatting | bytes 4194304
  (172 shorter events, 92.1 us)
Async XLA Ops:
  18.2 19.4 %collective-permute-start.2 = (bf16[4,32,576]{2,1,0:T(8,128)(2,1)S(1)}, bf16[4,32,576]{2,1,0:T(8,128)(2,1)S(1)}, u32[]{:S(2)}, u32[]{:S(2)}) collective-permute-start(bf16[4,32,576]{2,1,0:T(8,128)(2,1)S(1)} %collective-permute-done.1.refs_2_), channel_id=1, source_target_pairs={{0,224},{4,228},{8,232},{12,236},{16,240},{20,244},{24,248},{28,25... | collective-permute-start | bytes 442376 | tf_op jit(solution)/shard_map/ppermute | solution.py:39
  21.4 16.2 %collective-permute-start.6 = (bf16[4,32,576]{2,1,0:T(8,128)(2,1)S(1)}, bf16[4,32,576]{2,1,0:T(8,128)(2,1)S(1)}, u32[]{:S(2)}, u32[]{:S(2)}) collective-permute-start(bf16[4,32,576]{2,1,0:T(8,128)(2,1)S(1)} %collective-permute-done.5.refs_5_), channel_id=1, source_target_pairs={{0,32},{4,36},{8,40},{12,44},{16,48},{20,52},{24,56},{28,60},{96,1... | collective-permute-start | bytes 442376 | tf_op jit(solution)/shard_map/ppermute | solution.py:39
  24.4 12.6 %all-to-all-start = ((s32[8,1,6]{2,1,0:T(1,128)}), s32[8,1,6]{2,1,0:T(1,128)S(1)}, u32[]{:S(2)}, u32[]{:S(2)}) async-start(s32[8,1,6]{2,1,0:T(1,128)} %bitcast.1), calls=%async_computation | async-start | bytes 8192 | tf_op jit(solution)/shard_map/all_to_all | solution.py:82
  41.3 31.7 %all-to-all-start.1 = ((bf16[8,6,32,576]{3,2,1,0:T(8,128)(2,1)}), bf16[8,6,32,576]{3,2,1,0:T(8,128)(2,1)}, u32[]{:S(2)}, u32[]{:S(2)}) async-start(bf16[8,6,32,576]{3,2,1,0:T(8,128)(2,1)} %bitcast.35), calls=%async_computation.1 | async-start | bytes 3932160 | tf_op jit(solution)/shard_map/all_to_all | solution.py:82
  46.4 26.7 %collective-permute-start.10 = (bf16[32,576]{1,0:T(8,128)(2,1)S(1)}, bf16[32,576]{1,0:T(8,128)(2,1)S(1)}, u32[]{:S(2)}, u32[]{:S(2)}) collective-permute-start(bf16[32,576]{1,0:T(8,128)(2,1)S(1)} %get-tuple-element.90), channel_id=1, source_target_pairs={{192,12},{196,28},{200,44},{204,60},{208,76},{212,92},{216,108},{2... | collective-permute-start | bytes 110600 | tf_op jit(solution)/shard_map/ppermute | solution.py:386
  51.8 21.2 %collective-permute-start.9 = (bf16[32,576]{1,0:T(8,128)(2,1)S(1)}, bf16[32,576]{1,0:T(8,128)(2,1)S(1)}, u32[]{:S(2)}, u32[]{:S(2)}) collective-permute-start(bf16[32,576]{1,0:T(8,128)(2,1)S(1)} %get-tuple-element.91), channel_id=1, source_target_pairs={{192,8},{196,24},{200,40},{204,56},{208,72},{212,88},{216,104},{22... | collective-permute-start | bytes 110600 | tf_op jit(solution)/shard_map/ppermute | solution.py:386
  53.1 20.0 %collective-permute-start.8 = (bf16[32,576]{1,0:T(8,128)(2,1)S(1)}, bf16[32,576]{1,0:T(8,128)(2,1)S(1)}, u32[]{:S(2)}, u32[]{:S(2)}) collective-permute-start(bf16[32,576]{1,0:T(8,128)(2,1)S(1)} %get-tuple-element.92), channel_id=1, source_target_pairs={{192,4},{196,20},{200,36},{204,52},{208,68},{212,84},{216,100},{22... | collective-permute-start | bytes 110600 | tf_op jit(solution)/shard_map/ppermute | solution.py:386
  55.1 18.1 %collective-permute-start.7 = (bf16[32,576]{1,0:T(8,128)(2,1)S(1)}, bf16[32,576]{1,0:T(8,128)(2,1)S(1)}, u32[]{:S(2)}, u32[]{:S(2)}) collective-permute-start(bf16[32,576]{1,0:T(8,128)(2,1)S(1)} %get-tuple-element.93), channel_id=1, source_target_pairs={{192,0},{196,16},{200,32},{204,48},{208,64},{212,80},{216,96},{220... | collective-permute-start | bytes 110600 | tf_op jit(solution)/shard_map/ppermute | solution.py:386
  78.9 19.3 %collective-permute-start.13 = (bf16[7,32,576]{2,1,0:T(8,128)(2,1)}, bf16[7,32,576]{2,1,0:T(8,128)(2,1)S(1)}, u32[]{:S(2)}, u32[]{:S(2)}) collective-permute-start(bf16[7,32,576]{2,1,0:T(8,128)(2,1)} %get-tuple-element.47.refs_0_.refs_4_), channel_id=1, source_target_pairs={{0,3},{1,0},{2,1},{3,2},{4,7},{5,4},{6,5},{7,6},{8,11},{9,8},{10,9... | collective-permute-start | bytes 774152 | tf_op jit(solution)/shard_map/ppermute | solution.py:78
  85.1 13.2 %collective-permute-start.12 = (bf16[7,32,576]{2,1,0:T(8,128)(2,1)S(1)}, bf16[7,32,576]{2,1,0:T(8,128)(2,1)S(1)}, u32[]{:S(2)}, u32[]{:S(2)}) collective-permute-start(bf16[7,32,576]{2,1,0:T(8,128)(2,1)S(1)} %collective-permute-done.11.refs_1_.refs_5_), channel_id=1, source_target_pairs={{0,1},{1,2},{2,3},{3,0},{4,5},{5,6},{6,7},{7,4},{8,9},{9,10},{10,1... | collective-permute-start | bytes 774152 | tf_op jit(solution)/shard_map/ppermute | solution.py:78
  85.2 13.0 %collective-permute-start.14 = (bf16[6,32,576]{2,1,0:T(8,128)(2,1)}, bf16[6,32,576]{2,1,0:T(8,128)(2,1)}, u32[]{:S(2)}, u32[]{:S(2)}) collective-permute-start(bf16[6,32,576]{2,1,0:T(8,128)(2,1)} %get-tuple-element.48.refs_8_), channel_id=1, source_target_pairs={{0,1},{1,2},{2,3},{3,0},{4,5},{5,6},{6,7},{7,4},{8,9},{9,10},{10,1... | collective-permute-start | bytes 663560 | tf_op jit(solution)/shard_map/ppermute | solution.py:78
  127.0 19.3 %all-to-all-start.2 = ((bf16[4,1024,128]{2,1,0:T(8,128)(2,1)}), bf16[4,1024,128]{2,1,0:T(8,128)(2,1)}, u32[]{:S(2)}, u32[]{:S(2)}) async-start(bf16[4,1024,128]{2,1,0:T(8,128)(2,1)} %fusion), calls=%async_computation.2 | async-start | bytes 2097152 | tf_op jit(solution)/shard_map/all_to_all | solution.py:82
  131.5 26.1 %collective-permute-start.18 = (bf16[7,32,576]{2,1,0:T(8,128)(2,1)}, bf16[7,32,576]{2,1,0:T(8,128)(2,1)}, u32[]{:S(2)}, u32[]{:S(2)}) collective-permute-start(bf16[7,32,576]{2,1,0:T(8,128)(2,1)} %get-tuple-element.51), channel_id=1, source_target_pairs={{0,3},{1,0},{2,1},{3,2},{4,7},{5,4},{6,5},{7,6},{8,11},{9,8},{10,9... | collective-permute-start | bytes 774152 | tf_op jit(solution)/shard_map/ppermute | solution.py:78
  148.5 15.8 %all-to-all-start.3 = ((bf16[8,128,128]{2,1,0:T(8,128)(2,1)}), bf16[8,128,128]{2,1,0:T(8,128)(2,1)}, u32[]{:S(2)}, u32[]{:S(2)}) async-start(bf16[8,128,128]{2,1,0:T(8,128)(2,1)} %bitcast.22), calls=%async_computation.3 | async-start | bytes 524288 | tf_op jit(solution)/shard_map/all_to_all | solution.py:82
  156.1 17.4 %collective-permute-start.20 = (bf16[6,32,576]{2,1,0:T(8,128)(2,1)}, bf16[6,32,576]{2,1,0:T(8,128)(2,1)S(1)}, u32[]{:S(2)}, u32[]{:S(2)}) collective-permute-start(bf16[6,32,576]{2,1,0:T(8,128)(2,1)} %get-tuple-element.54), channel_id=1, source_target_pairs={{0,3},{1,0},{2,1},{3,2},{4,7},{5,4},{6,5},{7,6},{8,11},{9,8},{10,9... | collective-permute-start | bytes 663560 | tf_op jit(solution)/shard_map/ppermute | solution.py:78
  156.3 15.7 %collective-permute-start.21 = (bf16[6,32,576]{2,1,0:T(8,128)(2,1)}, bf16[6,32,576]{2,1,0:T(8,128)(2,1)}, u32[]{:S(2)}, u32[]{:S(2)}) collective-permute-start(bf16[6,32,576]{2,1,0:T(8,128)(2,1)} %get-tuple-element.55), channel_id=1, source_target_pairs={{0,1},{1,2},{2,3},{3,0},{4,5},{5,6},{6,7},{7,4},{8,9},{9,10},{10,1... | collective-permute-start | bytes 663560 | tf_op jit(solution)/shard_map/ppermute | solution.py:78
  157.6 16.6 %collective-permute-start.17 = (bf16[7,32,576]{2,1,0:T(8,128)(2,1)}, bf16[7,32,576]{2,1,0:T(8,128)(2,1)S(1)}, u32[]{:S(2)}, u32[]{:S(2)}) collective-permute-start(bf16[7,32,576]{2,1,0:T(8,128)(2,1)} %get-tuple-element.50), channel_id=1, source_target_pairs={{0,1},{1,2},{2,3},{3,0},{4,5},{5,6},{6,7},{7,4},{8,9},{9,10},{10,1... | collective-permute-start | bytes 774152 | tf_op jit(solution)/shard_map/ppermute | solution.py:78
  159.3 20.8 %collective-permute-start.19 = (bf16[7,32,576]{2,1,0:T(8,128)(2,1)}, bf16[7,32,576]{2,1,0:T(8,128)(2,1)S(1)}, u32[]{:S(2)}, u32[]{:S(2)}) collective-permute-start(bf16[7,32,576]{2,1,0:T(8,128)(2,1)} %add_convert_fusion), channel_id=1, source_target_pairs={{0,3},{1,0},{2,1},{3,2},{4,7},{5,4},{6,5},{7,6},{8,11},{9,8},{10,9... | collective-permute-start | bytes 774152 | tf_op jit(solution)/shard_map/ppermute | solution.py:78
  165.9 29.4 %all-to-all-start.4 = ((bf16[8,128,128]{2,1,0:T(8,128)(2,1)}), bf16[8,128,128]{2,1,0:T(8,128)(2,1)}, u32[]{:S(2)}, u32[]{:S(2)}) async-start(bf16[8,128,128]{2,1,0:T(8,128)(2,1)} %broadcast_in_dim.77), calls=%async_computation.4 | async-start | bytes 524288 | tf_op jit(solution)/shard_map/all_to_all | solution.py:82
  186.4 15.8 %collective-permute-start.23 = (bf16[6,32,576]{2,1,0:T(8,128)(2,1)}, bf16[6,32,576]{2,1,0:T(8,128)(2,1)S(1)}, u32[]{:S(2)}, u32[]{:S(2)}) collective-permute-start(bf16[6,32,576]{2,1,0:T(8,128)(2,1)} %get-tuple-element.58), channel_id=1, source_target_pairs={{0,4},{4,0},{8,12},{12,8},{16,20},{20,16},{24,28},{28,24},{32,36},... | collective-permute-start | bytes 663560 | tf_op jit(solution)/shard_map/ppermute | solution.py:70
  190.0 14.6 %collective-permute-start.24 = (bf16[6,32,576]{2,1,0:T(8,128)(2,1)}, bf16[6,32,576]{2,1,0:T(8,128)(2,1)S(1)}, u32[]{:S(2)}, u32[]{:S(2)}) collective-permute-start(bf16[6,32,576]{2,1,0:T(8,128)(2,1)} %get-tuple-element.59), channel_id=1, source_target_pairs={{0,8},{4,12},{8,16},{12,20},{16,24},{20,28},{24,0},{28,4},{32,40},... | collective-permute-start | bytes 663560 | tf_op jit(solution)/shard_map/ppermute | solution.py:70
  190.6 20.1 %collective-permute-start.25 = (bf16[6,32,576]{2,1,0:T(8,128)(2,1)}, bf16[6,32,576]{2,1,0:T(8,128)(2,1)S(1)}, u32[]{:S(2)}, u32[]{:S(2)}) collective-permute-start(bf16[6,32,576]{2,1,0:T(8,128)(2,1)} %copy-done.9), channel_id=1, source_target_pairs={{0,12},{4,8},{8,20},{12,16},{16,28},{20,24},{24,4},{28,0},{32,44},... | collective-permute-start | bytes 663560 | tf_op jit(solution)/shard_map/ppermute | solution.py:70
  191.9 18.8 %collective-permute-start.26 = (bf16[6,32,576]{2,1,0:T(8,128)(2,1)}, bf16[6,32,576]{2,1,0:T(8,128)(2,1)S(1)}, u32[]{:S(2)}, u32[]{:S(2)}) collective-permute-start(bf16[6,32,576]{2,1,0:T(8,128)(2,1)} %copy-done.8), channel_id=1, source_target_pairs={{0,16},{4,20},{8,24},{12,28},{16,0},{20,4},{24,8},{28,12},{32,48},... | collective-permute-start | bytes 663560 | tf_op jit(solution)/shard_map/ppermute | solution.py:70
  194.4 22.3 %collective-permute-start.27 = (bf16[6,32,576]{2,1,0:T(8,128)(2,1)}, bf16[6,32,576]{2,1,0:T(8,128)(2,1)}, u32[]{:S(2)}, u32[]{:S(2)}) collective-permute-start(bf16[6,32,576]{2,1,0:T(8,128)(2,1)} %copy-done.7), channel_id=1, source_target_pairs={{0,20},{4,16},{8,28},{12,24},{16,4},{20,0},{24,12},{28,8},{32,52},... | collective-permute-start | bytes 663560 | tf_op jit(solution)/shard_map/ppermute | solution.py:70
  197.8 90.9 %all-to-all-start.5 = ((bf16[8,1024,128]{2,1,0:T(8,128)(2,1)}), bf16[8,1024,128]{2,1,0:T(8,128)(2,1)}, u32[]{:S(2)}, u32[]{:S(2)}) async-start(bf16[8,1024,128]{2,1,0:T(8,128)(2,1)} %broadcast_in_dim.78), calls=%async_computation.5 | async-start | bytes 4194304 | tf_op jit(solution)/shard_map/all_to_all | solution.py:82
  202.2 31.2 %collective-permute-start.28 = (bf16[6,32,576]{2,1,0:T(8,128)(2,1)}, bf16[6,32,576]{2,1,0:T(8,128)(2,1)}, u32[]{:S(2)}, u32[]{:S(2)}) collective-permute-start(bf16[6,32,576]{2,1,0:T(8,128)(2,1)} %copy-done.6), channel_id=1, source_target_pairs={{0,24},{4,28},{8,0},{12,4},{16,8},{20,12},{24,16},{28,20},{32,56},... | collective-permute-start | bytes 663560 | tf_op jit(solution)/shard_map/ppermute | solution.py:70
  204.7 34.3 %collective-permute-start.29 = (bf16[6,32,576]{2,1,0:T(8,128)(2,1)}, bf16[6,32,576]{2,1,0:T(8,128)(2,1)}, u32[]{:S(2)}, u32[]{:S(2)}) collective-permute-start(bf16[6,32,576]{2,1,0:T(8,128)(2,1)} %copy-done.5), channel_id=1, source_target_pairs={{0,28},{4,24},{8,4},{12,0},{16,12},{20,8},{24,20},{28,16},{32,60},... | collective-permute-start | bytes 663560 | tf_op jit(solution)/shard_map/ppermute | solution.py:70
  257.7 30.2 %collective-permute-start.36 = (bf16[4,32,576]{2,1,0:T(8,128)(2,1)S(1)}, bf16[4,32,576]{2,1,0:T(8,128)(2,1)S(1)}, u32[]{:S(2)}, u32[]{:S(2)}) collective-permute-start(bf16[4,32,576]{2,1,0:T(8,128)(2,1)S(1)} %add_convert_fusion.2), channel_id=1, source_target_pairs={{32,0},{36,4},{40,8},{44,12},{48,16},{52,20},{56,24},{60,28},{64,3... | collective-permute-start | bytes 442376 | tf_op jit(solution)/shard_map/ppermute | solution.py:39
  260.6 27.3 %collective-permute-start.33 = (bf16[4,32,576]{2,1,0:T(8,128)(2,1)S(1)}, bf16[4,32,576]{2,1,0:T(8,128)(2,1)S(1)}, u32[]{:S(2)}, u32[]{:S(2)}) collective-permute-start(bf16[4,32,576]{2,1,0:T(8,128)(2,1)S(1)} %add_convert_fusion.4), channel_id=1, source_target_pairs={{0,32},{4,36},{8,40},{12,44},{16,48},{20,52},{24,56},{28,60},{32,6... | collective-permute-start | bytes 442376 | tf_op jit(solution)/shard_map/ppermute | solution.py:39
  261.3 16.8 %collective-permute-start.40 = (bf16[32,576]{1,0:T(8,128)(2,1)S(1)}, bf16[32,576]{1,0:T(8,128)(2,1)S(1)}, u32[]{:S(2)}, u32[]{:S(2)}) collective-permute-start(bf16[32,576]{1,0:T(8,128)(2,1)S(1)} %get-tuple-element.83), channel_id=1, source_target_pairs={{12,192},{28,196},{44,200},{60,204},{76,208},{92,212},{108,216},{1... | collective-permute-start | bytes 110600 | tf_op jit(solution)/shard_map/ppermute | solution.py:460
  262.6 16.8 %collective-permute-start.39 = (bf16[32,576]{1,0:T(8,128)(2,1)S(1)}, bf16[32,576]{1,0:T(8,128)(2,1)S(1)}, u32[]{:S(2)}, u32[]{:S(2)}) collective-permute-start(bf16[32,576]{1,0:T(8,128)(2,1)S(1)} %get-tuple-element.83), channel_id=1, source_target_pairs={{8,192},{24,196},{40,200},{56,204},{72,208},{88,212},{104,216},{12... | collective-permute-start | bytes 110600 | tf_op jit(solution)/shard_map/ppermute | solution.py:460
  263.9 15.5 %collective-permute-start.38 = (bf16[32,576]{1,0:T(8,128)(2,1)S(1)}, bf16[32,576]{1,0:T(8,128)(2,1)S(1)}, u32[]{:S(2)}, u32[]{:S(2)}) collective-permute-start(bf16[32,576]{1,0:T(8,128)(2,1)S(1)} %get-tuple-element.83), channel_id=1, source_target_pairs={{4,192},{20,196},{36,200},{52,204},{68,208},{84,212},{100,216},{11... | collective-permute-start | bytes 110600 | tf_op jit(solution)/shard_map/ppermute | solution.py:460
  (46 other events, 519.0 us)

commit v2 on v1

--- a/solution.py
+++ b/solution.py
@@ -40,24 +40,31 @@
 
 
 def gather_z(own, limit):
-    right, left = [own], [own]
-    for hop in range(4):
-        right.append(shift_z(right[-1], 1, lambda z: (z - hop) % Z < limit))
-        if hop < 3:
-            left.append(shift_z(left[-1], -1, lambda z: (z + hop) % Z < limit))
-    return [own, left[1], left[2], left[3], right[4], right[3], right[2], right[1]]
-
-
-def reduce_z(terms, limit):
-    right, left = terms[4], terms[5]
-    for hop in range(4):
-        right = shift_z(right, 1, lambda z: (z + 4 - hop) % Z < limit)
-        if hop < 3:
-            right = narrow(wide(right) + wide(terms[3 - hop]))
-            left = shift_z(left, -1, lambda z: (z - 3 + hop) % Z < limit)
-        if hop < 2:
-            left = narrow(wide(left) + wide(terms[6 + hop]))
-    return wide(terms[0]) + wide(right) + wide(left)
+    right_2 = shift_z(own, 2, lambda z: z < limit)
+    left_2 = shift_z(own, -2, lambda z: z < limit)
+    right_1 = shift_z(own, 1, lambda z: z < limit)
+    left_1 = shift_z(own, -1, lambda z: z < limit)
+    right_4 = shift_z(right_2, 2, lambda z: (z - 2) % Z < limit)
+    left_3 = shift_z(left_2, -1, lambda z: (z + 2) % Z < limit)
+    right_3 = shift_z(right_2, 1, lambda z: (z - 2) % Z < limit)
+    return [own, left_1, left_2, left_3, right_4, right_3, right_2, right_1]
+
+
+def reduce_z(terms, limit, beside):
+    right_4 = shift_z(terms[4], 2, lambda z: (z + 4) % Z < limit)
+    right_3 = shift_z(terms[3], 1, lambda z: (z + 3) % Z < limit)
+    left_3 = shift_z(terms[5], -1, lambda z: (z - 3) % Z < limit)
+    right_1 = shift_z(terms[1], 1, lambda z: (z + 1) % Z < limit)
+    left_1 = shift_z(terms[7], -1, lambda z: (z - 1) % Z < limit)
+    right_4, right_3, left_3, beside = lax.optimization_barrier((right_4, right_3, left_3, beside))
+    right_2 = narrow(wide(terms[2]) + wide(right_3) + wide(right_4))
+    left_2 = narrow(wide(terms[6]) + wide(left_3))
+    right_2 = shift_z(right_2, 2, lambda z: (z + 2) % Z < limit)
+    left_2 = shift_z(left_2, -2, lambda z: (z - 2) % Z < limit)
+    total = wide(terms[0])
+    for arrived in (right_1, left_1, right_2, left_2):
+        total = total + wide(arrived)
+    return total, beside
 
 
 def shift_yc(array, y_step, c_step):
@@ -74,6 +81,15 @@
     return lax.ppermute(array, "seq", [(s, s ^ 1) for s in range(Z * Y * C)])
 
 
+def exchange_yc(blocks):
+    relayed = shift_yc(blocks[5], -1, 1)
+    arrived = [blocks[0]] + [None] * (Y * C - 1)
+    for i in (4, 7, 3, 6, 2, 1):
+        arrived[i] = shift_yc(blocks[i], i // C, i % C)
+    arrived[5] = shift_yc(relayed, -1, 0)
+    return arrived
+
+
 def shift_x(array, step):
     return lax.ppermute(array, "head", [(x, (x + step) % X) for x in range(X)])
 
@@ -98,15 +114,14 @@
 
 
 def pack_kernel(block_ref, z_ref, *refs):
-    pieces, out_ref = refs[:Z], refs[Z]
+    pieces, out_refs = refs[:Z], refs[Z:]
     for j in range(Z):
         owner_z = (z_ref[0] + j) % Z
 
         @pl.when(owner_z < Z_FULL)
         def _():
-            for peer in range(Y * C):
-                place = peer * Z_FULL + owner_z
-                out_ref[place] = pieces[j][block_ref[place]]
+            for i, out_ref in enumerate(out_refs):
+                out_ref[owner_z] = pieces[j][block_ref[i * Z_FULL + owner_z]]
 
 
 def pack(blocks, z, pieces):
@@ -115,15 +130,18 @@
     return pl.pallas_call(
         pack_kernel,
         in_specs=[smem, smem] + [vmem] * Z,
-        out_specs=vmem,
-        out_shape=jax.ShapeDtypeStruct((blocks.shape[0], *pieces[0].shape[1:]), BF16),
+        out_specs=[vmem] * (Y * C),
+        out_shape=[jax.ShapeDtypeStruct((Z_FULL, *pieces[0].shape[1:]), BF16)] * (Y * C),
         name="pack",
     )(blocks, z.reshape(1), *pieces)
 
 
-def pick_kernel(place_ref, own_ref, fetched_ref, *refs):
-    owns, (low_ref, high_ref) = refs[:-2], refs[-2:]
+def pick_kernel(place_ref, own_ref, *refs):
+    fetched, owns = refs[: Y * C], refs[Y * C : -3]
+    low_ref, high_ref, blocks = refs[-3:]
     n_low, n_high = low_ref.shape[0], high_ref.shape[0]
+    for i, part in enumerate(fetched):
+        blocks[i * Z_FULL : (i + 1) * Z_FULL] = part[...]
     for j, own in enumerate(owns):
 
         @pl.when(own_ref[0] == j)
@@ -131,9 +149,9 @@
             low_ref[n_low - 1] = own[...]
 
     for slot in range(n_low - 1):
-        low_ref[slot] = fetched_ref[place_ref[slot]]
+        low_ref[slot] = blocks[place_ref[slot]]
     for slot in range(n_high):
-        high_ref[slot] = fetched_ref[place_ref[n_low - 1 + slot]]
+        high_ref[slot] = blocks[place_ref[n_low - 1 + slot]]
 
 
 def pick(place, own_index, fetched, owns):
@@ -141,16 +159,18 @@
     smem = pl.BlockSpec(memory_space=pltpu.SMEM)
     n_high = place.shape[0] // 2
     n_low = place.shape[0] - n_high + 1
+    block = fetched[0].shape[1:]
     return pl.pallas_call(
         pick_kernel,
-        in_specs=[smem, smem, vmem] + [vmem] * len(owns),
+        in_specs=[smem, smem] + [vmem] * (len(fetched) + len(owns)),
         out_specs=[vmem, vmem],
         out_shape=[
-            jax.ShapeDtypeStruct((n_low, *fetched.shape[1:]), BF16),
-            jax.ShapeDtypeStruct((n_high, *fetched.shape[1:]), BF16),
+            jax.ShapeDtypeStruct((n_low, *block), BF16),
+            jax.ShapeDtypeStruct((n_high, *block), BF16),
         ],
+        scratch_shapes=[pltpu.VMEM((Y * C * Z_FULL, *block), BF16)],
         name="pick",
-    )(place, own_index.reshape(1), fetched, *owns)
+    )(place, own_index.reshape(1), *fetched, *owns)
 
 
 def attend_kernel(x_ref, q_ref, dl_ref, *refs):
@@ -365,12 +385,16 @@
     asked_here = trade(wanted.reshape(peers, 1, Z_FULL), YC_GROUPS).reshape(peers, Z_FULL)
     z_off = (jnp.arange(Z_FULL, dtype=jnp.int32) - z) % Z
     distance = jnp.arange(peers, dtype=jnp.int32)
+    peer_ids = jnp.arange(peers, dtype=jnp.int32)[None, :, None]
+    to_peer = (y + distance // C) % Y * C + (c ^ distance % C)
+    asked_to = jnp.sum(jnp.where(to_peer[:, None, None] == peer_ids, asked_here[None], 0), axis=1)
     from_peer = (y - distance // C) % Y * C + (c ^ distance % C)
-    pick_peer = from_peer[:, None, None] == jnp.arange(peers, dtype=jnp.int32)[None, :, None]
-    asked_from = jnp.sum(jnp.where(pick_peer, asked_here[None], 0), axis=1)
+    asked_from = jnp.sum(jnp.where(from_peer[:, None, None] == peer_ids, asked_here[None], 0), axis=1)
     at_owner = jnp.where(
         asked_from >= 0, z_off[None, :] * block_count + asked_from, Z * block_count
     ).reshape(places)
+    place_fetched = (y - owner // C) % Y * C + (owner % C ^ c)
+    place_fetched = place_fetched * Z_FULL + owner // peers
     place_back = (owner // C % Y - y) % Y * C + (owner % C ^ c)
     place_back = place_back * Z_FULL + owner // peers
 
@@ -392,15 +416,16 @@
                 ],
             )
         )
-    packed = pack(jnp.maximum(asked_here, 0).reshape(places), z, pieces)
-    fetched = trade(packed.reshape(peers, Z_FULL, quarter, width), YC_GROUPS)
+    packed = pack(jnp.maximum(asked_to, 0).reshape(places), z, pieces)
+    packed, query = lax.optimization_barrier((packed, query))
+    fetched = exchange_yc(packed)
     d_latent = narrow(
         jnp.einsum("qhv,hcv->qhc", grad_out, value_weight, preferred_element_type=F32)
     )
     fetched, d_latent, query_rows = lax.optimization_barrier(
         (fetched, d_latent.reshape(rows, KVL), query.reshape(rows, width))
     )
-    low, high = pick(place, seq % block_count, fetched.reshape(places, quarter, width), owns)
+    low, high = pick(place_fetched, seq % block_count, fetched, owns)
 
     low_from_left = shift_x(low, 1)
     high_from_right = shift_x(high, -1)
@@ -451,9 +476,7 @@
     *back, own_share = send_back(
         place_back, [d_low[0], low_right, low_left], [d_high[0], high_left, high_right]
     )
-    received = [back[0]] + [None] * (peers - 1)
-    for i in (5, 4, 3, 7, 2, 6, 1):
-        received[i] = shift_yc(back[i], i // C, i % C)
+    received = exchange_yc(back)
     own_back = []
     for j in range(block_count):
         own_back.append(
@@ -467,9 +490,9 @@
             )
         )
     d_query = jnp.transpose(d_query.reshape(query.shape), (1, 2, 0))
-    received, d_query = lax.optimization_barrier((received, d_query))
     by_z = by_owner(at_owner, received, block_count)
-    d_cache = reduce_z(by_z, Z_FULL) + wide(jnp.stack(own_back))
+    d_cache, d_query = reduce_z(by_z, Z_FULL, d_query)
+    d_cache = d_cache + wide(jnp.stack(own_back))
     return jnp.transpose(d_query, (2, 0, 1)), d_cache, d_value_weight
 
 

time: 294 us -> 320 us (1.088)
  the two profiles are of different devices: /device:TPU:193 before, /device:TPU:208 now
where the time goes in v2:
time: 320 us; the launch traced here: 318 us
  starting transfers between devices  133 us (42%)
  waiting for transfers between devices  94.7 us (30%)
  local copies, waits for them, and re-layouts  29.1 us (9%)
  Pallas kernels  24.7 us (8%)
  blocking collectives  18.9 us (6%)
  other arithmetic  8.58 us (3%)
  matrix products  7.63 us (2%)
    ppermute x14, starting transfers between devices, shift_z(): return lax.ppermute(array, 'seq', pairs)  42.4 us
    ppermute x4, waiting for transfers between devices, local(): lax.ppermute(own_share, 'seq', [((o - FIRST_OWN_OWNER) * block_count + j,...  31.3 us
    ppermute x16, waiting for transfers between devices, shift_yc(): return lax.ppermute(array, 'seq', pairs)  26.8 us
    ppermute x16, starting transfers between devices, shift_yc(): return lax.ppermute(array, 'seq', pairs)  26.5 us
    all_to_all x4, starting transfers between devices, trade(): lax.all_to_all(blocks, 'seq', split_axis=0, concat_axis=0, axis_index_gro...  26.1 us
    ppermute x12, waiting for transfers between devices, shift_x(): return lax.ppermute(array, 'head', [(x, (x + step) % X) for x in range(X)])  20.3 us
    all_to_all x1, blocking collectives, trade(): lax.all_to_all(blocks, 'seq', split_axis=0, concat_axis=0, axis_index_gro...  18.9 us
    ppermute x12, starting transfers between devices, shift_x(): return lax.ppermute(array, 'head', [(x, (x + step) % X) for x in range(X)])  16.5 us
  transfers between devices with their start and end apart: 55, of which 21 were waited for; matrix products, arithmetic and copies ran while one was open for 8% of the time, Pallas kernels for 1%

profile of v2, /device:TPU:208, one launch (start us, length us, event | category | flops | bytes accessed | tf_op | source)
XLA Modules:
  0.0 318.3 jit_solution(6807089007329178218)
XLA Ops:
  10.1 4.8 %all-to-all-start = ((s32[8,1,6]{2,1,0:T(1,128)}), s32[8,1,6]{2,1,0:T(1,128)S(1)}, u32[]{:S(2)}, u32[]{:S(2)}) async-start(s32[8,1,6]{2,1,0:T(1,128)} %bitcast), calls=%async_computation | async-start | bytes 8192 | tf_op jit(solution)/shard_map/all_to_all | solution.py:98
  18.2 11.0 %collective-permute-start.4 = (bf16[4,32,576]{2,1,0:T(8,128)(2,1)S(1)}, bf16[4,32,576]{2,1,0:T(8,128)(2,1)}, u32[]{:S(2)}, u32[]{:S(2)}) collective-permute-start(bf16[4,32,576]{2,1,0:T(8,128)(2,1)S(1)} %collective-permute-done.3.refs_6_), channel_id=1, source_target_pairs={{64,128},{68,132},{72,136},{76,140},{80,144},{84,148},{88,152},{92... | collective-permute-start | bytes 442376 | tf_op jit(solution)/shard_map/ppermute | solution.py:39
  35.9 3.8 %collective-permute-done.2.refs_3_ = bf16[4,32,576]{2,1,0:T(8,128)(2,1)} collective-permute-done((bf16[4,32,576]{2,1,0:T(8,128)(2,1)S(1)}, bf16[4,32,576]{2,1,0:T(8,128)(2,1)}, u32[]{:S(2)}, u32[]{:S(2)}) %collective-permute-start.2) | collective-permute-done | bytes 147488 | tf_op jit(solution)/shard_map/ppermute | solution.py:39
  52.9 3.3 %collective-permute-done.9.refs_3_ = bf16[6,32,576]{2,1,0:T(8,128)(2,1)S(1)} collective-permute-done((bf16[6,32,576]{2,1,0:T(8,128)(2,1)}, bf16[6,32,576]{2,1,0:T(8,128)(2,1)S(1)}, u32[]{:S(2)}, u32[]{:S(2)}) %collective-permute-start.9) | collective-permute-done | bytes 221216 | tf_op jit(solution)/shard_map/ppermute | solution.py:77
  56.2 6.1 %collective-permute-start.15 = (bf16[32,576]{1,0:T(8,128)(2,1)S(1)}, bf16[32,576]{1,0:T(8,128)(2,1)}, u32[]{:S(2)}, u32[]{:S(2)}) collective-permute-start(bf16[32,576]{1,0:T(8,128)(2,1)S(1)} %get-tuple-element.135), channel_id=1, source_target_pairs={{192,0},{196,16},{200,32},{204,48},{208,64},{212,80},{216,96},{220... | collective-permute-start | bytes 110600 | tf_op jit(solution)/shard_map/ppermute | solution.py:410
  62.8 6.0 %collective-permute-start.16 = (bf16[32,576]{1,0:T(8,128)(2,1)S(1)}, bf16[32,576]{1,0:T(8,128)(2,1)}, u32[]{:S(2)}, u32[]{:S(2)}) collective-permute-start(bf16[32,576]{1,0:T(8,128)(2,1)S(1)} %get-tuple-element.134), channel_id=1, source_target_pairs={{192,4},{196,20},{200,36},{204,52},{208,68},{212,84},{216,100},{22... | collective-permute-start | bytes 110600 | tf_op jit(solution)/shard_map/ppermute | solution.py:410
  77.0 4.1 %copy.37 = bf16[128,16,512]{2,1,0:T(8,128)(2,1)} copy(bf16[128,16,512]{2,0,1:T(8,128)(2,1)} %convert_bitcast_fusion) | data formatting | bytes 4194304 | tf_op jit(solution)/shard_map/convert_element_type | solution.py:109
  81.1 4.9 %copy.38 = bf16[128,16,576]{2,1,0:T(8,128)(2,1)} copy(bf16[128,16,576]{0,2,1:T(8,128)(2,1)} %param.5) | data formatting | bytes 4718592 | tf_op jit(solution)/shard_map/optimization_barrier | solution.py:420
  93.5 3.7 %collective-permute-done.19.refs_1_.refs_5_ = bf16[7,32,576]{2,1,0:T(8,128)(2,1)S(1)} collective-permute-done((bf16[7,32,576]{2,1,0:T(8,128)(2,1)}, bf16[7,32,576]{2,1,0:T(8,128)(2,1)S(1)}, u32[]{:S(2)}, u32[]{:S(2)}) %collective-permute-start.19) | collective-permute-done | bytes 258080 | tf_op jit(solution)/shard_map/ppermute | solution.py:94
  102.3 7.8 %collective-permute-done.22.refs_9_ = bf16[6,32,576]{2,1,0:T(8,128)(2,1)} collective-permute-done((bf16[6,32,576]{2,1,0:T(8,128)(2,1)}, bf16[6,32,576]{2,1,0:T(8,128)(2,1)}, u32[]{:S(2)}, u32[]{:S(2)}) %collective-permute-start.22) | collective-permute-done | bytes 221216 | tf_op jit(solution)/shard_map/ppermute | solution.py:94
  110.9 14.6 %attend.1 = (bf16[2048,576]{1,0:T(8,128)(2,1)}, bf16[2048,512]{1,0:T(8,128)(2,1)}, bf16[7,32,576]{2,1,0:T(8,128)(2,1)}, bf16[7,32,576]{2,1,0:T(8,128)(2,1)}, bf1...) custom-call(s32[1]{0:T(128)} %bitcast.2.x_ref, ...), custom_call_target="tpu_custom_call" | custom-call | tf_op jit(solution)/shard_map/attend/pallas_call | solution.py:271
  125.5 4.0 %fusion.3 = bf16[16,512,128]{2,1,0:T(8,128)(2,1)S(1)} fusion(bf16[128,16,512]{2,1,0:T(8,128)(2,1)} %bitcast.34, bf16[128,16,128]{2,1,0:T(8,128)(2,1)S(1)} %copy-done.16), kind=kOutput, calls=%fused_computation.5 | convolution fusion | flops 269484032 | bytes 4718592 | tf_op jit(solution)/shard_map/qhc,qhv->hcv/dot_general | solution.py:456
  135.6 18.9 %all_to_all.25 = bf16[4,1024,128]{2,1,0:T(8,128)(2,1)S(1)} all-to-all(bf16[4,1024,128]{2,1,0:T(8,128)(2,1)S(1)} %fusion), channel_id=1, replica_groups={{0,8,16,24},{4,12,20,28},{32,40,48,56},{36,44,52,60},{64,72,80,88},{68,..., dimensions={0} | all-to-all | bytes 2097152 | tf_op jit(solution)/shard_map/all_to_all | solution.py:98
  155.4 6.8 %all-to-all-start.2 = ((bf16[8,128,128]{2,1,0:T(8,128)(2,1)}), bf16[8,128,128]{2,1,0:T(8,128)(2,1)S(1)}, u32[]{:S(2)}, u32[]{:S(2)}) async-start(bf16[8,128,128]{2,1,0:T(8,128)(2,1)} %bitcast.20), calls=%async_computation.2 | async-start | bytes 524288 | tf_op jit(solution)/shard_map/all_to_all | solution.py:98
  162.6 7.1 %all-to-all-done.2 = bf16[8,128,128]{2,1,0:T(8,128)(2,1)S(1)} async-done(((bf16[8,128,128]{2,1,0:T(8,128)(2,1)}), bf16[8,128,128]{2,1,0:T(8,128)(2,1)S(1)}, u32[]{:S(2)}, u32[]{:S(2)}) %all-to-all-start.2) | async-done | bytes 262176 | tf_op jit(solution)/shard_map/all_to_all | solution.py:98
  170.5 7.2 %all-to-all-start.3 = ((bf16[8,128,128]{2,1,0:T(8,128)(2,1)}), bf16[8,128,128]{2,1,0:T(8,128)(2,1)S(1)}, u32[]{:S(2)}, u32[]{:S(2)}) async-start(bf16[8,128,128]{2,1,0:T(8,128)(2,1)} %broadcast_in_dim.88), calls=%async_computation.3 | async-start | bytes 524288 | tf_op jit(solution)/shard_map/all_to_all | solution.py:98
  177.6 3.2 %collective-permute-start.28 = (bf16[6,32,576]{2,1,0:T(8,128)(2,1)}, bf16[6,32,576]{2,1,0:T(8,128)(2,1)S(1)}, u32[]{:S(2)}, u32[]{:S(2)}) collective-permute-start(bf16[6,32,576]{2,1,0:T(8,128)(2,1)} %get-tuple-element.97), channel_id=1, source_target_pairs={{0,3},{1,0},{2,1},{3,2},{4,7},{5,4},{6,5},{7,6},{8,11},{9,8},{10,9... | collective-permute-start | bytes 663560 | tf_op jit(solution)/shard_map/ppermute | solution.py:94
  181.6 3.2 %collective-permute-start.27 = (bf16[7,32,576]{2,1,0:T(8,128)(2,1)}, bf16[7,32,576]{2,1,0:T(8,128)(2,1)S(1)}, u32[]{:S(2)}, u32[]{:S(2)}) collective-permute-start(bf16[7,32,576]{2,1,0:T(8,128)(2,1)} %add_convert_fusion), channel_id=1, source_target_pairs={{0,3},{1,0},{2,1},{3,2},{4,7},{5,4},{6,5},{7,6},{8,11},{9,8},{10,9... | collective-permute-start | bytes 774152 | tf_op jit(solution)/shard_map/ppermute | solution.py:94
  186.5 7.4 %all-to-all-start.4 = ((bf16[8,1024,128]{2,1,0:T(8,128)(2,1)}), bf16[8,1024,128]{2,1,0:T(8,128)(2,1)}, u32[]{:S(2)}, u32[]{:S(2)}) async-start(bf16[8,1024,128]{2,1,0:T(8,128)(2,1)} %broadcast_in_dim.89), calls=%async_computation.4 | async-start | bytes 4194304 | tf_op jit(solution)/shard_map/all_to_all | solution.py:98
  195.8 8.5 %collective-permute-done.30.refs_5_ = bf16[6,32,576]{2,1,0:T(8,128)(2,1)S(1)} collective-permute-done((bf16[6,32,576]{2,1,0:T(8,128)(2,1)S(1)}, bf16[6,32,576]{2,1,0:T(8,128)(2,1)S(1)}, u32[]{:S(2)}, u32[]{:S(2)}) %collective-permute-start.30) | collective-permute-done | bytes 221216 | tf_op jit(solution)/shard_map/ppermute | solution.py:94
  211.1 10.5 %collective-permute-start.37 = (bf16[6,32,576]{2,1,0:T(8,128)(2,1)}, bf16[6,32,576]{2,1,0:T(8,128)(2,1)}, u32[]{:S(2)}, u32[]{:S(2)}) collective-permute-start(bf16[6,32,576]{2,1,0:T(8,128)(2,1)} %get-tuple-element.106), channel_id=1, source_target_pairs={{0,24},{4,28},{8,0},{12,4},{16,8},{20,12},{24,16},{28,20},{32,56},... | collective-permute-start | bytes 663560 | tf_op jit(solution)/shard_map/ppermute | solution.py:77
  228.3 5.4 %collective-permute-done.34.refs_4_ = bf16[6,32,576]{2,1,0:T(8,128)(2,1)S(1)} collective-permute-done((bf16[6,32,576]{2,1,0:T(8,128)(2,1)}, bf16[6,32,576]{2,1,0:T(8,128)(2,1)S(1)}, u32[]{:S(2)}, u32[]{:S(2)}) %collective-permute-start.34) | collective-permute-done | bytes 221216 | tf_op jit(solution)/shard_map/ppermute | solution.py:77
  235.3 4.1 %collective-permute-done.38.refs_7_ = bf16[6,32,576]{2,1,0:T(8,128)(2,1)} collective-permute-done((bf16[6,32,576]{2,1,0:T(8,128)(2,1)}, bf16[6,32,576]{2,1,0:T(8,128)(2,1)}, u32[]{:S(2)}, u32[]{:S(2)}) %collective-permute-start.38) | collective-permute-done | bytes 221216 | tf_op jit(solution)/shard_map/ppermute | solution.py:77
  239.4 5.8 %collective-permute-done.36.refs_5_ = bf16[6,32,576]{2,1,0:T(8,128)(2,1)} collective-permute-done((bf16[6,32,576]{2,1,0:T(8,128)(2,1)}, bf16[6,32,576]{2,1,0:T(8,128)(2,1)}, u32[]{:S(2)}, u32[]{:S(2)}) %collective-permute-start.36) | collective-permute-done | bytes 221216 | tf_op jit(solution)/shard_map/ppermute | solution.py:77
  251.1 5.1 %collective-permute-start.39 = (bf16[4,32,576]{2,1,0:T(8,128)(2,1)}, bf16[4,32,576]{2,1,0:T(8,128)(2,1)S(1)}, u32[]{:S(2)}, u32[]{:S(2)}) collective-permute-start(bf16[4,32,576]{2,1,0:T(8,128)(2,1)} %get-tuple-element.108), channel_id=1, source_target_pairs={{0,64},{4,68},{8,72},{12,76},{16,80},{20,84},{24,88},{28,92},{32,9... | collective-permute-start | bytes 442376 | tf_op jit(solution)/shard_map/ppermute | solution.py:39
  258.7 3.4 %collective-permute-start.41 = (bf16[4,32,576]{2,1,0:T(8,128)(2,1)}, bf16[4,32,576]{2,1,0:T(8,128)(2,1)S(1)}, u32[]{:S(2)}, u32[]{:S(2)}) collective-permute-start(bf16[4,32,576]{2,1,0:T(8,128)(2,1)} %get-tuple-element.110), channel_id=1, source_target_pairs={{0,224},{4,228},{8,232},{12,236},{16,240},{20,244},{24,248},{28,25... | collective-permute-start | bytes 442376 | tf_op jit(solution)/shard_map/ppermute | solution.py:39
  262.1 4.8 %copy.39 = bf16[128,16,576]{0,2,1:T(8,128)(2,1)} copy(bf16[128,16,576]{2,1,0:T(8,128)(2,1)} %bitcast.33) | data formatting | bytes 4718592 | tf_op jit(solution)/shard_map/reshape | solution.py:492
  270.3 4.6 %collective-permute-start.45 = (bf16[4,32,576]{2,1,0:T(8,128)(2,1)S(1)}, bf16[4,32,576]{2,1,0:T(8,128)(2,1)S(1)}, u32[]{:S(2)}, u32[]{:S(2)}) collective-permute-start(bf16[4,32,576]{2,1,0:T(8,128)(2,1)S(1)} %add_convert_fusion.2), channel_id=1, source_target_pairs={{64,0},{68,4},{72,8},{76,12},{80,16},{84,20},{88,24},{92,28},{96,3... | collective-permute-start | bytes 442376 | tf_op jit(solution)/shard_map/ppermute | solution.py:39
  275.0 3.5 %collective-permute-start.44 = (bf16[4,32,576]{2,1,0:T(8,128)(2,1)S(1)}, bf16[4,32,576]{2,1,0:T(8,128)(2,1)S(1)}, u32[]{:S(2)}, u32[]{:S(2)}) collective-permute-start(bf16[4,32,576]{2,1,0:T(8,128)(2,1)S(1)} %add_convert_fusion.3), channel_id=1, source_target_pairs={{0,64},{4,68},{8,72},{12,76},{16,80},{20,84},{24,88},{28,92},{32,9... | collective-permute-start | bytes 442376 | tf_op jit(solution)/shard_map/ppermute | solution.py:39
  279.8 10.6 %collective-permute-done.48 = bf16[32,576]{1,0:T(8,128)(2,1)S(1)} collective-permute-done((bf16[32,576]{1,0:T(8,128)(2,1)S(1)}, bf16[32,576]{1,0:T(8,128)(2,1)S(1)}, u32[]{:S(2)}, u32[]{:S(2)}) %collective-permute-start.48) | collective-permute-done | bytes 36896 | tf_op jit(solution)/shard_map/ppermute | solution.py:483
  291.7 10.3 %collective-permute-done.47 = bf16[32,576]{1,0:T(8,128)(2,1)S(1)} collective-permute-done((bf16[32,576]{1,0:T(8,128)(2,1)S(1)}, bf16[32,576]{1,0:T(8,128)(2,1)S(1)}, u32[]{:S(2)}, u32[]{:S(2)}) %collective-permute-start.47) | collective-permute-done | bytes 36896 | tf_op jit(solution)/shard_map/ppermute | solution.py:483
  304.0 10.3 %collective-permute-done.46 = bf16[32,576]{1,0:T(8,128)(2,1)S(1)} collective-permute-done((bf16[32,576]{1,0:T(8,128)(2,1)S(1)}, bf16[32,576]{1,0:T(8,128)(2,1)S(1)}, u32[]{:S(2)}, u32[]{:S(2)}) %collective-permute-start.46) | collective-permute-done | bytes 36896 | tf_op jit(solution)/shard_map/ppermute | solution.py:483
  (184 shorter events, 102.2 us)
Async XLA Ops:
  2.3 33.6 %collective-permute-start = (bf16[4,32,576]{2,1,0:T(8,128)(2,1)S(1)}, bf16[4,32,576]{2,1,0:T(8,128)(2,1)S(1)}, u32[]{:S(2)}, u32[]{:S(2)}) collective-permute-start(bf16[4,32,576]{2,1,0:T(8,128)(2,1)S(1)} %bitcast.35), channel_id=1, source_target_pairs={{0,224},{4,228},{8,232},{12,236},{16,240},{20,244},{24,248},{28,25... | collective-permute-start | bytes 442376 | tf_op jit(solution)/shard_map/ppermute | solution.py:39
  2.9 29.4 %collective-permute-start.1 = (bf16[4,32,576]{2,1,0:T(8,128)(2,1)S(1)}, bf16[4,32,576]{2,1,0:T(8,128)(2,1)S(1)}, u32[]{:S(2)}, u32[]{:S(2)}) collective-permute-start(bf16[4,32,576]{2,1,0:T(8,128)(2,1)S(1)} %bitcast.36), channel_id=1, source_target_pairs={{0,192},{4,196},{8,200},{12,204},{16,208},{20,212},{24,216},{28,22... | collective-permute-start | bytes 442376 | tf_op jit(solution)/shard_map/ppermute | solution.py:39
  5.5 30.3 %collective-permute-start.6 = (bf16[4,32,576]{2,1,0:T(8,128)(2,1)S(1)}, bf16[4,32,576]{2,1,0:T(8,128)(2,1)S(1)}, u32[]{:S(2)}, u32[]{:S(2)}) collective-permute-start(bf16[4,32,576]{2,1,0:T(8,128)(2,1)S(1)} %bitcast.38), channel_id=1, source_target_pairs={{0,32},{4,36},{8,40},{12,44},{16,48},{20,52},{24,56},{28,60},{32,6... | collective-permute-start | bytes 442376 | tf_op jit(solution)/shard_map/ppermute | solution.py:39
  18.2 21.5 %collective-permute-start.4 = (bf16[4,32,576]{2,1,0:T(8,128)(2,1)S(1)}, bf16[4,32,576]{2,1,0:T(8,128)(2,1)}, u32[]{:S(2)}, u32[]{:S(2)}) collective-permute-start(bf16[4,32,576]{2,1,0:T(8,128)(2,1)S(1)} %collective-permute-done.3.refs_6_), channel_id=1, source_target_pairs={{64,128},{68,132},{72,136},{76,140},{80,144},{84,148},{88,152},{92... | collective-permute-start | bytes 442376 | tf_op jit(solution)/shard_map/ppermute | solution.py:39
  46.1 16.8 %collective-permute-start.10 = (bf16[6,32,576]{2,1,0:T(8,128)(2,1)}, bf16[6,32,576]{2,1,0:T(8,128)(2,1)}, u32[]{:S(2)}, u32[]{:S(2)}) collective-permute-start(bf16[6,32,576]{2,1,0:T(8,128)(2,1)} %get-tuple-element.75), channel_id=1, source_target_pairs={{0,16},{4,20},{8,24},{12,28},{16,0},{20,4},{24,8},{28,12},{32,48},... | collective-permute-start | bytes 663560 | tf_op jit(solution)/shard_map/ppermute | solution.py:77
  46.1 22.8 %collective-permute-start.11 = (bf16[6,32,576]{2,1,0:T(8,128)(2,1)}, bf16[6,32,576]{2,1,0:T(8,128)(2,1)}, u32[]{:S(2)}, u32[]{:S(2)}) collective-permute-start(bf16[6,32,576]{2,1,0:T(8,128)(2,1)} %get-tuple-element.76), channel_id=1, source_target_pairs={{0,28},{4,24},{8,4},{12,0},{16,12},{20,8},{24,20},{28,16},{32,60},... | collective-permute-start | bytes 663560 | tf_op jit(solution)/shard_map/ppermute | solution.py:77
  47.8 23.0 %collective-permute-start.13 = (bf16[6,32,576]{2,1,0:T(8,128)(2,1)}, bf16[6,32,576]{2,1,0:T(8,128)(2,1)}, u32[]{:S(2)}, u32[]{:S(2)}) collective-permute-start(bf16[6,32,576]{2,1,0:T(8,128)(2,1)} %get-tuple-element.77), channel_id=1, source_target_pairs={{0,24},{4,28},{8,0},{12,4},{16,8},{20,12},{24,16},{28,20},{32,56},... | collective-permute-start | bytes 663560 | tf_op jit(solution)/shard_map/ppermute | solution.py:77
  51.8 20.8 %collective-permute-start.14 = (bf16[6,32,576]{2,1,0:T(8,128)(2,1)}, bf16[6,32,576]{2,1,0:T(8,128)(2,1)}, u32[]{:S(2)}, u32[]{:S(2)}) collective-permute-start(bf16[6,32,576]{2,1,0:T(8,128)(2,1)} %get-tuple-element.78), channel_id=1, source_target_pairs={{0,28},{4,24},{8,4},{12,0},{16,12},{20,8},{24,20},{28,16},{32,60},... | collective-permute-start | bytes 663560 | tf_op jit(solution)/shard_map/ppermute | solution.py:77
  56.2 29.8 %collective-permute-start.15 = (bf16[32,576]{1,0:T(8,128)(2,1)S(1)}, bf16[32,576]{1,0:T(8,128)(2,1)}, u32[]{:S(2)}, u32[]{:S(2)}) collective-permute-start(bf16[32,576]{1,0:T(8,128)(2,1)S(1)} %get-tuple-element.135), channel_id=1, source_target_pairs={{192,0},{196,16},{200,32},{204,48},{208,64},{212,80},{216,96},{220... | collective-permute-start | bytes 110600 | tf_op jit(solution)/shard_map/ppermute | solution.py:410
  62.8 23.2 %collective-permute-start.16 = (bf16[32,576]{1,0:T(8,128)(2,1)S(1)}, bf16[32,576]{1,0:T(8,128)(2,1)}, u32[]{:S(2)}, u32[]{:S(2)}) collective-permute-start(bf16[32,576]{1,0:T(8,128)(2,1)S(1)} %get-tuple-element.134), channel_id=1, source_target_pairs={{192,4},{196,20},{200,36},{204,52},{208,68},{212,84},{216,100},{22... | collective-permute-start | bytes 110600 | tf_op jit(solution)/shard_map/ppermute | solution.py:410
  68.8 17.2 %collective-permute-start.17 = (bf16[32,576]{1,0:T(8,128)(2,1)S(1)}, bf16[32,576]{1,0:T(8,128)(2,1)}, u32[]{:S(2)}, u32[]{:S(2)}) collective-permute-start(bf16[32,576]{1,0:T(8,128)(2,1)S(1)} %get-tuple-element.133), channel_id=1, source_target_pairs={{192,8},{196,24},{200,40},{204,56},{208,72},{212,88},{216,104},{22... | collective-permute-start | bytes 110600 | tf_op jit(solution)/shard_map/ppermute | solution.py:410
  70.7 15.3 %collective-permute-start.18 = (bf16[32,576]{1,0:T(8,128)(2,1)S(1)}, bf16[32,576]{1,0:T(8,128)(2,1)}, u32[]{:S(2)}, u32[]{:S(2)}) collective-permute-start(bf16[32,576]{1,0:T(8,128)(2,1)S(1)} %get-tuple-element.132), channel_id=1, source_target_pairs={{192,12},{196,28},{200,44},{204,60},{208,76},{212,92},{216,108},{2... | collective-permute-start | bytes 110600 | tf_op jit(solution)/shard_map/ppermute | solution.py:410
  91.9 18.1 %collective-permute-start.21 = (bf16[7,32,576]{2,1,0:T(8,128)(2,1)}, bf16[7,32,576]{2,1,0:T(8,128)(2,1)S(1)}, u32[]{:S(2)}, u32[]{:S(2)}) collective-permute-start(bf16[7,32,576]{2,1,0:T(8,128)(2,1)} %get-tuple-element.90.refs_0_.refs_4_), channel_id=1, source_target_pairs={{0,3},{1,0},{2,1},{3,2},{4,7},{5,4},{6,5},{7,6},{8,11},{9,8},{10,9... | collective-permute-start | bytes 774152 | tf_op jit(solution)/shard_map/ppermute | solution.py:94
  155.4 14.3 %all-to-all-start.2 = ((bf16[8,128,128]{2,1,0:T(8,128)(2,1)}), bf16[8,128,128]{2,1,0:T(8,128)(2,1)S(1)}, u32[]{:S(2)}, u32[]{:S(2)}) async-start(bf16[8,128,128]{2,1,0:T(8,128)(2,1)} %bitcast.20), calls=%async_computation.2 | async-start | bytes 524288 | tf_op jit(solution)/shard_map/all_to_all | solution.py:98
  162.2 18.7 %collective-permute-start.26 = (bf16[7,32,576]{2,1,0:T(8,128)(2,1)}, bf16[7,32,576]{2,1,0:T(8,128)(2,1)S(1)}, u32[]{:S(2)}, u32[]{:S(2)}) collective-permute-start(bf16[7,32,576]{2,1,0:T(8,128)(2,1)} %get-tuple-element.94), channel_id=1, source_target_pairs={{0,3},{1,0},{2,1},{3,2},{4,7},{5,4},{6,5},{7,6},{8,11},{9,8},{10,9... | collective-permute-start | bytes 774152 | tf_op jit(solution)/shard_map/ppermute | solution.py:94
  170.5 14.4 %all-to-all-start.3 = ((bf16[8,128,128]{2,1,0:T(8,128)(2,1)}), bf16[8,128,128]{2,1,0:T(8,128)(2,1)S(1)}, u32[]{:S(2)}, u32[]{:S(2)}) async-start(bf16[8,128,128]{2,1,0:T(8,128)(2,1)} %broadcast_in_dim.88), calls=%async_computation.3 | async-start | bytes 524288 | tf_op jit(solution)/shard_map/all_to_all | solution.py:98
  177.6 18.2 %collective-permute-start.25 = (bf16[7,32,576]{2,1,0:T(8,128)(2,1)}, bf16[7,32,576]{2,1,0:T(8,128)(2,1)S(1)}, u32[]{:S(2)}, u32[]{:S(2)}) collective-permute-start(bf16[7,32,576]{2,1,0:T(8,128)(2,1)} %get-tuple-element.93), channel_id=1, source_target_pairs={{0,1},{1,2},{2,3},{3,0},{4,5},{5,6},{6,7},{7,4},{8,9},{9,10},{10,1... | collective-permute-start | bytes 774152 | tf_op jit(solution)/shard_map/ppermute | solution.py:94
  177.6 17.5 %collective-permute-start.28 = (bf16[6,32,576]{2,1,0:T(8,128)(2,1)}, bf16[6,32,576]{2,1,0:T(8,128)(2,1)S(1)}, u32[]{:S(2)}, u32[]{:S(2)}) collective-permute-start(bf16[6,32,576]{2,1,0:T(8,128)(2,1)} %get-tuple-element.97), channel_id=1, source_target_pairs={{0,3},{1,0},{2,1},{3,2},{4,7},{5,4},{6,5},{7,6},{8,11},{9,8},{10,9... | collective-permute-start | bytes 663560 | tf_op jit(solution)/shard_map/ppermute | solution.py:94
  181.6 22.6 %collective-permute-start.27 = (bf16[7,32,576]{2,1,0:T(8,128)(2,1)}, bf16[7,32,576]{2,1,0:T(8,128)(2,1)S(1)}, u32[]{:S(2)}, u32[]{:S(2)}) collective-permute-start(bf16[7,32,576]{2,1,0:T(8,128)(2,1)} %add_convert_fusion), channel_id=1, source_target_pairs={{0,3},{1,0},{2,1},{3,2},{4,7},{5,4},{6,5},{7,6},{8,11},{9,8},{10,9... | collective-permute-start | bytes 774152 | tf_op jit(solution)/shard_map/ppermute | solution.py:94
  186.5 128.7 %all-to-all-start.4 = ((bf16[8,1024,128]{2,1,0:T(8,128)(2,1)}), bf16[8,1024,128]{2,1,0:T(8,128)(2,1)}, u32[]{:S(2)}, u32[]{:S(2)}) async-start(bf16[8,1024,128]{2,1,0:T(8,128)(2,1)} %broadcast_in_dim.89), calls=%async_computation.4 | async-start | bytes 4194304 | tf_op jit(solution)/shard_map/all_to_all | solution.py:98
  207.2 16.2 %collective-permute-start.32 = (bf16[6,32,576]{2,1,0:T(8,128)(2,1)S(1)}, bf16[6,32,576]{2,1,0:T(8,128)(2,1)S(1)}, u32[]{:S(2)}, u32[]{:S(2)}) collective-permute-start(bf16[6,32,576]{2,1,0:T(8,128)(2,1)S(1)} %get-tuple-element.102), channel_id=1, source_target_pairs={{0,8},{4,12},{8,16},{12,20},{16,24},{20,28},{24,0},{28,4},{32,40},... | collective-permute-start | bytes 663560 | tf_op jit(solution)/shard_map/ppermute | solution.py:77
  208.4 15.2 %collective-permute-start.35 = (bf16[6,32,576]{2,1,0:T(8,128)(2,1)S(1)}, bf16[6,32,576]{2,1,0:T(8,128)(2,1)}, u32[]{:S(2)}, u32[]{:S(2)}) collective-permute-start(bf16[6,32,576]{2,1,0:T(8,128)(2,1)S(1)} %get-tuple-element.105), channel_id=1, source_target_pairs={{0,28},{4,24},{8,4},{12,0},{16,12},{20,8},{24,20},{28,16},{32,60},... | collective-permute-start | bytes 663560 | tf_op jit(solution)/shard_map/ppermute | solution.py:77
  209.1 19.2 %collective-permute-start.33 = (bf16[6,32,576]{2,1,0:T(8,128)(2,1)}, bf16[6,32,576]{2,1,0:T(8,128)(2,1)S(1)}, u32[]{:S(2)}, u32[]{:S(2)}) collective-permute-start(bf16[6,32,576]{2,1,0:T(8,128)(2,1)} %get-tuple-element.103), channel_id=1, source_target_pairs={{0,12},{4,8},{8,20},{12,16},{16,28},{20,24},{24,4},{28,0},{32,44},... | collective-permute-start | bytes 663560 | tf_op jit(solution)/shard_map/ppermute | solution.py:77
  210.2 23.5 %collective-permute-start.34 = (bf16[6,32,576]{2,1,0:T(8,128)(2,1)}, bf16[6,32,576]{2,1,0:T(8,128)(2,1)S(1)}, u32[]{:S(2)}, u32[]{:S(2)}) collective-permute-start(bf16[6,32,576]{2,1,0:T(8,128)(2,1)} %get-tuple-element.104), channel_id=1, source_target_pairs={{0,16},{4,20},{8,24},{12,28},{16,0},{20,4},{24,8},{28,12},{32,48},... | collective-permute-start | bytes 663560 | tf_op jit(solution)/shard_map/ppermute | solution.py:77
  211.1 24.2 %collective-permute-start.37 = (bf16[6,32,576]{2,1,0:T(8,128)(2,1)}, bf16[6,32,576]{2,1,0:T(8,128)(2,1)}, u32[]{:S(2)}, u32[]{:S(2)}) collective-permute-start(bf16[6,32,576]{2,1,0:T(8,128)(2,1)} %get-tuple-element.106), channel_id=1, source_target_pairs={{0,24},{4,28},{8,0},{12,4},{16,8},{20,12},{24,16},{28,20},{32,56},... | collective-permute-start | bytes 663560 | tf_op jit(solution)/shard_map/ppermute | solution.py:77
  223.4 16.0 %collective-permute-start.38 = (bf16[6,32,576]{2,1,0:T(8,128)(2,1)}, bf16[6,32,576]{2,1,0:T(8,128)(2,1)}, u32[]{:S(2)}, u32[]{:S(2)}) collective-permute-start(bf16[6,32,576]{2,1,0:T(8,128)(2,1)} %get-tuple-element.107), channel_id=1, source_target_pairs={{0,28},{4,24},{8,4},{12,0},{16,12},{20,8},{24,20},{28,16},{32,60},... | collective-permute-start | bytes 663560 | tf_op jit(solution)/shard_map/ppermute | solution.py:77
  223.6 21.7 %collective-permute-start.36 = (bf16[6,32,576]{2,1,0:T(8,128)(2,1)}, bf16[6,32,576]{2,1,0:T(8,128)(2,1)}, u32[]{:S(2)}, u32[]{:S(2)}) collective-permute-start(bf16[6,32,576]{2,1,0:T(8,128)(2,1)} %collective-permute-done.35), channel_id=1, source_target_pairs={{0,24},{4,28},{8,0},{12,4},{16,8},{20,12},{24,16},{28,20},{32,56},... | collective-permute-start | bytes 663560 | tf_op jit(solution)/shard_map/ppermute | solution.py:77
  251.1 18.4 %collective-permute-start.39 = (bf16[4,32,576]{2,1,0:T(8,128)(2,1)}, bf16[4,32,576]{2,1,0:T(8,128)(2,1)S(1)}, u32[]{:S(2)}, u32[]{:S(2)}) collective-permute-start(bf16[4,32,576]{2,1,0:T(8,128)(2,1)} %get-tuple-element.108), channel_id=1, source_target_pairs={{0,64},{4,68},{8,72},{12,76},{16,80},{20,84},{24,88},{28,92},{32,9... | collective-permute-start | bytes 442376 | tf_op jit(solution)/shard_map/ppermute | solution.py:39
  268.2 46.1 %collective-permute-start.43 = (bf16[4,32,576]{2,1,0:T(8,128)(2,1)S(1)}, bf16[4,32,576]{2,1,0:T(8,128)(2,1)S(1)}, u32[]{:S(2)}, u32[]{:S(2)}) collective-permute-start(bf16[4,32,576]{2,1,0:T(8,128)(2,1)S(1)} %copy-done.14), channel_id=1, source_target_pairs={{32,0},{36,4},{40,8},{44,12},{48,16},{52,20},{56,24},{60,28},{64,3... | collective-permute-start | bytes 442376 | tf_op jit(solution)/shard_map/ppermute | solution.py:39
  269.5 44.8 %collective-permute-start.42 = (bf16[4,32,576]{2,1,0:T(8,128)(2,1)S(1)}, bf16[4,32,576]{2,1,0:T(8,128)(2,1)S(1)}, u32[]{:S(2)}, u32[]{:S(2)}) collective-permute-start(bf16[4,32,576]{2,1,0:T(8,128)(2,1)S(1)} %copy-done.12), channel_id=1, source_target_pairs={{0,32},{4,36},{8,40},{12,44},{16,48},{20,52},{24,56},{28,60},{32,6... | collective-permute-start | bytes 442376 | tf_op jit(solution)/shard_map/ppermute | solution.py:39
  270.3 44.0 %collective-permute-start.45 = (bf16[4,32,576]{2,1,0:T(8,128)(2,1)S(1)}, bf16[4,32,576]{2,1,0:T(8,128)(2,1)S(1)}, u32[]{:S(2)}, u32[]{:S(2)}) collective-permute-start(bf16[4,32,576]{2,1,0:T(8,128)(2,1)S(1)} %add_convert_fusion.2), channel_id=1, source_target_pairs={{64,0},{68,4},{72,8},{76,12},{80,16},{84,20},{88,24},{92,28},{96,3... | collective-permute-start | bytes 442376 | tf_op jit(solution)/shard_map/ppermute | solution.py:39
  275.0 39.3 %collective-permute-start.44 = (bf16[4,32,576]{2,1,0:T(8,128)(2,1)S(1)}, bf16[4,32,576]{2,1,0:T(8,128)(2,1)S(1)}, u32[]{:S(2)}, u32[]{:S(2)}) collective-permute-start(bf16[4,32,576]{2,1,0:T(8,128)(2,1)S(1)} %add_convert_fusion.3), channel_id=1, source_target_pairs={{0,64},{4,68},{8,72},{12,76},{16,80},{20,84},{24,88},{28,92},{32,9... | collective-permute-start | bytes 442376 | tf_op jit(solution)/shard_map/ppermute | solution.py:39
  (52 other events, 721.0 us)

commit v3 on v1

--- a/solution.py
+++ b/solution.py
@@ -48,16 +48,19 @@
     return [own, left[1], left[2], left[3], right[4], right[3], right[2], right[1]]
 
 
-def reduce_z(terms, limit):
+def reduce_z(terms, limit, beside):
     right, left = terms[4], terms[5]
     for hop in range(4):
         right = shift_z(right, 1, lambda z: (z + 4 - hop) % Z < limit)
         if hop < 3:
+            left = shift_z(left, -1, lambda z: (z - 3 + hop) % Z < limit)
+        if hop == 0:
+            right, left, beside = lax.optimization_barrier((right, left, beside))
+        if hop < 3:
             right = narrow(wide(right) + wide(terms[3 - hop]))
-            left = shift_z(left, -1, lambda z: (z - 3 + hop) % Z < limit)
         if hop < 2:
             left = narrow(wide(left) + wide(terms[6 + hop]))
-    return wide(terms[0]) + wide(right) + wide(left)
+    return wide(terms[0]) + wide(right) + wide(left), beside
 
 
 def shift_yc(array, y_step, c_step):
@@ -70,10 +73,6 @@
     return lax.ppermute(array, "seq", pairs)
 
 
-def swap_core(array):
-    return lax.ppermute(array, "seq", [(s, s ^ 1) for s in range(Z * Y * C)])
-
-
 def shift_x(array, step):
     return lax.ppermute(array, "head", [(x, (x + step) % X) for x in range(X)])
 
@@ -85,7 +84,6 @@
 
 
 YC_GROUPS = [[seq_of(z, y, c) for y in range(Y) for c in range(C)] for z in range(Z)]
-Y_GROUPS = [[seq_of(z, y, c) for y in range(Y)] for z in range(Z) for c in range(C)]
 Z_GROUPS = [[seq_of(z, y, c) for z in range(Z)] for y in range(Y) for c in range(C)]
 
 
@@ -436,16 +434,13 @@
         )
     )
     v_dim = terms.shape[-1]
-    terms = terms.reshape(Y, C, -1, v_dim)
-    arrived = swap_core(lax.dynamic_index_in_dim(terms, 1 - c, 1, keepdims=False))
-    terms = lax.dynamic_index_in_dim(terms, c, 1, keepdims=False)
-    terms = narrow(wide(terms) + wide(arrived))
-    terms = trade(terms, Y_GROUPS)
+    terms = lax.all_to_all(
+        terms.reshape(Z * peers, -1, v_dim), "seq", split_axis=0, concat_axis=0, tiled=True
+    )
     terms = narrow(jnp.sum(wide(terms), axis=0))
-    terms = trade(terms.reshape(Z, -1, v_dim), Z_GROUPS)
-    terms = narrow(jnp.sum(wide(terms), axis=0))
-    terms = trade(jnp.broadcast_to(terms, (Z, *terms.shape)), Z_GROUPS).reshape(-1, v_dim)
+    terms = trade(jnp.broadcast_to(terms, (Z, *terms.shape)), Z_GROUPS)
     terms = trade(jnp.broadcast_to(terms, (peers, *terms.shape)), YC_GROUPS)
+    terms = jnp.swapaxes(terms, 0, 1)
     d_value_weight = terms.reshape(value_weight.shape)
 
     *back, own_share = send_back(
@@ -467,9 +462,9 @@
             )
         )
     d_query = jnp.transpose(d_query.reshape(query.shape), (1, 2, 0))
-    received, d_query = lax.optimization_barrier((received, d_query))
     by_z = by_owner(at_owner, received, block_count)
-    d_cache = reduce_z(by_z, Z_FULL) + wide(jnp.stack(own_back))
+    d_cache, d_query = reduce_z(by_z, Z_FULL, d_query)
+    d_cache = d_cache + wide(jnp.stack(own_back))
     return jnp.transpose(d_query, (2, 0, 1)), d_cache, d_value_weight
 
 

time: 294 us -> 317 us (1.078)
  waiting for transfers between devices: 98.6 us -> 126 us
  other arithmetic: 12 us -> 7.04 us
  starting transfers between devices: 118 us -> 114 us
  local copies, waits for them, and re-layouts: 30.4 us -> 33.6 us
    all_to_all x0 -> x1, waiting for transfers between devices: none -> 39.5 us  [local(): lax.all_to_all(terms.reshape(Z * peers, -1, v_dim), 'seq', split_axis=0,...]
    all_to_all x6 -> x4, waiting for transfers between devices: 27.1 us -> 10.3 us  [trade(): lax.all_to_all(blocks, 'seq', split_axis=0, concat_axis=0, axis_index_gro...]
    all_to_all x0 -> x1, starting transfers between devices: none -> 13.8 us  [local(): lax.all_to_all(terms.reshape(Z * peers, -1, v_dim), 'seq', split_axis=0,...]
    all_to_all x6 -> x4, starting transfers between devices: 35.4 us -> 22 us  [trade(): lax.all_to_all(blocks, 'seq', split_axis=0, concat_axis=0, axis_index_gro...]
    ppermute x12, waiting for transfers between devices: 21.2 us -> 26.9 us  [shift_x(): return lax.ppermute(array, 'head', [(x, (x + step) % X) for x in range(X)])]
    ppermute x7, waiting for transfers between devices: 28.3 us -> 32.6 us  [shift_yc(): return lax.ppermute(array, 'seq', pairs)]
    convert_element_type x8 -> x7, other arithmetic: 5.86 us -> 2.12 us  [narrow(): return array.astype(BF16)]
    unnamed x62 -> x91, local copies, waits for them, and re-layouts: 16.6 us -> 16.3 us
  transfers between devices with their start and end apart: 48 -> 46, of which waited for: 18 -> 16; matrix products, arithmetic and copies ran while one was open for 10% -> 9% of each run, Pallas kernels for 1% -> 1%
where the time goes in v3:
time: 317 us; the launch traced here: 315 us
  waiting for transfers between devices  126 us (40%)
  starting transfers between devices  114 us (36%)
  local copies, waits for them, and re-layouts  33.6 us (11%)
  Pallas kernels  24.3 us (8%)
  matrix products  8.95 us (3%)
  other arithmetic  7.04 us (2%)
    all_to_all x1, waiting for transfers between devices, local(): lax.all_to_all(terms.reshape(Z * peers, -1, v_dim), 'seq', split_axis=0,...  39.5 us
    ppermute x7, waiting for transfers between devices, shift_yc(): return lax.ppermute(array, 'seq', pairs)  32.6 us
    ppermute x14, starting transfers between devices, shift_z(): return lax.ppermute(array, 'seq', pairs)  29.1 us
    ppermute x12, waiting for transfers between devices, shift_x(): return lax.ppermute(array, 'head', [(x, (x + step) % X) for x in range(X)])  26.9 us
    all_to_all x4, starting transfers between devices, trade(): lax.all_to_all(blocks, 'seq', split_axis=0, concat_axis=0, axis_index_gro...  22 us
    ppermute x4, starting transfers between devices, local(): lax.ppermute(own_share, 'seq', [((o - FIRST_OWN_OWNER) * block_count + j,...  16.9 us
    unnamed x91, local copies, waits for them, and re-layouts  16.3 us
    pallas_call x1, Pallas kernels, attend(): pl.pallas_call(attend_kernel, grid_spec=pltpu.PrefetchScalarGridSpec(num_...  14.6 us
  transfers between devices with their start and end apart: 46, of which 16 were waited for; matrix products, arithmetic and copies ran while one was open for 9% of the time, Pallas kernels for 1%

profile of v3, /device:TPU:193, one launch (start us, length us, event | category | flops | bytes accessed | tf_op | source)
XLA Modules:
  0.0 315.2 jit_solution(16213854573953316542)
XLA Ops:
  6.1 3.1 collective-permute-done.3.refs_7_
  12.5 2.8 collective-permute-done.4.refs_6_
  17.6 3.6 %collective-permute-start.2 = (bf16[4,32,576]{2,1,0:T(8,128)(2,1)S(1)}, bf16[4,32,576]{2,1,0:T(8,128)(2,1)S(1)}, u32[]{:S(2)}, u32[]{:S(2)}) collective-permute-start(bf16[4,32,576]{2,1,0:T(8,128)(2,1)S(1)} %collective-permute-done.1.refs_2_), channel_id=1, source_target_pairs={{0,224},{4,228},{8,232},{12,236},{16,240},{20,244},{24,248},{28,25... | collective-permute-start | bytes 442376 | tf_op jit(solution)/shard_map/ppermute | solution.py:39
  24.5 7.8 %all-to-all-start = ((s32[8,1,6]{2,1,0:T(1,128)}), s32[8,1,6]{2,1,0:T(1,128)S(1)}, u32[]{:S(2)}, u32[]{:S(2)}) async-start(s32[8,1,6]{2,1,0:T(1,128)} %bitcast), calls=%async_computation | async-start | bytes 8192 | tf_op jit(solution)/shard_map/all_to_all | solution.py:81
  32.4 4.6 %all-to-all-done = s32[8,1,6]{2,1,0:T(1,128)S(1)} async-done(((s32[8,1,6]{2,1,0:T(1,128)}), s32[8,1,6]{2,1,0:T(1,128)S(1)}, u32[]{:S(2)}, u32[]{:S(2)}) %all-to-all-start) | async-done | bytes 224 | tf_op jit(solution)/shard_map/all_to_all | solution.py:81
  38.3 2.9 pack.1
  41.3 5.1 %all-to-all-start.1 = ((bf16[8,6,32,576]{3,2,1,0:T(8,128)(2,1)}), bf16[8,6,32,576]{3,2,1,0:T(8,128)(2,1)}, u32[]{:S(2)}, u32[]{:S(2)}) async-start(bf16[8,6,32,576]{3,2,1,0:T(8,128)(2,1)} %bitcast.29), calls=%async_computation.1 | async-start | bytes 3932160 | tf_op jit(solution)/shard_map/all_to_all | solution.py:81
  46.3 5.4 %collective-permute-start.10 = (bf16[32,576]{1,0:T(8,128)(2,1)S(1)}, bf16[32,576]{1,0:T(8,128)(2,1)S(1)}, u32[]{:S(2)}, u32[]{:S(2)}) collective-permute-start(bf16[32,576]{1,0:T(8,128)(2,1)S(1)} %get-tuple-element.78), channel_id=1, source_target_pairs={{192,12},{196,28},{200,44},{204,60},{208,76},{212,92},{216,108},{2... | collective-permute-start | bytes 110600 | tf_op jit(solution)/shard_map/ppermute | solution.py:384
  58.4 4.1 %copy.45 = bf16[128,16,512]{2,1,0:T(8,128)(2,1)} copy(bf16[128,16,512]{2,0,1:T(8,128)(2,1)} %convert_bitcast_fusion) | data formatting | bytes 4194304 | tf_op jit(solution)/shard_map/convert_element_type | solution.py:91
  62.4 4.9 %copy.46 = bf16[128,16,576]{2,1,0:T(8,128)(2,1)} copy(bf16[128,16,576]{0,2,1:T(8,128)(2,1)} %param.5) | data formatting | bytes 4718592 | tf_op args[0]
  67.3 5.7 %all-to-all-done.1 = bf16[8,6,32,576]{3,2,1,0:T(8,128)(2,1)} async-done(((bf16[8,6,32,576]{3,2,1,0:T(8,128)(2,1)}), bf16[8,6,32,576]{3,2,1,0:T(8,128)(2,1)}, u32[]{:S(2)}, u32[]{:S(2)}) %all-to-all-start.1) | async-done | bytes 1769504 | tf_op jit(solution)/shard_map/all_to_all | solution.py:81
  80.1 4.9 %collective-permute-done.11.refs_1_.refs_5_ = bf16[7,32,576]{2,1,0:T(8,128)(2,1)S(1)} collective-permute-done((bf16[7,32,576]{2,1,0:T(8,128)(2,1)}, bf16[7,32,576]{2,1,0:T(8,128)(2,1)S(1)}, u32[]{:S(2)}, u32[]{:S(2)}) %collective-permute-start.11) | collective-permute-done | bytes 258080 | tf_op jit(solution)/shard_map/ppermute | solution.py:77
  88.0 10.1 %collective-permute-done.14.refs_9_ = bf16[6,32,576]{2,1,0:T(8,128)(2,1)S(1)} collective-permute-done((bf16[6,32,576]{2,1,0:T(8,128)(2,1)}, bf16[6,32,576]{2,1,0:T(8,128)(2,1)S(1)}, u32[]{:S(2)}, u32[]{:S(2)}) %collective-permute-start.14) | collective-permute-done | bytes 221216 | tf_op jit(solution)/shard_map/ppermute | solution.py:77
  99.1 14.6 %attend.1 = (bf16[2048,576]{1,0:T(8,128)(2,1)}, bf16[2048,512]{1,0:T(8,128)(2,1)}, bf16[7,32,576]{2,1,0:T(8,128)(2,1)}, bf16[7,32,576]{2,1,0:T(8,128)(2,1)}, bf1...) custom-call(s32[1]{0:T(128)} %bitcast.2.x_ref, ...), custom_call_target="tpu_custom_call" | custom-call | tf_op jit(solution)/shard_map/attend/pallas_call | solution.py:249
  113.7 5.4 %fusion.2 = bf16[16,512,128]{2,1,0:T(8,128)(2,1)} fusion(bf16[128,16,512]{2,1,0:T(8,128)(2,1)} %bitcast.31, bf16[128,16,128]{2,1,0:T(8,128)(2,1)S(1)} %copy-done.22), kind=kOutput, calls=%fused_computation.3 | convolution fusion | flops 269484032 | bytes 4718592 | tf_op jit(solution)/shard_map/qhc,qhv->hcv/dot_general | solution.py:429
  119.0 13.8 %all-to-all-start.2 = ((bf16[64,128,128]{2,1,0:T(8,128)(2,1)}), bf16[64,128,128]{2,1,0:T(8,128)(2,1)}, u32[]{:S(2)}, u32[]{:S(2)}) async-start(bf16[64,128,128]{2,1,0:T(8,128)(2,1)} %bitcast.27), calls=%async_computation.2 | async-start | bytes 4194304 | tf_op jit(solution)/shard_map/all_to_all | solution.py:437
  136.0 5.1 %collective-permute-done.18 = bf16[7,32,576]{2,1,0:T(8,128)(2,1)S(1)} collective-permute-done((bf16[7,32,576]{2,1,0:T(8,128)(2,1)S(1)}, bf16[7,32,576]{2,1,0:T(8,128)(2,1)S(1)}, u32[]{:S(2)}, u32[]{:S(2)}) %collective-permute-start.18) | collective-permute-done | bytes 258080 | tf_op jit(solution)/shard_map/ppermute | solution.py:77
  143.1 39.5 %all-to-all-done.2 = bf16[64,128,128]{2,1,0:T(8,128)(2,1)} async-done(((bf16[64,128,128]{2,1,0:T(8,128)(2,1)}), bf16[64,128,128]{2,1,0:T(8,128)(2,1)}, u32[]{:S(2)}, u32[]{:S(2)}) %all-to-all-start.2) | async-done | bytes 2097184 | tf_op jit(solution)/shard_map/all_to_all | solution.py:437
  185.2 4.8 %all-to-all-start.3 = ((bf16[8,128,128]{2,1,0:T(8,128)(2,1)}), bf16[8,128,128]{2,1,0:T(8,128)(2,1)}, u32[]{:S(2)}, u32[]{:S(2)}) async-start(bf16[8,128,128]{2,1,0:T(8,128)(2,1)} %broadcast_in_dim.77), calls=%async_computation.3 | async-start | bytes 524288 | tf_op jit(solution)/shard_map/all_to_all | solution.py:81
  192.1 6.8 %collective-permute-done.22.refs_5_ = bf16[6,32,576]{2,1,0:T(8,128)(2,1)S(1)} collective-permute-done((bf16[6,32,576]{2,1,0:T(8,128)(2,1)S(1)}, bf16[6,32,576]{2,1,0:T(8,128)(2,1)S(1)}, u32[]{:S(2)}, u32[]{:S(2)}) %collective-permute-start.22) | collective-permute-done | bytes 221216 | tf_op jit(solution)/shard_map/ppermute | solution.py:77
  212.5 2.8 broadcast_in_dim.78
  215.3 4.3 %all-to-all-start.4 = ((bf16[8,8,128,128]{3,2,1,0:T(8,128)(2,1)}), bf16[8,8,128,128]{3,2,1,0:T(8,128)(2,1)}, u32[]{:S(2)}, u32[]{:S(2)}) async-start(bf16[8,8,128,128]{3,2,1,0:T(8,128)(2,1)} %broadcast_in_dim.78), calls=%async_computation.4 | async-start | bytes 4194304 | tf_op jit(solution)/shard_map/all_to_all | solution.py:81
  223.5 3.2 %collective-permute-done.26.refs_4_ = bf16[6,32,576]{2,1,0:T(8,128)(2,1)S(1)} collective-permute-done((bf16[6,32,576]{2,1,0:T(8,128)(2,1)}, bf16[6,32,576]{2,1,0:T(8,128)(2,1)S(1)}, u32[]{:S(2)}, u32[]{:S(2)}) %collective-permute-start.26) | collective-permute-done | bytes 221216 | tf_op jit(solution)/shard_map/ppermute | solution.py:73
  226.7 6.3 %collective-permute-done.27.refs_5_ = bf16[6,32,576]{2,1,0:T(8,128)(2,1)} collective-permute-done((bf16[6,32,576]{2,1,0:T(8,128)(2,1)}, bf16[6,32,576]{2,1,0:T(8,128)(2,1)}, u32[]{:S(2)}, u32[]{:S(2)}) %collective-permute-start.27) | collective-permute-done | bytes 221216 | tf_op jit(solution)/shard_map/ppermute | solution.py:73
  233.0 17.4 %collective-permute-done.28.refs_6_ = bf16[6,32,576]{2,1,0:T(8,128)(2,1)} collective-permute-done((bf16[6,32,576]{2,1,0:T(8,128)(2,1)}, bf16[6,32,576]{2,1,0:T(8,128)(2,1)}, u32[]{:S(2)}, u32[]{:S(2)}) %collective-permute-start.28) | collective-permute-done | bytes 221216 | tf_op jit(solution)/shard_map/ppermute | solution.py:73
  250.4 5.7 %collective-permute-done.29.refs_7_ = bf16[6,32,576]{2,1,0:T(8,128)(2,1)} collective-permute-done((bf16[6,32,576]{2,1,0:T(8,128)(2,1)}, bf16[6,32,576]{2,1,0:T(8,128)(2,1)}, u32[]{:S(2)}, u32[]{:S(2)}) %collective-permute-start.29) | collective-permute-done | bytes 221216 | tf_op jit(solution)/shard_map/ppermute | solution.py:73
  264.8 3.1 collective-permute-start.31
  267.9 4.8 %copy.47 = bf16[128,16,576]{0,2,1:T(8,128)(2,1)} copy(bf16[128,16,576]{2,1,0:T(8,128)(2,1)} %bitcast.30) | data formatting | bytes 4718592 | tf_op jit(solution)/shard_map/reshape | solution.py:464
  272.8 2.7 collective-permute-start.32
  288.3 13.0 %collective-permute-start.38 = (bf16[32,576]{1,0:T(8,128)(2,1)S(1)}, bf16[32,576]{1,0:T(8,128)(2,1)S(1)}, u32[]{:S(2)}, u32[]{:S(2)}) collective-permute-start(bf16[32,576]{1,0:T(8,128)(2,1)S(1)} %get-tuple-element.71), channel_id=1, source_target_pairs={{4,192},{20,196},{36,200},{52,204},{68,208},{84,212},{100,216},{11... | collective-permute-start | bytes 110600 | tf_op jit(solution)/shard_map/ppermute | solution.py:455
  302.7 8.5 %collective-permute-done.37 = bf16[32,576]{1,0:T(8,128)(2,1)S(1)} collective-permute-done((bf16[32,576]{1,0:T(8,128)(2,1)S(1)}, bf16[32,576]{1,0:T(8,128)(2,1)S(1)}, u32[]{:S(2)}, u32[]{:S(2)}) %collective-permute-start.37) | collective-permute-done | bytes 36896 | tf_op jit(solution)/shard_map/ppermute | solution.py:455
  312.0 3.2 %copy.50 = bf16[8,8,128,128]{3,2,0,1:T(8,128)(2,1)} copy(bf16[8,8,128,128]{3,2,1,0:T(8,128)(2,1)} %all-to-all-done.4) | data formatting | bytes 4194304 | tf_op jit(solution)/shard_map/all_to_all | solution.py:81
  (195 shorter events, 84.1 us)
Async XLA Ops:
  17.6 20.0 %collective-permute-start.2 = (bf16[4,32,576]{2,1,0:T(8,128)(2,1)S(1)}, bf16[4,32,576]{2,1,0:T(8,128)(2,1)S(1)}, u32[]{:S(2)}, u32[]{:S(2)}) collective-permute-start(bf16[4,32,576]{2,1,0:T(8,128)(2,1)S(1)} %collective-permute-done.1.refs_2_), channel_id=1, source_target_pairs={{0,224},{4,228},{8,232},{12,236},{16,240},{20,244},{24,248},{28,25... | collective-permute-start | bytes 442376 | tf_op jit(solution)/shard_map/ppermute | solution.py:39
  21.9 15.7 %collective-permute-start.6 = (bf16[4,32,576]{2,1,0:T(8,128)(2,1)S(1)}, bf16[4,32,576]{2,1,0:T(8,128)(2,1)S(1)}, u32[]{:S(2)}, u32[]{:S(2)}) collective-permute-start(bf16[4,32,576]{2,1,0:T(8,128)(2,1)S(1)} %collective-permute-done.5.refs_5_), channel_id=1, source_target_pairs={{0,32},{4,36},{8,40},{12,44},{16,48},{20,52},{24,56},{28,60},{96,1... | collective-permute-start | bytes 442376 | tf_op jit(solution)/shard_map/ppermute | solution.py:39
  24.5 12.4 %all-to-all-start = ((s32[8,1,6]{2,1,0:T(1,128)}), s32[8,1,6]{2,1,0:T(1,128)S(1)}, u32[]{:S(2)}, u32[]{:S(2)}) async-start(s32[8,1,6]{2,1,0:T(1,128)} %bitcast), calls=%async_computation | async-start | bytes 8192 | tf_op jit(solution)/shard_map/all_to_all | solution.py:81
  41.3 31.8 %all-to-all-start.1 = ((bf16[8,6,32,576]{3,2,1,0:T(8,128)(2,1)}), bf16[8,6,32,576]{3,2,1,0:T(8,128)(2,1)}, u32[]{:S(2)}, u32[]{:S(2)}) async-start(bf16[8,6,32,576]{3,2,1,0:T(8,128)(2,1)} %bitcast.29), calls=%async_computation.1 | async-start | bytes 3932160 | tf_op jit(solution)/shard_map/all_to_all | solution.py:81
  46.3 26.7 %collective-permute-start.10 = (bf16[32,576]{1,0:T(8,128)(2,1)S(1)}, bf16[32,576]{1,0:T(8,128)(2,1)S(1)}, u32[]{:S(2)}, u32[]{:S(2)}) collective-permute-start(bf16[32,576]{1,0:T(8,128)(2,1)S(1)} %get-tuple-element.78), channel_id=1, source_target_pairs={{192,12},{196,28},{200,44},{204,60},{208,76},{212,92},{216,108},{2... | collective-permute-start | bytes 110600 | tf_op jit(solution)/shard_map/ppermute | solution.py:384
  51.8 21.2 %collective-permute-start.9 = (bf16[32,576]{1,0:T(8,128)(2,1)S(1)}, bf16[32,576]{1,0:T(8,128)(2,1)S(1)}, u32[]{:S(2)}, u32[]{:S(2)}) collective-permute-start(bf16[32,576]{1,0:T(8,128)(2,1)S(1)} %get-tuple-element.79), channel_id=1, source_target_pairs={{192,8},{196,24},{200,40},{204,56},{208,72},{212,88},{216,104},{22... | collective-permute-start | bytes 110600 | tf_op jit(solution)/shard_map/ppermute | solution.py:384
  53.1 20.0 %collective-permute-start.8 = (bf16[32,576]{1,0:T(8,128)(2,1)S(1)}, bf16[32,576]{1,0:T(8,128)(2,1)S(1)}, u32[]{:S(2)}, u32[]{:S(2)}) collective-permute-start(bf16[32,576]{1,0:T(8,128)(2,1)S(1)} %get-tuple-element.80), channel_id=1, source_target_pairs={{192,4},{196,20},{200,36},{204,52},{208,68},{212,84},{216,100},{22... | collective-permute-start | bytes 110600 | tf_op jit(solution)/shard_map/ppermute | solution.py:384
  55.0 18.1 %collective-permute-start.7 = (bf16[32,576]{1,0:T(8,128)(2,1)S(1)}, bf16[32,576]{1,0:T(8,128)(2,1)S(1)}, u32[]{:S(2)}, u32[]{:S(2)}) collective-permute-start(bf16[32,576]{1,0:T(8,128)(2,1)S(1)} %get-tuple-element.81), channel_id=1, source_target_pairs={{192,0},{196,16},{200,32},{204,48},{208,64},{212,80},{216,96},{220... | collective-permute-start | bytes 110600 | tf_op jit(solution)/shard_map/ppermute | solution.py:384
  78.8 19.2 %collective-permute-start.13 = (bf16[7,32,576]{2,1,0:T(8,128)(2,1)}, bf16[7,32,576]{2,1,0:T(8,128)(2,1)S(1)}, u32[]{:S(2)}, u32[]{:S(2)}) collective-permute-start(bf16[7,32,576]{2,1,0:T(8,128)(2,1)} %get-tuple-element.41.refs_0_.refs_4_), channel_id=1, source_target_pairs={{0,3},{1,0},{2,1},{3,2},{4,7},{5,4},{6,5},{7,6},{8,11},{9,8},{10,9... | collective-permute-start | bytes 774152 | tf_op jit(solution)/shard_map/ppermute | solution.py:77
  85.0 13.1 %collective-permute-start.12 = (bf16[7,32,576]{2,1,0:T(8,128)(2,1)S(1)}, bf16[7,32,576]{2,1,0:T(8,128)(2,1)S(1)}, u32[]{:S(2)}, u32[]{:S(2)}) collective-permute-start(bf16[7,32,576]{2,1,0:T(8,128)(2,1)S(1)} %collective-permute-done.11.refs_1_.refs_5_), channel_id=1, source_target_pairs={{0,1},{1,2},{2,3},{3,0},{4,5},{5,6},{6,7},{7,4},{8,9},{9,10},{10,1... | collective-permute-start | bytes 774152 | tf_op jit(solution)/shard_map/ppermute | solution.py:77
  85.0 13.0 %collective-permute-start.14 = (bf16[6,32,576]{2,1,0:T(8,128)(2,1)}, bf16[6,32,576]{2,1,0:T(8,128)(2,1)S(1)}, u32[]{:S(2)}, u32[]{:S(2)}) collective-permute-start(bf16[6,32,576]{2,1,0:T(8,128)(2,1)} %get-tuple-element.42.refs_8_), channel_id=1, source_target_pairs={{0,1},{1,2},{2,3},{3,0},{4,5},{5,6},{6,7},{7,4},{8,9},{9,10},{10,1... | collective-permute-start | bytes 663560 | tf_op jit(solution)/shard_map/ppermute | solution.py:77
  86.2 11.8 %collective-permute-start.16 = (bf16[6,32,576]{2,1,0:T(8,128)(2,1)S(1)}, bf16[6,32,576]{2,1,0:T(8,128)(2,1)S(1)}, u32[]{:S(2)}, u32[]{:S(2)}) collective-permute-start(bf16[6,32,576]{2,1,0:T(8,128)(2,1)S(1)} %collective-permute-done.15.refs_11_), channel_id=1, source_target_pairs={{0,3},{1,0},{2,1},{3,2},{4,7},{5,4},{6,5},{7,6},{8,11},{9,8},{10,9... | collective-permute-start | bytes 663560 | tf_op jit(solution)/shard_map/ppermute | solution.py:77
  119.0 63.6 %all-to-all-start.2 = ((bf16[64,128,128]{2,1,0:T(8,128)(2,1)}), bf16[64,128,128]{2,1,0:T(8,128)(2,1)}, u32[]{:S(2)}, u32[]{:S(2)}) async-start(bf16[64,128,128]{2,1,0:T(8,128)(2,1)} %bitcast.27), calls=%async_computation.2 | async-start | bytes 4194304 | tf_op jit(solution)/shard_map/all_to_all | solution.py:437
  133.0 58.3 %collective-permute-start.20 = (bf16[6,32,576]{2,1,0:T(8,128)(2,1)}, bf16[6,32,576]{2,1,0:T(8,128)(2,1)S(1)}, u32[]{:S(2)}, u32[]{:S(2)}) collective-permute-start(bf16[6,32,576]{2,1,0:T(8,128)(2,1)} %get-tuple-element.48), channel_id=1, source_target_pairs={{0,3},{1,0},{2,1},{3,2},{4,7},{5,4},{6,5},{7,6},{8,11},{9,8},{10,9... | collective-permute-start | bytes 663560 | tf_op jit(solution)/shard_map/ppermute | solution.py:77
  133.7 56.4 %collective-permute-start.21 = (bf16[6,32,576]{2,1,0:T(8,128)(2,1)}, bf16[6,32,576]{2,1,0:T(8,128)(2,1)}, u32[]{:S(2)}, u32[]{:S(2)}) collective-permute-start(bf16[6,32,576]{2,1,0:T(8,128)(2,1)} %get-tuple-element.49), channel_id=1, source_target_pairs={{0,1},{1,2},{2,3},{3,0},{4,5},{5,6},{6,7},{7,4},{8,9},{9,10},{10,1... | collective-permute-start | bytes 663560 | tf_op jit(solution)/shard_map/ppermute | solution.py:77
  134.6 57.5 %collective-permute-start.17 = (bf16[7,32,576]{2,1,0:T(8,128)(2,1)}, bf16[7,32,576]{2,1,0:T(8,128)(2,1)S(1)}, u32[]{:S(2)}, u32[]{:S(2)}) collective-permute-start(bf16[7,32,576]{2,1,0:T(8,128)(2,1)} %get-tuple-element.44), channel_id=1, source_target_pairs={{0,1},{1,2},{2,3},{3,0},{4,5},{5,6},{6,7},{7,4},{8,9},{9,10},{10,1... | collective-permute-start | bytes 774152 | tf_op jit(solution)/shard_map/ppermute | solution.py:77
  141.9 57.0 %collective-permute-start.19 = (bf16[7,32,576]{2,1,0:T(8,128)(2,1)}, bf16[7,32,576]{2,1,0:T(8,128)(2,1)S(1)}, u32[]{:S(2)}, u32[]{:S(2)}) collective-permute-start(bf16[7,32,576]{2,1,0:T(8,128)(2,1)} %add_convert_fusion), channel_id=1, source_target_pairs={{0,3},{1,0},{2,1},{3,2},{4,7},{5,4},{6,5},{7,6},{8,11},{9,8},{10,9... | collective-permute-start | bytes 774152 | tf_op jit(solution)/shard_map/ppermute | solution.py:77
  185.2 27.3 %all-to-all-start.3 = ((bf16[8,128,128]{2,1,0:T(8,128)(2,1)}), bf16[8,128,128]{2,1,0:T(8,128)(2,1)}, u32[]{:S(2)}, u32[]{:S(2)}) async-start(bf16[8,128,128]{2,1,0:T(8,128)(2,1)} %broadcast_in_dim.77), calls=%async_computation.3 | async-start | bytes 524288 | tf_op jit(solution)/shard_map/all_to_all | solution.py:81
  205.1 14.5 %collective-permute-start.23 = (bf16[6,32,576]{2,1,0:T(8,128)(2,1)}, bf16[6,32,576]{2,1,0:T(8,128)(2,1)S(1)}, u32[]{:S(2)}, u32[]{:S(2)}) collective-permute-start(bf16[6,32,576]{2,1,0:T(8,128)(2,1)} %get-tuple-element.52), channel_id=1, source_target_pairs={{0,4},{4,0},{8,12},{12,8},{16,20},{20,16},{24,28},{28,24},{32,36},... | collective-permute-start | bytes 663560 | tf_op jit(solution)/shard_map/ppermute | solution.py:73
  207.2 15.0 %collective-permute-start.24 = (bf16[6,32,576]{2,1,0:T(8,128)(2,1)}, bf16[6,32,576]{2,1,0:T(8,128)(2,1)S(1)}, u32[]{:S(2)}, u32[]{:S(2)}) collective-permute-start(bf16[6,32,576]{2,1,0:T(8,128)(2,1)} %get-tuple-element.53), channel_id=1, source_target_pairs={{0,8},{4,12},{8,16},{12,20},{16,24},{20,28},{24,0},{28,4},{32,40},... | collective-permute-start | bytes 663560 | tf_op jit(solution)/shard_map/ppermute | solution.py:73
  207.7 15.8 %collective-permute-start.25 = (bf16[6,32,576]{2,1,0:T(8,128)(2,1)}, bf16[6,32,576]{2,1,0:T(8,128)(2,1)S(1)}, u32[]{:S(2)}, u32[]{:S(2)}) collective-permute-start(bf16[6,32,576]{2,1,0:T(8,128)(2,1)} %copy-done.21), channel_id=1, source_target_pairs={{0,12},{4,8},{8,20},{12,16},{16,28},{20,24},{24,4},{28,0},{32,44},... | collective-permute-start | bytes 663560 | tf_op jit(solution)/shard_map/ppermute | solution.py:73
  209.2 17.5 %collective-permute-start.26 = (bf16[6,32,576]{2,1,0:T(8,128)(2,1)}, bf16[6,32,576]{2,1,0:T(8,128)(2,1)S(1)}, u32[]{:S(2)}, u32[]{:S(2)}) collective-permute-start(bf16[6,32,576]{2,1,0:T(8,128)(2,1)} %copy-done.20), channel_id=1, source_target_pairs={{0,16},{4,20},{8,24},{12,28},{16,0},{20,4},{24,8},{28,12},{32,48},... | collective-permute-start | bytes 663560 | tf_op jit(solution)/shard_map/ppermute | solution.py:73
  211.5 21.5 %collective-permute-start.27 = (bf16[6,32,576]{2,1,0:T(8,128)(2,1)}, bf16[6,32,576]{2,1,0:T(8,128)(2,1)}, u32[]{:S(2)}, u32[]{:S(2)}) collective-permute-start(bf16[6,32,576]{2,1,0:T(8,128)(2,1)} %copy-done.19), channel_id=1, source_target_pairs={{0,20},{4,16},{8,28},{12,24},{16,4},{20,0},{24,12},{28,8},{32,52},... | collective-permute-start | bytes 663560 | tf_op jit(solution)/shard_map/ppermute | solution.py:73
  215.3 96.7 %all-to-all-start.4 = ((bf16[8,8,128,128]{3,2,1,0:T(8,128)(2,1)}), bf16[8,8,128,128]{3,2,1,0:T(8,128)(2,1)}, u32[]{:S(2)}, u32[]{:S(2)}) async-start(bf16[8,8,128,128]{3,2,1,0:T(8,128)(2,1)} %broadcast_in_dim.78), calls=%async_computation.4 | async-start | bytes 4194304 | tf_op jit(solution)/shard_map/all_to_all | solution.py:81
  219.6 30.8 %collective-permute-start.28 = (bf16[6,32,576]{2,1,0:T(8,128)(2,1)}, bf16[6,32,576]{2,1,0:T(8,128)(2,1)}, u32[]{:S(2)}, u32[]{:S(2)}) collective-permute-start(bf16[6,32,576]{2,1,0:T(8,128)(2,1)} %copy-done.18), channel_id=1, source_target_pairs={{0,24},{4,28},{8,0},{12,4},{16,8},{20,12},{24,16},{28,20},{32,56},... | collective-permute-start | bytes 663560 | tf_op jit(solution)/shard_map/ppermute | solution.py:73
  222.1 34.0 %collective-permute-start.29 = (bf16[6,32,576]{2,1,0:T(8,128)(2,1)}, bf16[6,32,576]{2,1,0:T(8,128)(2,1)}, u32[]{:S(2)}, u32[]{:S(2)}) collective-permute-start(bf16[6,32,576]{2,1,0:T(8,128)(2,1)} %copy-done.17), channel_id=1, source_target_pairs={{0,28},{4,24},{8,4},{12,0},{16,12},{20,8},{24,20},{28,16},{32,60},... | collective-permute-start | bytes 663560 | tf_op jit(solution)/shard_map/ppermute | solution.py:73
  262.6 10.1 %collective-permute-start.30 = (bf16[4,32,576]{2,1,0:T(8,128)(2,1)}, bf16[4,32,576]{2,1,0:T(8,128)(2,1)S(1)}, u32[]{:S(2)}, u32[]{:S(2)}) collective-permute-start(bf16[4,32,576]{2,1,0:T(8,128)(2,1)} %get-tuple-element.59), channel_id=1, source_target_pairs={{0,32},{4,36},{8,40},{12,44},{16,48},{20,52},{24,56},{28,60},{32,6... | collective-permute-start | bytes 442376 | tf_op jit(solution)/shard_map/ppermute | solution.py:39
  282.3 28.9 %collective-permute-start.36 = (bf16[4,32,576]{2,1,0:T(8,128)(2,1)S(1)}, bf16[4,32,576]{2,1,0:T(8,128)(2,1)S(1)}, u32[]{:S(2)}, u32[]{:S(2)}) collective-permute-start(bf16[4,32,576]{2,1,0:T(8,128)(2,1)S(1)} %add_convert_fusion.2), channel_id=1, source_target_pairs={{32,0},{36,4},{40,8},{44,12},{48,16},{52,20},{56,24},{60,28},{64,3... | collective-permute-start | bytes 442376 | tf_op jit(solution)/shard_map/ppermute | solution.py:39
  285.1 26.2 %collective-permute-start.34 = (bf16[4,32,576]{2,1,0:T(8,128)(2,1)S(1)}, bf16[4,32,576]{2,1,0:T(8,128)(2,1)S(1)}, u32[]{:S(2)}, u32[]{:S(2)}) collective-permute-start(bf16[4,32,576]{2,1,0:T(8,128)(2,1)S(1)} %add_convert_fusion.4), channel_id=1, source_target_pairs={{0,32},{4,36},{8,40},{12,44},{16,48},{20,52},{24,56},{28,60},{32,6... | collective-permute-start | bytes 442376 | tf_op jit(solution)/shard_map/ppermute | solution.py:39
  285.7 15.6 %collective-permute-start.40 = (bf16[32,576]{1,0:T(8,128)(2,1)S(1)}, bf16[32,576]{1,0:T(8,128)(2,1)S(1)}, u32[]{:S(2)}, u32[]{:S(2)}) collective-permute-start(bf16[32,576]{1,0:T(8,128)(2,1)S(1)} %get-tuple-element.71), channel_id=1, source_target_pairs={{12,192},{28,196},{44,200},{60,204},{76,208},{92,212},{108,216},{1... | collective-permute-start | bytes 110600 | tf_op jit(solution)/shard_map/ppermute | solution.py:455
  287.0 15.6 %collective-permute-start.39 = (bf16[32,576]{1,0:T(8,128)(2,1)S(1)}, bf16[32,576]{1,0:T(8,128)(2,1)S(1)}, u32[]{:S(2)}, u32[]{:S(2)}) collective-permute-start(bf16[32,576]{1,0:T(8,128)(2,1)S(1)} %get-tuple-element.71), channel_id=1, source_target_pairs={{8,192},{24,196},{40,200},{56,204},{72,208},{88,212},{104,216},{12... | collective-permute-start | bytes 110600 | tf_op jit(solution)/shard_map/ppermute | solution.py:455
  288.3 14.4 %collective-permute-start.38 = (bf16[32,576]{1,0:T(8,128)(2,1)S(1)}, bf16[32,576]{1,0:T(8,128)(2,1)S(1)}, u32[]{:S(2)}, u32[]{:S(2)}) collective-permute-start(bf16[32,576]{1,0:T(8,128)(2,1)S(1)} %get-tuple-element.71), channel_id=1, source_target_pairs={{4,192},{20,196},{36,200},{52,204},{68,208},{84,212},{100,216},{11... | collective-permute-start | bytes 110600 | tf_op jit(solution)/shard_map/ppermute | solution.py:455
  (59 other events, 638.9 us)

commit v4 on v1

--- a/solution.py
+++ b/solution.py
@@ -48,16 +48,19 @@
     return [own, left[1], left[2], left[3], right[4], right[3], right[2], right[1]]
 
 
-def reduce_z(terms, limit):
+def reduce_z(terms, limit, beside):
     right, left = terms[4], terms[5]
     for hop in range(4):
         right = shift_z(right, 1, lambda z: (z + 4 - hop) % Z < limit)
         if hop < 3:
+            left = shift_z(left, -1, lambda z: (z - 3 + hop) % Z < limit)
+        if hop == 1:
+            right, left, beside = lax.optimization_barrier((right, left, beside))
+        if hop < 3:
             right = narrow(wide(right) + wide(terms[3 - hop]))
-            left = shift_z(left, -1, lambda z: (z - 3 + hop) % Z < limit)
         if hop < 2:
             left = narrow(wide(left) + wide(terms[6 + hop]))
-    return wide(terms[0]) + wide(right) + wide(left)
+    return wide(terms[0]) + wide(right) + wide(left), beside
 
 
 def shift_yc(array, y_step, c_step):
@@ -310,34 +313,47 @@
         out_shape=[jax.ShapeDtypeStruct((Z_FULL, quarter, width), BF16)] * (Y * C)
         + [jax.ShapeDtypeStruct((quarter, width), BF16)],
         scratch_shapes=[pltpu.VMEM((Y * C * Z_FULL, quarter, width), F32)],
-        compiler_params=pltpu.CompilerParams(vmem_limit_bytes=40 * 2**20),
+        compiler_params=pltpu.CompilerParams(vmem_limit_bytes=12 * 2**20),
         name="send_back",
     )(at, *low, *high)
 
 
+FIRST_TERMS = (4, 5)
+LATER_TERMS = (0, 1, 2, 3, 6, 7)
+
+
 def by_owner_kernel(at_ref, *refs):
-    in_refs, out_refs, total = refs[: Y * C], refs[Y * C : -1], refs[-1]
+    in_refs, first_refs, later_ref, total = refs[: Y * C], refs[Y * C : -2], refs[-2], refs[-1]
     total[...] = jnp.zeros_like(total)
     for i, in_ref in enumerate(in_refs):
         for slot in range(Z_FULL):
             total[at_ref[i * Z_FULL + slot]] += wide(in_ref[slot])
-    blocks = out_refs[0].shape[0]
-    for j, out_ref in enumerate(out_refs):
+    blocks = later_ref.shape[1]
+    for j, out_ref in zip(FIRST_TERMS, first_refs):
         out_ref[...] = narrow(total[j * blocks : (j + 1) * blocks])
+    for i, j in enumerate(LATER_TERMS):
+        later_ref[i] = narrow(total[j * blocks : (j + 1) * blocks])
 
 
 def by_owner(at, received, blocks):
     _, quarter, width = received[0].shape
     vmem = pl.BlockSpec(memory_space=pltpu.VMEM)
-    return pl.pallas_call(
+    *first, later = pl.pallas_call(
         by_owner_kernel,
         in_specs=[pl.BlockSpec(memory_space=pltpu.SMEM)] + [vmem] * (Y * C),
-        out_specs=[vmem] * Z,
-        out_shape=[jax.ShapeDtypeStruct((blocks, quarter, width), BF16)] * Z,
+        out_specs=[vmem] * (len(FIRST_TERMS) + 1),
+        out_shape=[jax.ShapeDtypeStruct((blocks, quarter, width), BF16)] * len(FIRST_TERMS)
+        + [jax.ShapeDtypeStruct((len(LATER_TERMS), blocks, quarter, width), BF16)],
         scratch_shapes=[pltpu.VMEM((Z * blocks + 1, quarter, width), F32)],
-        compiler_params=pltpu.CompilerParams(vmem_limit_bytes=40 * 2**20),
+        compiler_params=pltpu.CompilerParams(vmem_limit_bytes=12 * 2**20),
         name="by_owner",
     )(at, *received)
+    terms = [None] * Z
+    for j, term in zip(FIRST_TERMS, first):
+        terms[j] = term
+    for i, j in enumerate(LATER_TERMS):
+        terms[j] = later[i]
+    return terms
 
 
 def local(query, cache, grad_out, value_weight, picked):
@@ -467,9 +483,9 @@
             )
         )
     d_query = jnp.transpose(d_query.reshape(query.shape), (1, 2, 0))
-    received, d_query = lax.optimization_barrier((received, d_query))
     by_z = by_owner(at_owner, received, block_count)
-    d_cache = reduce_z(by_z, Z_FULL) + wide(jnp.stack(own_back))
+    d_cache, d_query = reduce_z(by_z, Z_FULL, d_query)
+    d_cache = d_cache + wide(jnp.stack(own_back))
     return jnp.transpose(d_query, (2, 0, 1)), d_cache, d_value_weight
 
 

time: 294 us -> 311 us (1.058)
  waiting for transfers between devices: 98.6 us -> 108 us
  local copies, waits for them, and re-layouts: 30.4 us -> 37.3 us
    unnamed x62 -> x86, local copies, waits for them, and re-layouts: 16.6 us -> 23.5 us
    ppermute x7, waiting for transfers between devices: 28.3 us -> 34.3 us  [shift_yc(): return lax.ppermute(array, 'seq', pairs)]
    ppermute x14, waiting for transfers between devices: 11.1 us -> 15.8 us  [shift_z(): return lax.ppermute(array, 'seq', pairs)]
    convert_element_type x8 -> x6, other arithmetic: 5.86 us -> 7.5 us  [narrow(): return array.astype(BF16)]
  transfers between devices with their start and end apart: 48 -> 48, of which waited for: 18 -> 19; matrix products, arithmetic and copies ran while one was open for 10% -> 10% of each run, Pallas kernels for 1% -> 1%
where the time goes in v4:
time: 311 us; the launch traced here: 309 us
  starting transfers between devices  118 us (38%)
  waiting for transfers between devices  108 us (35%)
  local copies, waits for them, and re-layouts  37.3 us (12%)
  Pallas kernels  23.6 us (8%)
  other arithmetic  13.6 us (4%)
  matrix products  7.62 us (2%)
    all_to_all x6, starting transfers between devices, trade(): lax.all_to_all(blocks, 'seq', split_axis=0, concat_axis=0, axis_index_gro...  36.7 us
    ppermute x7, waiting for transfers between devices, shift_yc(): return lax.ppermute(array, 'seq', pairs)  34.3 us
    ppermute x14, starting transfers between devices, shift_z(): return lax.ppermute(array, 'seq', pairs)  28.1 us
    all_to_all x6, waiting for transfers between devices, trade(): lax.all_to_all(blocks, 'seq', split_axis=0, concat_axis=0, axis_index_gro...  26.3 us
    unnamed x86, local copies, waits for them, and re-layouts  23.5 us
    ppermute x12, waiting for transfers between devices, shift_x(): return lax.ppermute(array, 'head', [(x, (x + step) % X) for x in range(X)])  21 us
    ppermute x14, waiting for transfers between devices, shift_z(): return lax.ppermute(array, 'seq', pairs)  15.8 us
    ppermute x4, starting transfers between devices, local(): lax.ppermute(own_share, 'seq', [((o - FIRST_OWN_OWNER) * block_count + j,...  15.6 us
  transfers between devices with their start and end apart: 48, of which 19 were waited for; matrix products, arithmetic and copies ran while one was open for 10% of the time, Pallas kernels for 1%

profile of v4, /device:TPU:193, one launch (start us, length us, event | category | flops | bytes accessed | tf_op | source)
XLA Modules:
  0.0 309.4 jit_solution(10628661185590581874)
XLA Ops:
  6.1 5.0 %collective-permute-done.3.refs_7_ = bf16[4,32,576]{2,1,0:T(8,128)(2,1)S(1)} collective-permute-done((bf16[4,32,576]{2,1,0:T(8,128)(2,1)S(1)}, bf16[4,32,576]{2,1,0:T(8,128)(2,1)S(1)}, u32[]{:S(2)}, u32[]{:S(2)}) %collective-permute-start.3) | collective-permute-done | bytes 147488 | tf_op jit(solution)/shard_map/ppermute | solution.py:39
  19.5 3.0 collective-permute-start.2
  26.3 8.0 %all-to-all-start = ((s32[8,1,6]{2,1,0:T(1,128)}), s32[8,1,6]{2,1,0:T(1,128)S(1)}, u32[]{:S(2)}, u32[]{:S(2)}) async-start(s32[8,1,6]{2,1,0:T(1,128)} %bitcast), calls=%async_computation | async-start | bytes 8192 | tf_op jit(solution)/shard_map/all_to_all | solution.py:85
  34.3 4.6 %all-to-all-done = s32[8,1,6]{2,1,0:T(1,128)S(1)} async-done(((s32[8,1,6]{2,1,0:T(1,128)}), s32[8,1,6]{2,1,0:T(1,128)S(1)}, u32[]{:S(2)}, u32[]{:S(2)}) %all-to-all-start) | async-done | bytes 224 | tf_op jit(solution)/shard_map/all_to_all | solution.py:85
  40.3 2.9 pack.1
  43.2 5.1 %all-to-all-start.1 = ((bf16[8,6,32,576]{3,2,1,0:T(8,128)(2,1)}), bf16[8,6,32,576]{3,2,1,0:T(8,128)(2,1)}, u32[]{:S(2)}, u32[]{:S(2)}) async-start(bf16[8,6,32,576]{3,2,1,0:T(8,128)(2,1)} %bitcast.53), calls=%async_computation.1 | async-start | bytes 3932160 | tf_op jit(solution)/shard_map/all_to_all | solution.py:85
  48.3 5.2 %collective-permute-start.7 = (bf16[32,576]{1,0:T(8,128)(2,1)S(1)}, bf16[32,576]{1,0:T(8,128)(2,1)S(1)}, u32[]{:S(2)}, u32[]{:S(2)}) collective-permute-start(bf16[32,576]{1,0:T(8,128)(2,1)S(1)} %get-tuple-element.75), channel_id=1, source_target_pairs={{192,0},{196,16},{200,32},{204,48},{208,64},{212,80},{216,96},{220... | collective-permute-start | bytes 110600 | tf_op jit(solution)/shard_map/ppermute | solution.py:402
  60.1 4.1 %copy.36 = bf16[128,16,512]{2,1,0:T(8,128)(2,1)} copy(bf16[128,16,512]{2,0,1:T(8,128)(2,1)} %convert_bitcast_fusion) | data formatting | bytes 4194304 | tf_op jit(solution)/shard_map/convert_element_type | solution.py:96
  64.1 4.9 %copy.37 = bf16[128,16,576]{2,1,0:T(8,128)(2,1)} copy(bf16[128,16,576]{0,2,1:T(8,128)(2,1)} %param.5) | data formatting | bytes 4718592 | tf_op args[0]
  69.0 6.0 %all-to-all-done.1 = bf16[8,6,32,576]{3,2,1,0:T(8,128)(2,1)} async-done(((bf16[8,6,32,576]{3,2,1,0:T(8,128)(2,1)}), bf16[8,6,32,576]{3,2,1,0:T(8,128)(2,1)}, u32[]{:S(2)}, u32[]{:S(2)}) %all-to-all-start.1) | async-done | bytes 1769504 | tf_op jit(solution)/shard_map/all_to_all | solution.py:85
  82.1 4.9 %collective-permute-done.11.refs_1_.refs_5_ = bf16[7,32,576]{2,1,0:T(8,128)(2,1)S(1)} collective-permute-done((bf16[7,32,576]{2,1,0:T(8,128)(2,1)}, bf16[7,32,576]{2,1,0:T(8,128)(2,1)S(1)}, u32[]{:S(2)}, u32[]{:S(2)}) %collective-permute-start.11) | collective-permute-done | bytes 258080 | tf_op jit(solution)/shard_map/ppermute | solution.py:81
  89.9 10.2 %collective-permute-done.14.refs_9_ = bf16[6,32,576]{2,1,0:T(8,128)(2,1)} collective-permute-done((bf16[6,32,576]{2,1,0:T(8,128)(2,1)}, bf16[6,32,576]{2,1,0:T(8,128)(2,1)}, u32[]{:S(2)}, u32[]{:S(2)}) %collective-permute-start.14) | collective-permute-done | bytes 221216 | tf_op jit(solution)/shard_map/ppermute | solution.py:81
  100.8 14.6 %attend.1 = (bf16[2048,576]{1,0:T(8,128)(2,1)}, bf16[2048,512]{1,0:T(8,128)(2,1)}, bf16[7,32,576]{2,1,0:T(8,128)(2,1)}, bf16[7,32,576]{2,1,0:T(8,128)(2,1)}, bf1...) custom-call(s32[1]{0:T(128)} %bitcast.2.x_ref, ...), custom_call_target="tpu_custom_call" | custom-call | tf_op jit(solution)/shard_map/attend/pallas_call | solution.py:254
  115.4 4.0 %fusion.3 = bf16[16,512,128]{2,1,0:T(8,128)(2,1)S(1)} fusion(bf16[128,16,512]{2,1,0:T(8,128)(2,1)} %bitcast.55, bf16[128,16,128]{2,1,0:T(8,128)(2,1)S(1)} %copy-done.22), kind=kOutput, calls=%fused_computation.5 | convolution fusion | flops 269484032 | bytes 4718592 | tf_op jit(solution)/shard_map/qhc,qhv->hcv/dot_general | solution.py:447
  128.8 4.4 %all-to-all-start.2 = ((bf16[4,1024,128]{2,1,0:T(8,128)(2,1)}), bf16[4,1024,128]{2,1,0:T(8,128)(2,1)}, u32[]{:S(2)}, u32[]{:S(2)}) async-start(bf16[4,1024,128]{2,1,0:T(8,128)(2,1)} %fusion), calls=%async_computation.2 | async-start | bytes 2097152 | tf_op jit(solution)/shard_map/all_to_all | solution.py:85
  133.4 14.7 %all-to-all-done.2 = bf16[4,1024,128]{2,1,0:T(8,128)(2,1)} async-done(((bf16[4,1024,128]{2,1,0:T(8,128)(2,1)}), bf16[4,1024,128]{2,1,0:T(8,128)(2,1)}, u32[]{:S(2)}, u32[]{:S(2)}) %all-to-all-start.2) | async-done | bytes 1048608 | tf_op jit(solution)/shard_map/all_to_all | solution.py:85
  150.2 7.6 %all-to-all-start.3 = ((bf16[8,128,128]{2,1,0:T(8,128)(2,1)}), bf16[8,128,128]{2,1,0:T(8,128)(2,1)}, u32[]{:S(2)}, u32[]{:S(2)}) async-start(bf16[8,128,128]{2,1,0:T(8,128)(2,1)} %bitcast.28), calls=%async_computation.3 | async-start | bytes 524288 | tf_op jit(solution)/shard_map/all_to_all | solution.py:85
  167.8 6.1 %all-to-all-start.4 = ((bf16[8,128,128]{2,1,0:T(8,128)(2,1)}), bf16[8,128,128]{2,1,0:T(8,128)(2,1)}, u32[]{:S(2)}, u32[]{:S(2)}) async-start(bf16[8,128,128]{2,1,0:T(8,128)(2,1)} %broadcast_in_dim.77), calls=%async_computation.4 | async-start | bytes 524288 | tf_op jit(solution)/shard_map/all_to_all | solution.py:85
  176.1 5.9 %collective-permute-done.22.refs_5_ = bf16[6,32,576]{2,1,0:T(8,128)(2,1)S(1)} collective-permute-done((bf16[6,32,576]{2,1,0:T(8,128)(2,1)S(1)}, bf16[6,32,576]{2,1,0:T(8,128)(2,1)S(1)}, u32[]{:S(2)}, u32[]{:S(2)}) %collective-permute-start.22) | collective-permute-done | bytes 221216 | tf_op jit(solution)/shard_map/ppermute | solution.py:81
  184.8 3.9 %collective-permute-start.23 = (bf16[6,32,576]{2,1,0:T(8,128)(2,1)}, bf16[6,32,576]{2,1,0:T(8,128)(2,1)S(1)}, u32[]{:S(2)}, u32[]{:S(2)}) collective-permute-start(bf16[6,32,576]{2,1,0:T(8,128)(2,1)} %get-tuple-element.47), channel_id=1, source_target_pairs={{0,4},{4,0},{8,12},{12,8},{16,20},{20,16},{24,28},{28,24},{32,36},... | collective-permute-start | bytes 663560 | tf_op jit(solution)/shard_map/ppermute | solution.py:73
  191.6 5.6 %all-to-all-start.5 = ((bf16[8,1024,128]{2,1,0:T(8,128)(2,1)}), bf16[8,1024,128]{2,1,0:T(8,128)(2,1)}, u32[]{:S(2)}, u32[]{:S(2)}) async-start(bf16[8,1024,128]{2,1,0:T(8,128)(2,1)} %broadcast_in_dim.78), calls=%async_computation.5 | async-start | bytes 4194304 | tf_op jit(solution)/shard_map/all_to_all | solution.py:85
  206.9 22.0 %collective-permute-done.25.refs_3_ = bf16[6,32,576]{2,1,0:T(8,128)(2,1)S(1)} collective-permute-done((bf16[6,32,576]{2,1,0:T(8,128)(2,1)}, bf16[6,32,576]{2,1,0:T(8,128)(2,1)S(1)}, u32[]{:S(2)}, u32[]{:S(2)}) %collective-permute-start.25) | collective-permute-done | bytes 221216 | tf_op jit(solution)/shard_map/ppermute | solution.py:73
  229.6 4.4 %collective-permute-done.26.refs_4_ = bf16[6,32,576]{2,1,0:T(8,128)(2,1)S(1)} collective-permute-done((bf16[6,32,576]{2,1,0:T(8,128)(2,1)}, bf16[6,32,576]{2,1,0:T(8,128)(2,1)S(1)}, u32[]{:S(2)}, u32[]{:S(2)}) %collective-permute-start.26) | collective-permute-done | bytes 221216 | tf_op jit(solution)/shard_map/ppermute | solution.py:73
  234.7 4.9 %collective-permute-done.27.refs_5_ = bf16[6,32,576]{2,1,0:T(8,128)(2,1)} collective-permute-done((bf16[6,32,576]{2,1,0:T(8,128)(2,1)}, bf16[6,32,576]{2,1,0:T(8,128)(2,1)}, u32[]{:S(2)}, u32[]{:S(2)}) %collective-permute-start.27) | collective-permute-done | bytes 221216 | tf_op jit(solution)/shard_map/ppermute | solution.py:73
  240.3 3.0 collective-permute-done.29.refs_7_
  251.3 3.1 collective-permute-start.32
  264.7 3.1 %collective-permute-start.33 = (bf16[4,32,576]{2,1,0:T(8,128)(2,1)}, bf16[4,32,576]{2,1,0:T(8,128)(2,1)S(1)}, u32[]{:S(2)}, u32[]{:S(2)}) collective-permute-start(bf16[4,32,576]{2,1,0:T(8,128)(2,1)} %get-tuple-element.70), channel_id=1, source_target_pairs={{64,32},{68,36},{72,40},{76,44},{80,48},{84,52},{88,56},{92,60},{9... | collective-permute-start | bytes 442376 | tf_op jit(solution)/shard_map/ppermute | solution.py:39
  267.8 4.7 %copy.38 = bf16[128,16,576]{0,2,1:T(8,128)(2,1)} copy(bf16[128,16,576]{2,1,0:T(8,128)(2,1)} %bitcast.54) | data formatting | bytes 4718592 | tf_op jit(solution)/shard_map/reshape | solution.py:485
  273.2 2.8 collective-permute-start.34
  283.9 11.7 %collective-permute-start.38 = (bf16[32,576]{1,0:T(8,128)(2,1)S(1)}, bf16[32,576]{1,0:T(8,128)(2,1)S(1)}, u32[]{:S(2)}, u32[]{:S(2)}) collective-permute-start(bf16[32,576]{1,0:T(8,128)(2,1)S(1)} %get-tuple-element.61), channel_id=1, source_target_pairs={{4,192},{20,196},{36,200},{52,204},{68,208},{84,212},{100,216},{11... | collective-permute-start | bytes 110600 | tf_op jit(solution)/shard_map/ppermute | solution.py:476
  296.9 8.5 %collective-permute-done.37 = bf16[32,576]{1,0:T(8,128)(2,1)S(1)} collective-permute-done((bf16[32,576]{1,0:T(8,128)(2,1)S(1)}, bf16[32,576]{1,0:T(8,128)(2,1)S(1)}, u32[]{:S(2)}, u32[]{:S(2)}) %collective-permute-start.37) | collective-permute-done | bytes 36896 | tf_op jit(solution)/shard_map/ppermute | solution.py:476
  306.3 3.1 %copy.51 = bf16[16,512,128]{2,1,0:T(8,128)(2,1)} copy(bf16[16,512,128]{2,1,0:T(8,128)(2,1)} %bitcast.30) | data formatting | bytes 4194304
  (194 shorter events, 106.3 us)
Async XLA Ops:
  19.5 20.0 %collective-permute-start.2 = (bf16[4,32,576]{2,1,0:T(8,128)(2,1)S(1)}, bf16[4,32,576]{2,1,0:T(8,128)(2,1)S(1)}, u32[]{:S(2)}, u32[]{:S(2)}) collective-permute-start(bf16[4,32,576]{2,1,0:T(8,128)(2,1)S(1)} %collective-permute-done.1.refs_2_), channel_id=1, source_target_pairs={{0,224},{4,228},{8,232},{12,236},{16,240},{20,244},{24,248},{28,25... | collective-permute-start | bytes 442376 | tf_op jit(solution)/shard_map/ppermute | solution.py:39
  23.3 16.3 %collective-permute-start.6 = (bf16[4,32,576]{2,1,0:T(8,128)(2,1)S(1)}, bf16[4,32,576]{2,1,0:T(8,128)(2,1)S(1)}, u32[]{:S(2)}, u32[]{:S(2)}) collective-permute-start(bf16[4,32,576]{2,1,0:T(8,128)(2,1)S(1)} %collective-permute-done.5.refs_5_), channel_id=1, source_target_pairs={{0,32},{4,36},{8,40},{12,44},{16,48},{20,52},{24,56},{28,60},{96,1... | collective-permute-start | bytes 442376 | tf_op jit(solution)/shard_map/ppermute | solution.py:39
  26.3 12.6 %all-to-all-start = ((s32[8,1,6]{2,1,0:T(1,128)}), s32[8,1,6]{2,1,0:T(1,128)S(1)}, u32[]{:S(2)}, u32[]{:S(2)}) async-start(s32[8,1,6]{2,1,0:T(1,128)} %bitcast), calls=%async_computation | async-start | bytes 8192 | tf_op jit(solution)/shard_map/all_to_all | solution.py:85
  43.2 31.7 %all-to-all-start.1 = ((bf16[8,6,32,576]{3,2,1,0:T(8,128)(2,1)}), bf16[8,6,32,576]{3,2,1,0:T(8,128)(2,1)}, u32[]{:S(2)}, u32[]{:S(2)}) async-start(bf16[8,6,32,576]{3,2,1,0:T(8,128)(2,1)} %bitcast.53), calls=%async_computation.1 | async-start | bytes 3932160 | tf_op jit(solution)/shard_map/all_to_all | solution.py:85
  48.3 26.7 %collective-permute-start.7 = (bf16[32,576]{1,0:T(8,128)(2,1)S(1)}, bf16[32,576]{1,0:T(8,128)(2,1)S(1)}, u32[]{:S(2)}, u32[]{:S(2)}) collective-permute-start(bf16[32,576]{1,0:T(8,128)(2,1)S(1)} %get-tuple-element.75), channel_id=1, source_target_pairs={{192,0},{196,16},{200,32},{204,48},{208,64},{212,80},{216,96},{220... | collective-permute-start | bytes 110600 | tf_op jit(solution)/shard_map/ppermute | solution.py:402
  53.5 21.5 %collective-permute-start.8 = (bf16[32,576]{1,0:T(8,128)(2,1)S(1)}, bf16[32,576]{1,0:T(8,128)(2,1)S(1)}, u32[]{:S(2)}, u32[]{:S(2)}) collective-permute-start(bf16[32,576]{1,0:T(8,128)(2,1)S(1)} %get-tuple-element.74), channel_id=1, source_target_pairs={{192,4},{196,20},{200,36},{204,52},{208,68},{212,84},{216,100},{22... | collective-permute-start | bytes 110600 | tf_op jit(solution)/shard_map/ppermute | solution.py:402
  55.4 19.6 %collective-permute-start.9 = (bf16[32,576]{1,0:T(8,128)(2,1)S(1)}, bf16[32,576]{1,0:T(8,128)(2,1)S(1)}, u32[]{:S(2)}, u32[]{:S(2)}) collective-permute-start(bf16[32,576]{1,0:T(8,128)(2,1)S(1)} %get-tuple-element.73), channel_id=1, source_target_pairs={{192,8},{196,24},{200,40},{204,56},{208,72},{212,88},{216,104},{22... | collective-permute-start | bytes 110600 | tf_op jit(solution)/shard_map/ppermute | solution.py:402
  56.7 18.3 %collective-permute-start.10 = (bf16[32,576]{1,0:T(8,128)(2,1)S(1)}, bf16[32,576]{1,0:T(8,128)(2,1)S(1)}, u32[]{:S(2)}, u32[]{:S(2)}) collective-permute-start(bf16[32,576]{1,0:T(8,128)(2,1)S(1)} %get-tuple-element.72), channel_id=1, source_target_pairs={{192,12},{196,28},{200,44},{204,60},{208,76},{212,92},{216,108},{2... | collective-permute-start | bytes 110600 | tf_op jit(solution)/shard_map/ppermute | solution.py:402
  80.8 19.3 %collective-permute-start.13 = (bf16[7,32,576]{2,1,0:T(8,128)(2,1)}, bf16[7,32,576]{2,1,0:T(8,128)(2,1)S(1)}, u32[]{:S(2)}, u32[]{:S(2)}) collective-permute-start(bf16[7,32,576]{2,1,0:T(8,128)(2,1)} %get-tuple-element.36.refs_0_.refs_4_), channel_id=1, source_target_pairs={{0,3},{1,0},{2,1},{3,2},{4,7},{5,4},{6,5},{7,6},{8,11},{9,8},{10,9... | collective-permute-start | bytes 774152 | tf_op jit(solution)/shard_map/ppermute | solution.py:81
  87.0 13.2 %collective-permute-start.12 = (bf16[7,32,576]{2,1,0:T(8,128)(2,1)S(1)}, bf16[7,32,576]{2,1,0:T(8,128)(2,1)}, u32[]{:S(2)}, u32[]{:S(2)}) collective-permute-start(bf16[7,32,576]{2,1,0:T(8,128)(2,1)S(1)} %collective-permute-done.11.refs_1_.refs_5_), channel_id=1, source_target_pairs={{0,1},{1,2},{2,3},{3,0},{4,5},{5,6},{6,7},{7,4},{8,9},{9,10},{10,1... | collective-permute-start | bytes 774152 | tf_op jit(solution)/shard_map/ppermute | solution.py:81
  87.0 13.2 %collective-permute-start.14 = (bf16[6,32,576]{2,1,0:T(8,128)(2,1)}, bf16[6,32,576]{2,1,0:T(8,128)(2,1)}, u32[]{:S(2)}, u32[]{:S(2)}) collective-permute-start(bf16[6,32,576]{2,1,0:T(8,128)(2,1)} %get-tuple-element.37.refs_8_), channel_id=1, source_target_pairs={{0,1},{1,2},{2,3},{3,0},{4,5},{5,6},{6,7},{7,4},{8,9},{9,10},{10,1... | collective-permute-start | bytes 663560 | tf_op jit(solution)/shard_map/ppermute | solution.py:81
  128.8 19.3 %all-to-all-start.2 = ((bf16[4,1024,128]{2,1,0:T(8,128)(2,1)}), bf16[4,1024,128]{2,1,0:T(8,128)(2,1)}, u32[]{:S(2)}, u32[]{:S(2)}) async-start(bf16[4,1024,128]{2,1,0:T(8,128)(2,1)} %fusion), calls=%async_computation.2 | async-start | bytes 2097152 | tf_op jit(solution)/shard_map/all_to_all | solution.py:85
  133.2 27.4 %collective-permute-start.18 = (bf16[7,32,576]{2,1,0:T(8,128)(2,1)}, bf16[7,32,576]{2,1,0:T(8,128)(2,1)}, u32[]{:S(2)}, u32[]{:S(2)}) collective-permute-start(bf16[7,32,576]{2,1,0:T(8,128)(2,1)} %get-tuple-element.40), channel_id=1, source_target_pairs={{0,3},{1,0},{2,1},{3,2},{4,7},{5,4},{6,5},{7,6},{8,11},{9,8},{10,9... | collective-permute-start | bytes 774152 | tf_op jit(solution)/shard_map/ppermute | solution.py:81
  150.2 15.8 %all-to-all-start.3 = ((bf16[8,128,128]{2,1,0:T(8,128)(2,1)}), bf16[8,128,128]{2,1,0:T(8,128)(2,1)}, u32[]{:S(2)}, u32[]{:S(2)}) async-start(bf16[8,128,128]{2,1,0:T(8,128)(2,1)} %bitcast.28), calls=%async_computation.3 | async-start | bytes 524288 | tf_op jit(solution)/shard_map/all_to_all | solution.py:85
  157.9 18.2 %collective-permute-start.17 = (bf16[7,32,576]{2,1,0:T(8,128)(2,1)}, bf16[7,32,576]{2,1,0:T(8,128)(2,1)S(1)}, u32[]{:S(2)}, u32[]{:S(2)}) collective-permute-start(bf16[7,32,576]{2,1,0:T(8,128)(2,1)} %get-tuple-element.39), channel_id=1, source_target_pairs={{0,1},{1,2},{2,3},{3,0},{4,5},{5,6},{6,7},{7,4},{8,9},{9,10},{10,1... | collective-permute-start | bytes 774152 | tf_op jit(solution)/shard_map/ppermute | solution.py:81
  158.0 17.4 %collective-permute-start.20 = (bf16[6,32,576]{2,1,0:T(8,128)(2,1)}, bf16[6,32,576]{2,1,0:T(8,128)(2,1)S(1)}, u32[]{:S(2)}, u32[]{:S(2)}) collective-permute-start(bf16[6,32,576]{2,1,0:T(8,128)(2,1)} %get-tuple-element.43), channel_id=1, source_target_pairs={{0,3},{1,0},{2,1},{3,2},{4,7},{5,4},{6,5},{7,6},{8,11},{9,8},{10,9... | collective-permute-start | bytes 663560 | tf_op jit(solution)/shard_map/ppermute | solution.py:81
  160.6 13.2 %collective-permute-start.21 = (bf16[6,32,576]{2,1,0:T(8,128)(2,1)}, bf16[6,32,576]{2,1,0:T(8,128)(2,1)}, u32[]{:S(2)}, u32[]{:S(2)}) collective-permute-start(bf16[6,32,576]{2,1,0:T(8,128)(2,1)} %get-tuple-element.44), channel_id=1, source_target_pairs={{0,1},{1,2},{2,3},{3,0},{4,5},{5,6},{6,7},{7,4},{8,9},{9,10},{10,1... | collective-permute-start | bytes 663560 | tf_op jit(solution)/shard_map/ppermute | solution.py:81
  162.4 19.6 %collective-permute-start.19 = (bf16[7,32,576]{2,1,0:T(8,128)(2,1)}, bf16[7,32,576]{2,1,0:T(8,128)(2,1)S(1)}, u32[]{:S(2)}, u32[]{:S(2)}) collective-permute-start(bf16[7,32,576]{2,1,0:T(8,128)(2,1)} %add_convert_fusion), channel_id=1, source_target_pairs={{0,3},{1,0},{2,1},{3,2},{4,7},{5,4},{6,5},{7,6},{8,11},{9,8},{10,9... | collective-permute-start | bytes 774152 | tf_op jit(solution)/shard_map/ppermute | solution.py:81
  167.8 21.3 %all-to-all-start.4 = ((bf16[8,128,128]{2,1,0:T(8,128)(2,1)}), bf16[8,128,128]{2,1,0:T(8,128)(2,1)}, u32[]{:S(2)}, u32[]{:S(2)}) async-start(bf16[8,128,128]{2,1,0:T(8,128)(2,1)} %broadcast_in_dim.77), calls=%async_computation.4 | async-start | bytes 524288 | tf_op jit(solution)/shard_map/all_to_all | solution.py:85
  184.8 17.5 %collective-permute-start.23 = (bf16[6,32,576]{2,1,0:T(8,128)(2,1)}, bf16[6,32,576]{2,1,0:T(8,128)(2,1)S(1)}, u32[]{:S(2)}, u32[]{:S(2)}) collective-permute-start(bf16[6,32,576]{2,1,0:T(8,128)(2,1)} %get-tuple-element.47), channel_id=1, source_target_pairs={{0,4},{4,0},{8,12},{12,8},{16,20},{20,16},{24,28},{28,24},{32,36},... | collective-permute-start | bytes 663560 | tf_op jit(solution)/shard_map/ppermute | solution.py:73
  188.7 15.7 %collective-permute-start.24 = (bf16[6,32,576]{2,1,0:T(8,128)(2,1)}, bf16[6,32,576]{2,1,0:T(8,128)(2,1)S(1)}, u32[]{:S(2)}, u32[]{:S(2)}) collective-permute-start(bf16[6,32,576]{2,1,0:T(8,128)(2,1)} %get-tuple-element.48), channel_id=1, source_target_pairs={{0,8},{4,12},{8,16},{12,20},{16,24},{20,28},{24,0},{28,4},{32,40},... | collective-permute-start | bytes 663560 | tf_op jit(solution)/shard_map/ppermute | solution.py:73
  191.6 114.6 %all-to-all-start.5 = ((bf16[8,1024,128]{2,1,0:T(8,128)(2,1)}), bf16[8,1024,128]{2,1,0:T(8,128)(2,1)}, u32[]{:S(2)}, u32[]{:S(2)}) async-start(bf16[8,1024,128]{2,1,0:T(8,128)(2,1)} %broadcast_in_dim.78), calls=%async_computation.5 | async-start | bytes 4194304 | tf_op jit(solution)/shard_map/all_to_all | solution.py:85
  197.4 31.5 %collective-permute-start.25 = (bf16[6,32,576]{2,1,0:T(8,128)(2,1)}, bf16[6,32,576]{2,1,0:T(8,128)(2,1)S(1)}, u32[]{:S(2)}, u32[]{:S(2)}) collective-permute-start(bf16[6,32,576]{2,1,0:T(8,128)(2,1)} %get-tuple-element.49), channel_id=1, source_target_pairs={{0,12},{4,8},{8,20},{12,16},{16,28},{20,24},{24,4},{28,0},{32,44},... | collective-permute-start | bytes 663560 | tf_op jit(solution)/shard_map/ppermute | solution.py:73
  199.1 34.9 %collective-permute-start.26 = (bf16[6,32,576]{2,1,0:T(8,128)(2,1)}, bf16[6,32,576]{2,1,0:T(8,128)(2,1)S(1)}, u32[]{:S(2)}, u32[]{:S(2)}) collective-permute-start(bf16[6,32,576]{2,1,0:T(8,128)(2,1)} %copy-done.20), channel_id=1, source_target_pairs={{0,16},{4,20},{8,24},{12,28},{16,0},{20,4},{24,8},{28,12},{32,48},... | collective-permute-start | bytes 663560 | tf_op jit(solution)/shard_map/ppermute | solution.py:73
  201.5 38.2 %collective-permute-start.27 = (bf16[6,32,576]{2,1,0:T(8,128)(2,1)}, bf16[6,32,576]{2,1,0:T(8,128)(2,1)}, u32[]{:S(2)}, u32[]{:S(2)}) collective-permute-start(bf16[6,32,576]{2,1,0:T(8,128)(2,1)} %copy-done.19), channel_id=1, source_target_pairs={{0,20},{4,16},{8,28},{12,24},{16,4},{20,0},{24,12},{28,8},{32,52},... | collective-permute-start | bytes 663560 | tf_op jit(solution)/shard_map/ppermute | solution.py:73
  203.0 36.6 %collective-permute-start.28 = (bf16[6,32,576]{2,1,0:T(8,128)(2,1)}, bf16[6,32,576]{2,1,0:T(8,128)(2,1)S(1)}, u32[]{:S(2)}, u32[]{:S(2)}) collective-permute-start(bf16[6,32,576]{2,1,0:T(8,128)(2,1)} %copy-done.18), channel_id=1, source_target_pairs={{0,24},{4,28},{8,0},{12,4},{16,8},{20,12},{24,16},{28,20},{32,56},... | collective-permute-start | bytes 663560 | tf_op jit(solution)/shard_map/ppermute | solution.py:73
  205.1 38.2 %collective-permute-start.29 = (bf16[6,32,576]{2,1,0:T(8,128)(2,1)}, bf16[6,32,576]{2,1,0:T(8,128)(2,1)S(1)}, u32[]{:S(2)}, u32[]{:S(2)}) collective-permute-start(bf16[6,32,576]{2,1,0:T(8,128)(2,1)} %copy-done.17), channel_id=1, source_target_pairs={{0,28},{4,24},{8,4},{12,0},{16,12},{20,8},{24,20},{28,16},{32,60},... | collective-permute-start | bytes 663560 | tf_op jit(solution)/shard_map/ppermute | solution.py:73
  279.3 26.2 %collective-permute-start.36 = (bf16[4,32,576]{2,1,0:T(8,128)(2,1)S(1)}, bf16[4,32,576]{2,1,0:T(8,128)(2,1)S(1)}, u32[]{:S(2)}, u32[]{:S(2)}) collective-permute-start(bf16[4,32,576]{2,1,0:T(8,128)(2,1)S(1)} %get-tuple-element.69), channel_id=1, source_target_pairs={{32,0},{36,4},{40,8},{44,12},{48,16},{52,20},{56,24},{60,28},{64,3... | collective-permute-start | bytes 442376 | tf_op jit(solution)/shard_map/ppermute | solution.py:39
  280.6 24.9 %collective-permute-start.35 = (bf16[4,32,576]{2,1,0:T(8,128)(2,1)S(1)}, bf16[4,32,576]{2,1,0:T(8,128)(2,1)S(1)}, u32[]{:S(2)}, u32[]{:S(2)}) collective-permute-start(bf16[4,32,576]{2,1,0:T(8,128)(2,1)S(1)} %get-tuple-element.68), channel_id=1, source_target_pairs={{0,32},{4,36},{8,40},{12,44},{16,48},{20,52},{24,56},{28,60},{32,6... | collective-permute-start | bytes 442376 | tf_op jit(solution)/shard_map/ppermute | solution.py:39
  281.3 14.3 %collective-permute-start.40 = (bf16[32,576]{1,0:T(8,128)(2,1)S(1)}, bf16[32,576]{1,0:T(8,128)(2,1)S(1)}, u32[]{:S(2)}, u32[]{:S(2)}) collective-permute-start(bf16[32,576]{1,0:T(8,128)(2,1)S(1)} %get-tuple-element.61), channel_id=1, source_target_pairs={{12,192},{28,196},{44,200},{60,204},{76,208},{92,212},{108,216},{1... | collective-permute-start | bytes 110600 | tf_op jit(solution)/shard_map/ppermute | solution.py:476
  282.6 14.3 %collective-permute-start.39 = (bf16[32,576]{1,0:T(8,128)(2,1)S(1)}, bf16[32,576]{1,0:T(8,128)(2,1)S(1)}, u32[]{:S(2)}, u32[]{:S(2)}) collective-permute-start(bf16[32,576]{1,0:T(8,128)(2,1)S(1)} %get-tuple-element.61), channel_id=1, source_target_pairs={{8,192},{24,196},{40,200},{56,204},{72,208},{88,212},{104,216},{12... | collective-permute-start | bytes 110600 | tf_op jit(solution)/shard_map/ppermute | solution.py:476
  283.9 13.0 %collective-permute-start.38 = (bf16[32,576]{1,0:T(8,128)(2,1)S(1)}, bf16[32,576]{1,0:T(8,128)(2,1)S(1)}, u32[]{:S(2)}, u32[]{:S(2)}) collective-permute-start(bf16[32,576]{1,0:T(8,128)(2,1)S(1)} %get-tuple-element.61), channel_id=1, source_target_pairs={{4,192},{20,196},{36,200},{52,204},{68,208},{84,212},{100,216},{11... | collective-permute-start | bytes 110600 | tf_op jit(solution)/shard_map/ppermute | solution.py:476
  (58 other events, 567.6 us)

commit v5 on v1

--- a/solution.py
+++ b/solution.py
@@ -48,16 +48,19 @@
     return [own, left[1], left[2], left[3], right[4], right[3], right[2], right[1]]
 
 
-def reduce_z(terms, limit):
+def reduce_z(terms, limit, beside):
     right, left = terms[4], terms[5]
     for hop in range(4):
         right = shift_z(right, 1, lambda z: (z + 4 - hop) % Z < limit)
         if hop < 3:
+            left = shift_z(left, -1, lambda z: (z - 3 + hop) % Z < limit)
+        if hop == 1:
+            right, left, beside = lax.optimization_barrier((right, left, beside))
+        if hop < 3:
             right = narrow(wide(right) + wide(terms[3 - hop]))
-            left = shift_z(left, -1, lambda z: (z - 3 + hop) % Z < limit)
         if hop < 2:
             left = narrow(wide(left) + wide(terms[6 + hop]))
-    return wide(terms[0]) + wide(right) + wide(left)
+    return wide(terms[0]) + wide(right) + wide(left), beside
 
 
 def shift_yc(array, y_step, c_step):
@@ -467,9 +470,9 @@
             )
         )
     d_query = jnp.transpose(d_query.reshape(query.shape), (1, 2, 0))
-    received, d_query = lax.optimization_barrier((received, d_query))
     by_z = by_owner(at_owner, received, block_count)
-    d_cache = reduce_z(by_z, Z_FULL) + wide(jnp.stack(own_back))
+    d_cache, d_query = reduce_z(by_z, Z_FULL, d_query)
+    d_cache = d_cache + wide(jnp.stack(own_back))
     return jnp.transpose(d_query, (2, 0, 1)), d_cache, d_value_weight
 
 

time: 294 us -> 278 us (0.946)
  the two profiles are of different devices: /device:TPU:193 before, /device:TPU:216 now
where the time goes in v5:
time: 278 us; the launch traced here: 276 us
  starting transfers between devices  110 us (40%)
  waiting for transfers between devices  87.4 us (31%)
  local copies, waits for them, and re-layouts  34.7 us (12%)
  Pallas kernels  24.4 us (9%)
  other arithmetic  11.1 us (4%)
  matrix products  7.62 us (3%)
    all_to_all x6, starting transfers between devices, trade(): lax.all_to_all(blocks, 'seq', split_axis=0, concat_axis=0, axis_index_gro...  37.5 us
    ppermute x12, waiting for transfers between devices, shift_x(): return lax.ppermute(array, 'head', [(x, (x + step) % X) for x in range(X)])  31.1 us
    ppermute x14, starting transfers between devices, shift_z(): return lax.ppermute(array, 'seq', pairs)  29.3 us
    unnamed x86, local copies, waits for them, and re-layouts  20.7 us
    ppermute x7, waiting for transfers between devices, shift_yc(): return lax.ppermute(array, 'seq', pairs)  20.2 us
    pallas_call x1, Pallas kernels, attend(): pl.pallas_call(attend_kernel, grid_spec=pltpu.PrefetchScalarGridSpec(num_...  14.6 us
    ppermute x14, waiting for transfers between devices, shift_z(): return lax.ppermute(array, 'seq', pairs)  14.5 us
    ppermute x4, waiting for transfers between devices, local(): lax.ppermute(own_share, 'seq', [((o - FIRST_OWN_OWNER) * block_count + j,...  14.3 us
  transfers between devices with their start and end apart: 48, of which 21 were waited for; matrix products, arithmetic and copies ran while one was open for 11% of the time, Pallas kernels for 2%

profile of v5, /device:TPU:216, one launch (start us, length us, event | category | flops | bytes accessed | tf_op | source)
XLA Modules:
  0.0 276.3 jit_solution(4751283391810352754)
XLA Ops:
  6.1 5.9 %collective-permute-done.3.refs_7_ = bf16[4,32,576]{2,1,0:T(8,128)(2,1)S(1)} collective-permute-done((bf16[4,32,576]{2,1,0:T(8,128)(2,1)S(1)}, bf16[4,32,576]{2,1,0:T(8,128)(2,1)S(1)}, u32[]{:S(2)}, u32[]{:S(2)}) %collective-permute-start.3) | collective-permute-done | bytes 147488 | tf_op jit(solution)/shard_map/ppermute | solution.py:39
  15.3 3.9 %collective-permute-done.4.refs_6_ = bf16[4,32,576]{2,1,0:T(8,128)(2,1)S(1)} collective-permute-done((bf16[4,32,576]{2,1,0:T(8,128)(2,1)S(1)}, bf16[4,32,576]{2,1,0:T(8,128)(2,1)S(1)}, u32[]{:S(2)}, u32[]{:S(2)}) %collective-permute-start.4) | collective-permute-done | bytes 147488 | tf_op jit(solution)/shard_map/ppermute | solution.py:39
  21.2 3.9 %collective-permute-start.2 = (bf16[4,32,576]{2,1,0:T(8,128)(2,1)S(1)}, bf16[4,32,576]{2,1,0:T(8,128)(2,1)S(1)}, u32[]{:S(2)}, u32[]{:S(2)}) collective-permute-start(bf16[4,32,576]{2,1,0:T(8,128)(2,1)S(1)} %collective-permute-done.1.refs_2_), channel_id=1, source_target_pairs={{0,224},{4,228},{8,232},{12,236},{16,240},{20,244},{24,248},{28,25... | collective-permute-start | bytes 442376 | tf_op jit(solution)/shard_map/ppermute | solution.py:39
  29.1 4.7 %all-to-all-start = ((s32[8,1,6]{2,1,0:T(1,128)}), s32[8,1,6]{2,1,0:T(1,128)S(1)}, u32[]{:S(2)}, u32[]{:S(2)}) async-start(s32[8,1,6]{2,1,0:T(1,128)} %bitcast), calls=%async_computation | async-start | bytes 8192 | tf_op jit(solution)/shard_map/all_to_all | solution.py:85
  33.8 3.2 %all-to-all-done = s32[8,1,6]{2,1,0:T(1,128)S(1)} async-done(((s32[8,1,6]{2,1,0:T(1,128)}), s32[8,1,6]{2,1,0:T(1,128)S(1)}, u32[]{:S(2)}, u32[]{:S(2)}) %all-to-all-start) | async-done | bytes 224 | tf_op jit(solution)/shard_map/all_to_all | solution.py:85
  38.5 2.9 %pack.1 = bf16[48,32,576]{2,1,0:T(8,128)(2,1)} custom-call(s32[48]{0:T(128)} %max.8.block_ref, s32[1]{0:T(128)} %bitcast.3.z_ref, bf16[4,32,576]{2,1,0:T(8,128)(2,1)} %bitcast.40, bf16[4,32,576]{2,1,0:T(8,128)(2,1)} %copy-done.30, bf16[4,32,576]{2,1,0:T(8,128)(2,1)} %copy-done.33, bf16[4,32,576]{2,1,0:T(8,128)(2,1)} %copy-done.35, ...), custom_call_target="tpu_custom_call" | custom-call | tf_op jit(solution)/shard_map/pack/pallas_call | solution.py:118
  41.4 6.5 %all-to-all-start.1 = ((bf16[8,6,32,576]{3,2,1,0:T(8,128)(2,1)}), bf16[8,6,32,576]{3,2,1,0:T(8,128)(2,1)}, u32[]{:S(2)}, u32[]{:S(2)}) async-start(bf16[8,6,32,576]{3,2,1,0:T(8,128)(2,1)} %bitcast.35), calls=%async_computation.1 | async-start | bytes 3932160 | tf_op jit(solution)/shard_map/all_to_all | solution.py:85
  47.9 9.2 %collective-permute-start.7 = (bf16[32,576]{1,0:T(8,128)(2,1)S(1)}, bf16[32,576]{1,0:T(8,128)(2,1)S(1)}, u32[]{:S(2)}, u32[]{:S(2)}) collective-permute-start(bf16[32,576]{1,0:T(8,128)(2,1)S(1)} %get-tuple-element.81), channel_id=1, source_target_pairs={{192,0},{196,16},{200,32},{204,48},{208,64},{212,80},{216,96},{220... | collective-permute-start | bytes 110600 | tf_op jit(solution)/shard_map/ppermute | solution.py:389
  63.6 4.1 %copy.36 = bf16[128,16,512]{2,1,0:T(8,128)(2,1)} copy(bf16[128,16,512]{2,0,1:T(8,128)(2,1)} %convert_bitcast_fusion) | data formatting | bytes 4194304 | tf_op jit(solution)/shard_map/convert_element_type | solution.py:96
  67.7 4.9 %copy.37 = bf16[128,16,576]{2,1,0:T(8,128)(2,1)} copy(bf16[128,16,576]{0,2,1:T(8,128)(2,1)} %param.5) | data formatting | bytes 4718592 | tf_op args[0]
  80.6 6.2 %collective-permute-done.11.refs_1_.refs_5_ = bf16[7,32,576]{2,1,0:T(8,128)(2,1)S(1)} collective-permute-done((bf16[7,32,576]{2,1,0:T(8,128)(2,1)}, bf16[7,32,576]{2,1,0:T(8,128)(2,1)S(1)}, u32[]{:S(2)}, u32[]{:S(2)}) %collective-permute-start.11) | collective-permute-done | bytes 258080 | tf_op jit(solution)/shard_map/ppermute | solution.py:81
  90.3 11.8 %collective-permute-done.14.refs_9_ = bf16[6,32,576]{2,1,0:T(8,128)(2,1)} collective-permute-done((bf16[6,32,576]{2,1,0:T(8,128)(2,1)}, bf16[6,32,576]{2,1,0:T(8,128)(2,1)}, u32[]{:S(2)}, u32[]{:S(2)}) %collective-permute-start.14) | collective-permute-done | bytes 221216 | tf_op jit(solution)/shard_map/ppermute | solution.py:81
  103.0 14.6 %attend.1 = (bf16[2048,576]{1,0:T(8,128)(2,1)}, bf16[2048,512]{1,0:T(8,128)(2,1)}, bf16[7,32,576]{2,1,0:T(8,128)(2,1)}, bf16[7,32,576]{2,1,0:T(8,128)(2,1)}, bf1...) custom-call(s32[1]{0:T(128)} %bitcast.2.x_ref, ...), custom_call_target="tpu_custom_call" | custom-call | tf_op jit(solution)/shard_map/attend/pallas_call | solution.py:254
  117.6 4.0 %fusion.3 = bf16[16,512,128]{2,1,0:T(8,128)(2,1)S(1)} fusion(bf16[128,16,512]{2,1,0:T(8,128)(2,1)} %bitcast.37, bf16[128,16,128]{2,1,0:T(8,128)(2,1)S(1)} %copy-done.23), kind=kOutput, calls=%fused_computation.5 | convolution fusion | flops 269484032 | bytes 4718592 | tf_op jit(solution)/shard_map/qhc,qhv->hcv/dot_general | solution.py:434
  123.2 2.8 collective-permute-done.41
  125.9 2.8 %fusion = bf16[4,1024,128]{2,1,0:T(8,128)(2,1)} fusion(bf16[4,1024,128]{2,1,0:T(8,128)(2,1)} %collective-permute-done.41, bf16[4,2,1024,128]{3,2,1,0:T(8,128)(2,1)} %bitcast.33, s32[]{:T(128)S(6)} %select_n.179), kind=kLoop, calls=%fused_computation.1 | loop fusion | flops 2097152 | bytes 3145732 | tf_op jit(solution)/shard_map/convert_element_type | solution.py:96
  128.7 4.5 %all-to-all-start.2 = ((bf16[4,1024,128]{2,1,0:T(8,128)(2,1)}), bf16[4,1024,128]{2,1,0:T(8,128)(2,1)}, u32[]{:S(2)}, u32[]{:S(2)}) async-start(bf16[4,1024,128]{2,1,0:T(8,128)(2,1)} %fusion), calls=%async_computation.2 | async-start | bytes 2097152 | tf_op jit(solution)/shard_map/all_to_all | solution.py:85
  137.3 5.8 %collective-permute-done.18 = bf16[7,32,576]{2,1,0:T(8,128)(2,1)S(1)} collective-permute-done((bf16[7,32,576]{2,1,0:T(8,128)(2,1)}, bf16[7,32,576]{2,1,0:T(8,128)(2,1)S(1)}, u32[]{:S(2)}, u32[]{:S(2)}) %collective-permute-start.18) | collective-permute-done | bytes 258080 | tf_op jit(solution)/shard_map/ppermute | solution.py:81
  149.0 9.3 %all-to-all-start.3 = ((bf16[8,128,128]{2,1,0:T(8,128)(2,1)}), bf16[8,128,128]{2,1,0:T(8,128)(2,1)}, u32[]{:S(2)}, u32[]{:S(2)}) async-start(bf16[8,128,128]{2,1,0:T(8,128)(2,1)} %bitcast.41), calls=%async_computation.3 | async-start | bytes 524288 | tf_op jit(solution)/shard_map/all_to_all | solution.py:85
  160.3 7.3 %collective-permute-done.22.refs_5_ = bf16[6,32,576]{2,1,0:T(8,128)(2,1)S(1)} collective-permute-done((bf16[6,32,576]{2,1,0:T(8,128)(2,1)S(1)}, bf16[6,32,576]{2,1,0:T(8,128)(2,1)S(1)}, u32[]{:S(2)}, u32[]{:S(2)}) %collective-permute-start.22) | collective-permute-done | bytes 221216 | tf_op jit(solution)/shard_map/ppermute | solution.py:81
  176.3 7.2 %all-to-all-start.4 = ((bf16[8,128,128]{2,1,0:T(8,128)(2,1)}), bf16[8,128,128]{2,1,0:T(8,128)(2,1)}, u32[]{:S(2)}, u32[]{:S(2)}) async-start(bf16[8,128,128]{2,1,0:T(8,128)(2,1)} %broadcast_in_dim.77), calls=%async_computation.4 | async-start | bytes 524288 | tf_op jit(solution)/shard_map/all_to_all | solution.py:85
  194.6 4.6 %collective-permute-done.27.refs_5_ = bf16[6,32,576]{2,1,0:T(8,128)(2,1)} collective-permute-done((bf16[6,32,576]{2,1,0:T(8,128)(2,1)}, bf16[6,32,576]{2,1,0:T(8,128)(2,1)}, u32[]{:S(2)}, u32[]{:S(2)}) %collective-permute-start.27) | collective-permute-done | bytes 221216 | tf_op jit(solution)/shard_map/ppermute | solution.py:73
  199.2 5.6 %collective-permute-done.28.refs_6_ = bf16[6,32,576]{2,1,0:T(8,128)(2,1)} collective-permute-done((bf16[6,32,576]{2,1,0:T(8,128)(2,1)}, bf16[6,32,576]{2,1,0:T(8,128)(2,1)}, u32[]{:S(2)}, u32[]{:S(2)}) %collective-permute-start.28) | collective-permute-done | bytes 221216 | tf_op jit(solution)/shard_map/ppermute | solution.py:73
  204.8 5.1 %collective-permute-done.29.refs_7_ = bf16[6,32,576]{2,1,0:T(8,128)(2,1)} collective-permute-done((bf16[6,32,576]{2,1,0:T(8,128)(2,1)}, bf16[6,32,576]{2,1,0:T(8,128)(2,1)}, u32[]{:S(2)}, u32[]{:S(2)}) %collective-permute-start.29) | collective-permute-done | bytes 221216 | tf_op jit(solution)/shard_map/ppermute | solution.py:73
  221.5 5.4 %all-to-all-start.5 = ((bf16[8,1024,128]{2,1,0:T(8,128)(2,1)}), bf16[8,1024,128]{2,1,0:T(8,128)(2,1)}, u32[]{:S(2)}, u32[]{:S(2)}) async-start(bf16[8,1024,128]{2,1,0:T(8,128)(2,1)} %broadcast_in_dim.78), calls=%async_computation.5 | async-start | bytes 4194304 | tf_op jit(solution)/shard_map/all_to_all | solution.py:85
  226.9 3.4 %collective-permute-start.32 = (bf16[4,32,576]{2,1,0:T(8,128)(2,1)S(1)}, bf16[4,32,576]{2,1,0:T(8,128)(2,1)S(1)}, u32[]{:S(2)}, u32[]{:S(2)}) collective-permute-start(bf16[4,32,576]{2,1,0:T(8,128)(2,1)S(1)} %get-tuple-element.61), channel_id=1, source_target_pairs={{0,224},{4,228},{8,232},{12,236},{16,240},{20,244},{24,248},{28,25... | collective-permute-start | bytes 442376 | tf_op jit(solution)/shard_map/ppermute | solution.py:39
  235.1 3.4 %collective-permute-start.33 = (bf16[4,32,576]{2,1,0:T(8,128)(2,1)S(1)}, bf16[4,32,576]{2,1,0:T(8,128)(2,1)S(1)}, u32[]{:S(2)}, u32[]{:S(2)}) collective-permute-start(bf16[4,32,576]{2,1,0:T(8,128)(2,1)S(1)} %add_convert_fusion.5), channel_id=1, source_target_pairs={{64,32},{68,36},{72,40},{76,44},{80,48},{84,52},{88,56},{92,60},{9... | collective-permute-start | bytes 442376 | tf_op jit(solution)/shard_map/ppermute | solution.py:39
  238.5 4.8 %copy.38 = bf16[128,16,576]{0,2,1:T(8,128)(2,1)} copy(bf16[128,16,576]{2,1,0:T(8,128)(2,1)} %bitcast.36) | data formatting | bytes 4718592 | tf_op jit(solution)/shard_map/reshape | solution.py:472
  250.6 4.9 %collective-permute-start.39 = (bf16[32,576]{1,0:T(8,128)(2,1)S(1)}, bf16[32,576]{1,0:T(8,128)(2,1)S(1)}, u32[]{:S(2)}, u32[]{:S(2)}) collective-permute-start(bf16[32,576]{1,0:T(8,128)(2,1)S(1)} %get-tuple-element.71), channel_id=1, source_target_pairs={{8,192},{24,196},{40,200},{56,204},{72,208},{88,212},{104,216},{12... | collective-permute-start | bytes 110600 | tf_op jit(solution)/shard_map/ppermute | solution.py:463
  256.9 4.2 %collective-permute-done.40 = bf16[32,576]{1,0:T(8,128)(2,1)S(1)} collective-permute-done((bf16[32,576]{1,0:T(8,128)(2,1)S(1)}, bf16[32,576]{1,0:T(8,128)(2,1)S(1)}, u32[]{:S(2)}, u32[]{:S(2)}) %collective-permute-start.40) | collective-permute-done | bytes 36896 | tf_op jit(solution)/shard_map/ppermute | solution.py:463
  266.0 6.4 %collective-permute-done.37 = bf16[32,576]{1,0:T(8,128)(2,1)S(1)} collective-permute-done((bf16[32,576]{1,0:T(8,128)(2,1)S(1)}, bf16[32,576]{1,0:T(8,128)(2,1)S(1)}, u32[]{:S(2)}, u32[]{:S(2)}) %collective-permute-start.37) | collective-permute-done | bytes 36896 | tf_op jit(solution)/shard_map/ppermute | solution.py:463
  273.2 3.1 %copy.51 = bf16[16,512,128]{2,1,0:T(8,128)(2,1)} copy(bf16[16,512,128]{2,1,0:T(8,128)(2,1)} %bitcast.24) | data formatting | bytes 4194304
  (196 shorter events, 98.9 us)
Async XLA Ops:
  2.2 11.7 %collective-permute-start = (bf16[4,32,576]{2,1,0:T(8,128)(2,1)S(1)}, bf16[4,32,576]{2,1,0:T(8,128)(2,1)S(1)}, u32[]{:S(2)}, u32[]{:S(2)}) collective-permute-start(bf16[4,32,576]{2,1,0:T(8,128)(2,1)S(1)} %bitcast.38), channel_id=1, source_target_pairs={{0,224},{4,228},{8,232},{12,236},{16,240},{20,244},{24,248},{28,25... | collective-permute-start | bytes 442376 | tf_op jit(solution)/shard_map/ppermute | solution.py:39
  21.2 16.5 %collective-permute-start.2 = (bf16[4,32,576]{2,1,0:T(8,128)(2,1)S(1)}, bf16[4,32,576]{2,1,0:T(8,128)(2,1)S(1)}, u32[]{:S(2)}, u32[]{:S(2)}) collective-permute-start(bf16[4,32,576]{2,1,0:T(8,128)(2,1)S(1)} %collective-permute-done.1.refs_2_), channel_id=1, source_target_pairs={{0,224},{4,228},{8,232},{12,236},{16,240},{20,244},{24,248},{28,25... | collective-permute-start | bytes 442376 | tf_op jit(solution)/shard_map/ppermute | solution.py:39
  26.4 11.3 %collective-permute-start.6 = (bf16[4,32,576]{2,1,0:T(8,128)(2,1)S(1)}, bf16[4,32,576]{2,1,0:T(8,128)(2,1)S(1)}, u32[]{:S(2)}, u32[]{:S(2)}) collective-permute-start(bf16[4,32,576]{2,1,0:T(8,128)(2,1)S(1)} %collective-permute-done.5.refs_5_), channel_id=1, source_target_pairs={{0,32},{4,36},{8,40},{12,44},{16,48},{20,52},{24,56},{28,60},{96,1... | collective-permute-start | bytes 442376 | tf_op jit(solution)/shard_map/ppermute | solution.py:39
  41.4 31.2 %all-to-all-start.1 = ((bf16[8,6,32,576]{3,2,1,0:T(8,128)(2,1)}), bf16[8,6,32,576]{3,2,1,0:T(8,128)(2,1)}, u32[]{:S(2)}, u32[]{:S(2)}) async-start(bf16[8,6,32,576]{3,2,1,0:T(8,128)(2,1)} %bitcast.35), calls=%async_computation.1 | async-start | bytes 3932160 | tf_op jit(solution)/shard_map/all_to_all | solution.py:85
  47.9 24.7 %collective-permute-start.7 = (bf16[32,576]{1,0:T(8,128)(2,1)S(1)}, bf16[32,576]{1,0:T(8,128)(2,1)S(1)}, u32[]{:S(2)}, u32[]{:S(2)}) collective-permute-start(bf16[32,576]{1,0:T(8,128)(2,1)S(1)} %get-tuple-element.81), channel_id=1, source_target_pairs={{192,0},{196,16},{200,32},{204,48},{208,64},{212,80},{216,96},{220... | collective-permute-start | bytes 110600 | tf_op jit(solution)/shard_map/ppermute | solution.py:389
  57.1 15.6 %collective-permute-start.8 = (bf16[32,576]{1,0:T(8,128)(2,1)S(1)}, bf16[32,576]{1,0:T(8,128)(2,1)S(1)}, u32[]{:S(2)}, u32[]{:S(2)}) collective-permute-start(bf16[32,576]{1,0:T(8,128)(2,1)S(1)} %get-tuple-element.80), channel_id=1, source_target_pairs={{192,4},{196,20},{200,36},{204,52},{208,68},{212,84},{216,100},{22... | collective-permute-start | bytes 110600 | tf_op jit(solution)/shard_map/ppermute | solution.py:389
  58.4 14.3 %collective-permute-start.9 = (bf16[32,576]{1,0:T(8,128)(2,1)S(1)}, bf16[32,576]{1,0:T(8,128)(2,1)S(1)}, u32[]{:S(2)}, u32[]{:S(2)}) collective-permute-start(bf16[32,576]{1,0:T(8,128)(2,1)S(1)} %get-tuple-element.79), channel_id=1, source_target_pairs={{192,8},{196,24},{200,40},{204,56},{208,72},{212,88},{216,104},{22... | collective-permute-start | bytes 110600 | tf_op jit(solution)/shard_map/ppermute | solution.py:389
  60.3 12.4 %collective-permute-start.10 = (bf16[32,576]{1,0:T(8,128)(2,1)S(1)}, bf16[32,576]{1,0:T(8,128)(2,1)S(1)}, u32[]{:S(2)}, u32[]{:S(2)}) collective-permute-start(bf16[32,576]{1,0:T(8,128)(2,1)S(1)} %get-tuple-element.78), channel_id=1, source_target_pairs={{192,12},{196,28},{200,44},{204,60},{208,76},{212,92},{216,108},{2... | collective-permute-start | bytes 110600 | tf_op jit(solution)/shard_map/ppermute | solution.py:389
  79.0 23.1 %collective-permute-start.13 = (bf16[7,32,576]{2,1,0:T(8,128)(2,1)}, bf16[7,32,576]{2,1,0:T(8,128)(2,1)S(1)}, u32[]{:S(2)}, u32[]{:S(2)}) collective-permute-start(bf16[7,32,576]{2,1,0:T(8,128)(2,1)} %get-tuple-element.41.refs_0_.refs_4_), channel_id=1, source_target_pairs={{0,3},{1,0},{2,1},{3,2},{4,7},{5,4},{6,5},{7,6},{8,11},{9,8},{10,9... | collective-permute-start | bytes 774152 | tf_op jit(solution)/shard_map/ppermute | solution.py:81
  86.8 15.3 %collective-permute-start.12 = (bf16[7,32,576]{2,1,0:T(8,128)(2,1)S(1)}, bf16[7,32,576]{2,1,0:T(8,128)(2,1)S(1)}, u32[]{:S(2)}, u32[]{:S(2)}) collective-permute-start(bf16[7,32,576]{2,1,0:T(8,128)(2,1)S(1)} %collective-permute-done.11.refs_1_.refs_5_), channel_id=1, source_target_pairs={{0,1},{1,2},{2,3},{3,0},{4,5},{5,6},{6,7},{7,4},{8,9},{9,10},{10,1... | collective-permute-start | bytes 774152 | tf_op jit(solution)/shard_map/ppermute | solution.py:81
  87.1 15.0 %collective-permute-start.14 = (bf16[6,32,576]{2,1,0:T(8,128)(2,1)}, bf16[6,32,576]{2,1,0:T(8,128)(2,1)}, u32[]{:S(2)}, u32[]{:S(2)}) collective-permute-start(bf16[6,32,576]{2,1,0:T(8,128)(2,1)} %get-tuple-element.42.refs_8_), channel_id=1, source_target_pairs={{0,1},{1,2},{2,3},{3,0},{4,5},{5,6},{6,7},{7,4},{8,9},{9,10},{10,1... | collective-permute-start | bytes 663560 | tf_op jit(solution)/shard_map/ppermute | solution.py:81
  88.6 13.6 %collective-permute-start.16 = (bf16[6,32,576]{2,1,0:T(8,128)(2,1)}, bf16[6,32,576]{2,1,0:T(8,128)(2,1)}, u32[]{:S(2)}, u32[]{:S(2)}) collective-permute-start(bf16[6,32,576]{2,1,0:T(8,128)(2,1)} %collective-permute-done.15.refs_11_), channel_id=1, source_target_pairs={{0,3},{1,0},{2,1},{3,2},{4,7},{5,4},{6,5},{7,6},{8,11},{9,8},{10,9... | collective-permute-start | bytes 663560 | tf_op jit(solution)/shard_map/ppermute | solution.py:81
  128.7 18.2 %all-to-all-start.2 = ((bf16[4,1024,128]{2,1,0:T(8,128)(2,1)}), bf16[4,1024,128]{2,1,0:T(8,128)(2,1)}, u32[]{:S(2)}, u32[]{:S(2)}) async-start(bf16[4,1024,128]{2,1,0:T(8,128)(2,1)} %fusion), calls=%async_computation.2 | async-start | bytes 2097152 | tf_op jit(solution)/shard_map/all_to_all | solution.py:85
  133.7 26.6 %collective-permute-start.17 = (bf16[7,32,576]{2,1,0:T(8,128)(2,1)}, bf16[7,32,576]{2,1,0:T(8,128)(2,1)S(1)}, u32[]{:S(2)}, u32[]{:S(2)}) collective-permute-start(bf16[7,32,576]{2,1,0:T(8,128)(2,1)} %get-tuple-element.44), channel_id=1, source_target_pairs={{0,1},{1,2},{2,3},{3,0},{4,5},{5,6},{6,7},{7,4},{8,9},{9,10},{10,1... | collective-permute-start | bytes 774152 | tf_op jit(solution)/shard_map/ppermute | solution.py:81
  135.3 24.3 %collective-permute-start.20 = (bf16[6,32,576]{2,1,0:T(8,128)(2,1)}, bf16[6,32,576]{2,1,0:T(8,128)(2,1)S(1)}, u32[]{:S(2)}, u32[]{:S(2)}) collective-permute-start(bf16[6,32,576]{2,1,0:T(8,128)(2,1)} %get-tuple-element.48), channel_id=1, source_target_pairs={{0,3},{1,0},{2,1},{3,2},{4,7},{5,4},{6,5},{7,6},{8,11},{9,8},{10,9... | collective-permute-start | bytes 663560 | tf_op jit(solution)/shard_map/ppermute | solution.py:81
  137.0 21.3 %collective-permute-start.21 = (bf16[6,32,576]{2,1,0:T(8,128)(2,1)}, bf16[6,32,576]{2,1,0:T(8,128)(2,1)}, u32[]{:S(2)}, u32[]{:S(2)}) collective-permute-start(bf16[6,32,576]{2,1,0:T(8,128)(2,1)} %get-tuple-element.49), channel_id=1, source_target_pairs={{0,1},{1,2},{2,3},{3,0},{4,5},{5,6},{6,7},{7,4},{8,9},{9,10},{10,1... | collective-permute-start | bytes 663560 | tf_op jit(solution)/shard_map/ppermute | solution.py:81
  143.9 23.7 %collective-permute-start.19 = (bf16[7,32,576]{2,1,0:T(8,128)(2,1)}, bf16[7,32,576]{2,1,0:T(8,128)(2,1)S(1)}, u32[]{:S(2)}, u32[]{:S(2)}) collective-permute-start(bf16[7,32,576]{2,1,0:T(8,128)(2,1)} %add_convert_fusion), channel_id=1, source_target_pairs={{0,3},{1,0},{2,1},{3,2},{4,7},{5,4},{6,5},{7,6},{8,11},{9,8},{10,9... | collective-permute-start | bytes 774152 | tf_op jit(solution)/shard_map/ppermute | solution.py:81
  149.0 25.6 %all-to-all-start.3 = ((bf16[8,128,128]{2,1,0:T(8,128)(2,1)}), bf16[8,128,128]{2,1,0:T(8,128)(2,1)}, u32[]{:S(2)}, u32[]{:S(2)}) async-start(bf16[8,128,128]{2,1,0:T(8,128)(2,1)} %bitcast.41), calls=%async_computation.3 | async-start | bytes 524288 | tf_op jit(solution)/shard_map/all_to_all | solution.py:85
  173.9 13.5 %collective-permute-start.23 = (bf16[6,32,576]{2,1,0:T(8,128)(2,1)}, bf16[6,32,576]{2,1,0:T(8,128)(2,1)S(1)}, u32[]{:S(2)}, u32[]{:S(2)}) collective-permute-start(bf16[6,32,576]{2,1,0:T(8,128)(2,1)} %get-tuple-element.52), channel_id=1, source_target_pairs={{0,4},{4,0},{8,12},{12,8},{16,20},{20,16},{24,28},{28,24},{32,36},... | collective-permute-start | bytes 663560 | tf_op jit(solution)/shard_map/ppermute | solution.py:73
  173.9 15.0 %collective-permute-start.24 = (bf16[6,32,576]{2,1,0:T(8,128)(2,1)}, bf16[6,32,576]{2,1,0:T(8,128)(2,1)S(1)}, u32[]{:S(2)}, u32[]{:S(2)}) collective-permute-start(bf16[6,32,576]{2,1,0:T(8,128)(2,1)} %get-tuple-element.53), channel_id=1, source_target_pairs={{0,8},{4,12},{8,16},{12,20},{16,24},{20,28},{24,0},{28,4},{32,40},... | collective-permute-start | bytes 663560 | tf_op jit(solution)/shard_map/ppermute | solution.py:73
  176.3 42.7 %all-to-all-start.4 = ((bf16[8,128,128]{2,1,0:T(8,128)(2,1)}), bf16[8,128,128]{2,1,0:T(8,128)(2,1)}, u32[]{:S(2)}, u32[]{:S(2)}) async-start(bf16[8,128,128]{2,1,0:T(8,128)(2,1)} %broadcast_in_dim.77), calls=%async_computation.4 | async-start | bytes 524288 | tf_op jit(solution)/shard_map/all_to_all | solution.py:85
  186.5 12.7 %collective-permute-start.27 = (bf16[6,32,576]{2,1,0:T(8,128)(2,1)}, bf16[6,32,576]{2,1,0:T(8,128)(2,1)}, u32[]{:S(2)}, u32[]{:S(2)}) collective-permute-start(bf16[6,32,576]{2,1,0:T(8,128)(2,1)} %copy-done.19), channel_id=1, source_target_pairs={{0,20},{4,16},{8,28},{12,24},{16,4},{20,0},{24,12},{28,8},{32,52},... | collective-permute-start | bytes 663560 | tf_op jit(solution)/shard_map/ppermute | solution.py:73
  187.4 17.4 %collective-permute-start.28 = (bf16[6,32,576]{2,1,0:T(8,128)(2,1)}, bf16[6,32,576]{2,1,0:T(8,128)(2,1)}, u32[]{:S(2)}, u32[]{:S(2)}) collective-permute-start(bf16[6,32,576]{2,1,0:T(8,128)(2,1)} %copy-done.18), channel_id=1, source_target_pairs={{0,24},{4,28},{8,0},{12,4},{16,8},{20,12},{24,16},{28,20},{32,56},... | collective-permute-start | bytes 663560 | tf_op jit(solution)/shard_map/ppermute | solution.py:73
  188.9 21.1 %collective-permute-start.29 = (bf16[6,32,576]{2,1,0:T(8,128)(2,1)}, bf16[6,32,576]{2,1,0:T(8,128)(2,1)}, u32[]{:S(2)}, u32[]{:S(2)}) collective-permute-start(bf16[6,32,576]{2,1,0:T(8,128)(2,1)} %copy-done.17), channel_id=1, source_target_pairs={{0,28},{4,24},{8,4},{12,0},{16,12},{20,8},{24,20},{28,16},{32,60},... | collective-permute-start | bytes 663560 | tf_op jit(solution)/shard_map/ppermute | solution.py:73
  216.5 13.8 %collective-permute-start.30 = (bf16[4,32,576]{2,1,0:T(8,128)(2,1)}, bf16[4,32,576]{2,1,0:T(8,128)(2,1)S(1)}, u32[]{:S(2)}, u32[]{:S(2)}) collective-permute-start(bf16[4,32,576]{2,1,0:T(8,128)(2,1)} %get-tuple-element.59), channel_id=1, source_target_pairs={{0,32},{4,36},{8,40},{12,44},{16,48},{20,52},{24,56},{28,60},{32,6... | collective-permute-start | bytes 442376 | tf_op jit(solution)/shard_map/ppermute | solution.py:39
  221.5 51.7 %all-to-all-start.5 = ((bf16[8,1024,128]{2,1,0:T(8,128)(2,1)}), bf16[8,1024,128]{2,1,0:T(8,128)(2,1)}, u32[]{:S(2)}, u32[]{:S(2)}) async-start(bf16[8,1024,128]{2,1,0:T(8,128)(2,1)} %broadcast_in_dim.78), calls=%async_computation.5 | async-start | bytes 4194304 | tf_op jit(solution)/shard_map/all_to_all | solution.py:85
  230.4 12.9 %collective-permute-start.31 = (bf16[4,32,576]{2,1,0:T(8,128)(2,1)S(1)}, bf16[4,32,576]{2,1,0:T(8,128)(2,1)S(1)}, u32[]{:S(2)}, u32[]{:S(2)}) collective-permute-start(bf16[4,32,576]{2,1,0:T(8,128)(2,1)S(1)} %add_convert_fusion.6), channel_id=1, source_target_pairs={{0,32},{4,36},{8,40},{12,44},{16,48},{20,52},{24,56},{28,60},{32,6... | collective-permute-start | bytes 442376 | tf_op jit(solution)/shard_map/ppermute | solution.py:39
  245.9 26.6 %collective-permute-start.36 = (bf16[4,32,576]{2,1,0:T(8,128)(2,1)S(1)}, bf16[4,32,576]{2,1,0:T(8,128)(2,1)S(1)}, u32[]{:S(2)}, u32[]{:S(2)}) collective-permute-start(bf16[4,32,576]{2,1,0:T(8,128)(2,1)S(1)} %add_convert_fusion.2), channel_id=1, source_target_pairs={{32,0},{36,4},{40,8},{44,12},{48,16},{52,20},{56,24},{60,28},{64,3... | collective-permute-start | bytes 442376 | tf_op jit(solution)/shard_map/ppermute | solution.py:39
  248.7 23.8 %collective-permute-start.35 = (bf16[4,32,576]{2,1,0:T(8,128)(2,1)S(1)}, bf16[4,32,576]{2,1,0:T(8,128)(2,1)S(1)}, u32[]{:S(2)}, u32[]{:S(2)}) collective-permute-start(bf16[4,32,576]{2,1,0:T(8,128)(2,1)S(1)} %add_convert_fusion.3), channel_id=1, source_target_pairs={{0,32},{4,36},{8,40},{12,44},{16,48},{20,52},{24,56},{28,60},{32,6... | collective-permute-start | bytes 442376 | tf_op jit(solution)/shard_map/ppermute | solution.py:39
  249.3 11.7 %collective-permute-start.40 = (bf16[32,576]{1,0:T(8,128)(2,1)S(1)}, bf16[32,576]{1,0:T(8,128)(2,1)S(1)}, u32[]{:S(2)}, u32[]{:S(2)}) collective-permute-start(bf16[32,576]{1,0:T(8,128)(2,1)S(1)} %get-tuple-element.71), channel_id=1, source_target_pairs={{12,192},{28,196},{44,200},{60,204},{76,208},{92,212},{108,216},{1... | collective-permute-start | bytes 110600 | tf_op jit(solution)/shard_map/ppermute | solution.py:463
  250.6 13.3 %collective-permute-start.39 = (bf16[32,576]{1,0:T(8,128)(2,1)S(1)}, bf16[32,576]{1,0:T(8,128)(2,1)S(1)}, u32[]{:S(2)}, u32[]{:S(2)}) collective-permute-start(bf16[32,576]{1,0:T(8,128)(2,1)S(1)} %get-tuple-element.71), channel_id=1, source_target_pairs={{8,192},{24,196},{40,200},{56,204},{72,208},{88,212},{104,216},{12... | collective-permute-start | bytes 110600 | tf_op jit(solution)/shard_map/ppermute | solution.py:463
  261.0 11.4 %collective-permute-start.37 = (bf16[32,576]{1,0:T(8,128)(2,1)S(1)}, bf16[32,576]{1,0:T(8,128)(2,1)S(1)}, u32[]{:S(2)}, u32[]{:S(2)}) collective-permute-start(bf16[32,576]{1,0:T(8,128)(2,1)S(1)} %get-tuple-element.71), channel_id=1, source_target_pairs={{0,192},{16,196},{32,200},{48,204},{64,208},{80,212},{96,216},{112... | collective-permute-start | bytes 110600 | tf_op jit(solution)/shard_map/ppermute | solution.py:463
  (58 other events, 571.2 us)
